TPU v7x, 512 devices: a whole 4x4x16 slice. The times are simulated.
512 devices in a mesh: dp: 32 (over x, y, core), expert: 16 (over z).
Axes of the slice: x: 4, y: 4, z: 16, core: 2. Of those that a mesh axis runs over, the one named last changes fastest.
Arguments:
- tokens: bfloat16 [4096, 2048], P('dp', 'expert'), may hold values from -6 to 6
- cotangent: bfloat16 [4096, 2048], P('dp', 'expert'), may hold values from -6 to 6
- expert_ids: int32 [4096, 8], P('dp'), may hold values from 0 to 127, all different within a row; in each aligned block of 128 rows (0 to 127, 128 to 255, ...) at most 16 rows name the same one
- gate_weights: float32 [4096, 8], P('dp'), may hold values from 0.05 to 1
- w_gate: bfloat16 [512, 192, 2048], P(('dp', 'expert')), may hold values from -0.125 to 0.125
- w_up: bfloat16 [512, 192, 2048], P(('dp', 'expert')), may hold values from -0.125 to 0.125
- w_down: bfloat16 [512, 192, 2048], P(('dp', 'expert')), may hold values from -0.21875 to 0.21875
Outputs:
- layer_out: bfloat16 [4096, 2048], P('dp', 'expert')
- grad_tokens: bfloat16 [4096, 2048], P('dp', 'expert')
- grad_gates: float32 [4096, 8], P('dp')
- grad_w_gate: bfloat16 [512, 192, 2048], P(('dp', 'expert'))
- grad_w_up: bfloat16 [512, 192, 2048], P(('dp', 'expert'))
- grad_w_down: bfloat16 [512, 192, 2048], P(('dp', 'expert'))
Inputs may be any that keep to these rules, and one draw needn't show every extreme that they name: `expert_ids`: each row names 8 different experts. In each aligned block of 128 rows (the rows of one index of dp) no expert is named by more than 16 rows, and in some block an expert is named by exactly 16 rows.
All inputs are finite; a program needn't handle non-finite values.
Results may differ from a plain program's by a relative error of at most 0.0064.
Values may be sent and summed in bfloat16 or wider, within the bound.
No kernel may reach another device: no remote copies, remote signals or barrier semaphores. Data moves between devices by JAX's collectives and lax.ppermute only.
A program may use at most 64 MiB of HBM per device.

v0:
```python
import jax
import jax.numpy as jnp
from jax import lax
from jax.sharding import PartitionSpec as P

SHARDS = 4


def silu_parts(preact):
    sigmoid_of = jax.nn.sigmoid(preact)
    activated = preact * sigmoid_of
    derivative = sigmoid_of * (1.0 + preact * (1.0 - sigmoid_of))
    return (activated, derivative)


def contract_last(first_op, second_op):
    return lax.dot_general(
        first_op, second_op, (((1,), (1,)), ((), ())), preferred_element_type=jnp.float32
    )


def contract_first(first_op, second_op):
    return lax.dot_general(
        first_op, second_op, (((0,), (0,)), ((), ())), preferred_element_type=jnp.float32
    )


def forward_rows(rows_x, gate_w, up_w, down_w):
    pre_gate = contract_last(rows_x, gate_w)
    pre_up = contract_last(rows_x, up_w)
    activated, derivative = silu_parts(pre_gate)
    hidden = (activated * pre_up).astype(jnp.bfloat16)
    return jnp.dot(hidden, down_w, preferred_element_type=jnp.float32).astype(jnp.bfloat16)


def backward_rows(rows_x, rows_do, gate_w, up_w, down_w):
    pre_gate = contract_last(rows_x, gate_w)
    pre_up = contract_last(rows_x, up_w)
    activated, derivative = silu_parts(pre_gate)
    hidden = (activated * pre_up).astype(jnp.bfloat16)
    d_hidden = contract_last(rows_do, down_w)
    d_pre_gate = (d_hidden * pre_up * derivative).astype(jnp.bfloat16)
    d_pre_up = (d_hidden * activated).astype(jnp.bfloat16)
    part_grad = (
        jnp.dot(d_pre_gate, gate_w, preferred_element_type=jnp.float32)
        + jnp.dot(d_pre_up, up_w, preferred_element_type=jnp.float32)
    ).astype(jnp.bfloat16)
    gradients = (
        contract_first(d_pre_gate, rows_x),
        contract_first(d_pre_up, rows_x),
        contract_first(hidden, rows_do),
    )
    return (part_grad, gradients)


def per_device(tokens, cotangent, expert_ids, gate_weights, w_gate, w_up, w_down):
    full_x, full_dy = (
        lax.all_gather(tokens, "expert", axis=1, tiled=True),
        lax.all_gather(cotangent, "expert", axis=1, tiled=True),
    )
    dp_count = lax.axis_size("dp")
    column_count = lax.axis_size("expert")
    column = lax.axis_index("expert")
    tok_count, chosen = expert_ids.shape
    features = full_x.shape[1]
    experts_all = dp_count * column_count // SHARDS
    capacity = min(tok_count, max(2, 2 * tok_count * chosen // experts_all))
    per_row = column_count // SHARDS
    assigned = tok_count * chosen
    flat_ids = expert_ids.reshape(-1)
    flat_gates = gate_weights.reshape(-1)
    owned_here = flat_ids % per_row == column // SHARDS
    target_row = flat_ids // per_row
    onehot = (
        (target_row[:, None] == jnp.arange(dp_count, dtype=jnp.int32)[None, :])
        & owned_here[:, None]
    ).astype(jnp.int32)
    rank_of = jnp.sum((jnp.cumsum(onehot, axis=0) - 1) * onehot, axis=1)
    target = jnp.where(owned_here, target_row * capacity + rank_of, dp_count * capacity)
    slot_src = (
        jnp.full((dp_count * capacity,), assigned, jnp.int32)
        .at[target]
        .set(jnp.arange(assigned, dtype=jnp.int32), mode="drop")
    )
    filled = slot_src < assigned
    safe_index = jnp.where(filled, slot_src, 0)
    slot_token = safe_index // chosen
    slot_gate = jnp.where(filled, flat_gates[safe_index], 0.0)
    slot_dy = full_dy[slot_token].astype(jnp.float32)
    send_x = jnp.where(filled[:, None], full_x[slot_token], jnp.zeros((), full_x.dtype)).reshape(
        dp_count, capacity, features
    )
    send_do = (
        (slot_gate[:, None] * slot_dy).astype(jnp.bfloat16).reshape(dp_count, capacity, features)
    )
    weights = (w_gate[0], w_up[0], w_down[0])
    recv_x = lax.all_to_all(send_x, "dp", split_axis=0, concat_axis=0, tiled=True)
    rows_x = recv_x.reshape(dp_count * capacity, features)
    expert_out = forward_rows(rows_x, *weights)
    back_out = lax.all_to_all(
        expert_out.reshape(dp_count, capacity, features),
        "dp",
        split_axis=0,
        concat_axis=0,
        tiled=True,
    )
    recv_do = lax.all_to_all(send_do, "dp", split_axis=0, concat_axis=0, tiled=True)
    rows_do = recv_do.reshape(dp_count * capacity, features)
    part_grad, gradients = backward_rows(rows_x, rows_do, *weights)
    back_grad = lax.all_to_all(
        part_grad.reshape(dp_count, capacity, features),
        "dp",
        split_axis=0,
        concat_axis=0,
        tiled=True,
    )
    width_now = back_out.shape[2]
    out_float = back_out.reshape(dp_count * capacity, width_now).astype(jnp.float32)
    grad_float = back_grad.reshape(dp_count * capacity, width_now).astype(jnp.float32)
    out_part = (
        jnp.zeros((tok_count, width_now), jnp.float32)
        .at[slot_token]
        .add(slot_gate[:, None] * out_float)
    )
    grad_part = jnp.zeros((tok_count, width_now), jnp.float32).at[slot_token].add(grad_float)
    gate_terms = jnp.sum(slot_dy * out_float, axis=1)
    gate_part = (
        jnp.zeros((assigned,), jnp.float32)
        .at[slot_src]
        .add(gate_terms, mode="drop")
        .reshape(tok_count, chosen)
    )
    out_slice, grad_slice = (
        lax.psum_scatter(out_part, "expert", scatter_dimension=1, tiled=True),
        lax.psum_scatter(grad_part, "expert", scatter_dimension=1, tiled=True),
    )
    grad_gates = lax.psum(gate_part, "expert")
    return (
        out_slice.astype(jnp.bfloat16),
        grad_slice.astype(jnp.bfloat16),
        grad_gates,
        gradients[0].astype(jnp.bfloat16)[None],
        gradients[1].astype(jnp.bfloat16)[None],
        gradients[2].astype(jnp.bfloat16)[None],
    )


def solution(mesh):
    placed = (
        P("dp", "expert"),
        P("dp", "expert"),
        P("dp", None),
        P("dp", None),
        P(("dp", "expert"), None, None),
        P(("dp", "expert"), None, None),
        P(("dp", "expert"), None, None),
    )
    return jax.shard_map(
        per_device,
        mesh=mesh,
        in_specs=placed,
        out_specs=(
            P("dp", "expert"),
            P("dp", "expert"),
            P("dp", None),
            P(("dp", "expert"), None, None),
            P(("dp", "expert"), None, None),
            P(("dp", "expert"), None, None),
        ),
        check_vma=False,
    )
```

profile of v0, /device:TPU:6, one launch (start us, length us, event | category | flops | bytes accessed | tf_op | source)
XLA Modules:
  0.0 339.7 jit_solution(6316037226412424405)
XLA Ops:
  7.2 0.0 copy-start
  7.2 0.9 copy.13
  8.0 0.1 reshape.230
  8.1 0.1 reshape.229
  8.2 0.1 reshape.228
  8.4 9.0 %reduce-window.6 = s32[32,8,128]{2,1,0:T(8,128)S(1)} reduce-window(s32[32,8,128]{2,1,0:T(8,128)S(1)} %fusion.25, s32[]{:T(128)} %constant.66.clone.1), window={size=1x1x128 pad=0_0x0_0x127_0}, to_apply=%region_0.1 | reduce-window | flops 4161536 | bytes 262148 | tf_op jit(solution)/shard_map/reduce-window
  17.5 0.1 slice.14
  17.6 0.1 copy.16
  17.7 0.1 copy.17
  17.8 0.1 add_add_fusion
  18.0 4.3 %scatter_custom_fusion = s32[512]{0:T(512)S(1)} fusion(s32[1024]{0:T(1024)S(1)} %bitcast.72, s32[1024]{0:T(1024)S(1)} %iota.11, s32[]{:T(128)} %constant.65.clone.1), kind=kCustom, calls=%fused_computation.91 | custom fusion | bytes 2052 | tf_op jit(solution)/shard_map/scatter | solution.py:83
  22.4 0.1 broadcast_in_dim.62
  22.5 38.8 %all_gather.6 = bf16[128,2048]{1,0:T(8,128)(2,1)S(1)} all-gather(bf16[128,128]{1,0:T(8,128)(2,1)} %param.7), channel_id=1, replica_groups=mesh['dp'=32,'expert'=16] {'expert'}, dimensions={1}, use_global_device_ids=true | all-gather | bytes 557056 | tf_op jit(solution)/shard_map/all_gather | solution.py:58
  61.3 2.5 gather_fusion.1
  63.7 1.6 broadcast_select_fusion
  65.3 0.0 copy-start.3
  65.3 7.8 %all-to-all-start = ((bf16[32,16,2048]{2,1,0:T(8,128)(2,1)}), bf16[32,16,2048]{2,1,0:T(8,128)(2,1)}, u32[]{:S(2)}, u32[]{:S(2)}) async-start(bf16[32,16,2048]{2,1,0:T(8,128)(2,1)} %broadcast_select_fusion), calls=%async_computation | async-start | bytes 4194304 | tf_op jit(solution)/shard_map/all_to_all | solution.py:97
  73.1 0.0 copy-done.3
  73.1 0.0 copy-start.2
  73.1 0.1 copy.18
  73.2 0.1 reshape.232
  73.3 2.3 gather_fusion
  75.6 0.1 mul.69
  75.7 0.0 copy-done.2
  75.7 28.7 %all_gather.7 = bf16[128,2048]{1,0:T(8,128)(2,1)S(1)} all-gather(bf16[128,128]{1,0:T(8,128)(2,1)S(1)} %copy-done.2), channel_id=1, replica_groups=mesh['dp'=32,'expert'=16] {'expert'}, dimensions={1}, use_global_device_ids=true | all-gather | bytes 557056 | tf_op jit(solution)/shard_map/all_gather | solution.py:59
  104.4 2.5 gather_fusion.2
  106.9 1.7 fusion
  108.6 0.0 all-to-all-done
  108.6 7.4 %all-to-all-start.2 = ((bf16[32,16,2048]{2,1,0:T(8,128)(2,1)}), bf16[32,16,2048]{2,1,0:T(8,128)(2,1)}, u32[]{:S(2)}, u32[]{:S(2)}) async-start(bf16[32,16,2048]{2,1,0:T(8,128)(2,1)} %fusion), calls=%async_computation.3 | async-start | bytes 4194304 | tf_op jit(solution)/shard_map/all_to_all | solution.py:107
  116.1 0.0 copy-start.1
  116.1 3.4 %fusion.11 = f32[512,192]{0,1:T(8,128)} fusion(bf16[512,2048]{1,0:T(8,128)(2,1)} %bitcast.5, bf16[1,192,2048]{2,1,0:T(8,128)(2,1)} %param.12), kind=kOutput, calls=%fused_computation.27 | convolution fusion | flops 402653184 | bytes 3276800 | tf_op jit(solution)/shard_map/dot_general | solution.py:17
  119.5 0.0 copy-done.1
  119.5 3.2 fusion.15
  122.7 19.7 %all-to-all-done.2 = bf16[32,16,2048]{2,1,0:T(8,128)(2,1)} async-done(((bf16[32,16,2048]{2,1,0:T(8,128)(2,1)}), bf16[32,16,2048]{2,1,0:T(8,128)(2,1)}, u32[]{:S(2)}, u32[]{:S(2)}) %all-to-all-start.2) | async-done | bytes 2097184 | tf_op jit(solution)/shard_map/all_to_all | solution.py:107
  142.4 0.0 copy-done
  142.4 2.7 multiply_convert_fusion
  145.1 2.1 convolution_convert_fusion
  147.2 7.3 %all-to-all-start.1 = ((bf16[32,16,2048]{2,1,0:T(8,128)(2,1)}), bf16[32,16,2048]{2,1,0:T(8,128)(2,1)}, u32[]{:S(2)}, u32[]{:S(2)}) async-start(bf16[32,16,2048]{2,1,0:T(8,128)(2,1)} %bitcast.67), calls=%async_computation.1 | async-start | bytes 4194304 | tf_op jit(solution)/shard_map/all_to_all | solution.py:100
  154.5 0.2 reduce-scatter.3.cloned.1.call-start
  154.7 3.8 %fusion.13 = f32[512,2048]{1,0:T(8,128)} fusion(bf16[512,192]{0,1:T(8,128)(2,1)S(1)} %get-tuple-element.15, bf16[1,192,2048]{2,1,0:T(8,128)(2,1)} %param.11), kind=kOutput, calls=%fused_computation.29 | convolution fusion | flops 402653184 | bytes 5177344 | tf_op jit(solution)/shard_map/dot_general | solution.py:45
  158.5 22.3 %all-to-all-done.1 = bf16[32,16,2048]{2,1,0:T(8,128)(2,1)} async-done(((bf16[32,16,2048]{2,1,0:T(8,128)(2,1)}), bf16[32,16,2048]{2,1,0:T(8,128)(2,1)}, u32[]{:S(2)}, u32[]{:S(2)}) %all-to-all-start.1) | async-done | bytes 2097184 | tf_op jit(solution)/shard_map/all_to_all | solution.py:100
  180.9 3.9 %bitcast_multiply_fusion = f32[512,2048]{1,0:T(8,128)} fusion(f32[512]{0:T(512)S(1)} %broadcast_select_fusion.1, bf16[32,16,2048]{2,1,0:T(8,128)(2,1)} %all-to-all-done.1), kind=kLoop, calls=%fused_computation.13 | loop fusion | flops 2097152 | bytes 6293504 | tf_op jit(solution)/shard_map/mul | solution.py:123
  184.8 9.4 %scatter_custom_fusion.1 = f32[128,2048]{1,0:T(8,128)} fusion(s32[512]{0:T(512)S(1)} %get-tuple-element.18, f32[512,2048]{1,0:T(8,128)} %bitcast_multiply_fusion, f32[]{:T(128)} %constant.64.clone.1), kind=kCustom, calls=%fused_computation.34 | custom fusion | flops 1048576 | bytes 1049088 | tf_op jit(solution)/shard_map/scatter-add | solution.py:123
  194.2 0.0 reduce-scatter.3.cloned.1.call-update
  194.2 0.0 reduce-scatter.5.cloned.1.call-start
  194.3 3.2 add_convert_fusion
  197.5 32.7 %all_to_all.20 = bf16[32,16,2048]{2,1,0:T(8,128)(2,1)} all-to-all(bf16[32,16,2048]{2,1,0:T(8,128)(2,1)S(1)} %bitcast.66), channel_id=1, replica_groups=mesh['dp'=32,'expert'=16] {'dp'}, dimensions={0} | all-to-all | bytes 4194304 | tf_op jit(solution)/shard_map/all_to_all | solution.py:110
  230.2 9.1 %scatter_custom_fusion.2 = f32[128,2048]{1,0:T(8,128)} fusion(s32[512]{0:T(512)S(1)} %get-tuple-element.18, bf16[512,2048]{1,0:T(8,128)(2,1)} %bitcast.68, f32[]{:T(128)} %constant.64.clone.1), kind=kCustom, calls=%fused_computation.11 | custom fusion | flops 2097152 | bytes 3145732 | tf_op jit(solution)/shard_map/scatter-add | solution.py:125
  239.3 0.0 reduce-scatter.5.cloned.1.call-update
  239.4 3.1 fusion.6
  242.4 3.1 fusion.5
  245.5 3.1 fusion.4
  248.5 2.2 fusion.1
  250.7 0.1 reshape.293
  250.8 3.5 %scatter_custom_fusion.3 = f32[1024]{0:T(1024)S(1)} fusion(s32[512]{0:T(512)S(1)} %get-tuple-element.17, f32[512]{0:T(512)S(1)} %reshape.293, f32[]{:T(128)} %constant.64.clone.1), kind=kCustom, calls=%fused_computation.85 | custom fusion | flops 512 | bytes 4100 | tf_op jit(solution)/shard_map/scatter-add | solution.py:130
  254.3 0.1 reshape.237
  254.4 54.8 %psum.7 = f32[128,8]{1,0:T(8,128)S(1)} all-reduce(f32[128,8]{1,0:T(8,128)S(1)} %reshape.237), channel_id=1, replica_groups=mesh['dp'=32,'expert'=16] {'expert'}, use_global_device_ids=true, to_apply=%region_10.11 | all-reduce | flops 1024 | bytes 8192 | tf_op jit(solution)/shard_map/psum | solution.py:137
  309.2 0.7 copy.19
  309.8 0.0 reduce-scatter.3.cloned.1.call-done
  309.8 1.5 convert_element_type.68
  311.3 20.1 %reduce-scatter.5.cloned.1.call-done = f32[128,128]{1,0:T(8,128)} async-done(((f32[128,2048]{1,0:T(8,128)}), f32[128,128]{1,0:T(8,128)}) %reduce-scatter.5.cloned.1.call-update) | async-done | bytes 65552 | tf_op jit(solution)/shard_map/reduce_scatter | solution.py:135
  331.4 1.5 convert_element_type.77
  (15 shorter events, 0.2 us)
Async XLA Ops:
  7.2 135.3 %copy-start = (bf16[1,192,2048]{2,1,0:T(8,128)(2,1)S(1)}, bf16[1,192,2048]{2,1,0:T(8,128)(2,1)}, u32[]{:S(2)}) copy-start(bf16[1,192,2048]{2,1,0:T(8,128)(2,1)} %param.13) | copy-start | bytes 2359300
  65.3 7.8 %copy-start.3 = (f32[128,8]{0,1:T(8,128)S(1)}, f32[128,8]{0,1:T(8,128)}, u32[]{:S(2)}) copy-start(f32[128,8]{0,1:T(8,128)} %param.10) | copy-start | bytes 12292
  65.3 43.3 %all-to-all-start = ((bf16[32,16,2048]{2,1,0:T(8,128)(2,1)}), bf16[32,16,2048]{2,1,0:T(8,128)(2,1)}, u32[]{:S(2)}, u32[]{:S(2)}) async-start(bf16[32,16,2048]{2,1,0:T(8,128)(2,1)} %broadcast_select_fusion), calls=%async_computation | async-start | bytes 4194304 | tf_op jit(solution)/shard_map/all_to_all | solution.py:97
  73.1 2.6 copy-start.2
  108.6 33.8 %all-to-all-start.2 = ((bf16[32,16,2048]{2,1,0:T(8,128)(2,1)}), bf16[32,16,2048]{2,1,0:T(8,128)(2,1)}, u32[]{:S(2)}, u32[]{:S(2)}) async-start(bf16[32,16,2048]{2,1,0:T(8,128)(2,1)} %fusion), calls=%async_computation.3 | async-start | bytes 4194304 | tf_op jit(solution)/shard_map/all_to_all | solution.py:107
  116.1 3.5 %copy-start.1 = (bf16[1,192,2048]{2,1,0:T(8,128)(2,1)S(1)}, bf16[1,192,2048]{2,1,0:T(8,128)(2,1)}, u32[]{:S(2)}) copy-start(bf16[1,192,2048]{2,1,0:T(8,128)(2,1)} %param.11) | copy-start | bytes 2359300
  147.2 33.7 %all-to-all-start.1 = ((bf16[32,16,2048]{2,1,0:T(8,128)(2,1)}), bf16[32,16,2048]{2,1,0:T(8,128)(2,1)}, u32[]{:S(2)}, u32[]{:S(2)}) async-start(bf16[32,16,2048]{2,1,0:T(8,128)(2,1)} %bitcast.67), calls=%async_computation.1 | async-start | bytes 4194304 | tf_op jit(solution)/shard_map/all_to_all | solution.py:100
  154.5 155.3 %reduce-scatter.3.cloned.1.call-start = ((), (), s32[]{:S(2)}) async-start(), calls=%async_computation.6 | async-start | bytes 1114112 | tf_op jit(solution)/shard_map/reduce_scatter | solution.py:134
  194.2 137.2 %reduce-scatter.5.cloned.1.call-start = ((), (), s32[]{:S(2)}) async-start(), calls=%async_computation.7 | async-start | bytes 1114112 | tf_op jit(solution)/shard_map/reduce_scatter | solution.py:135
Sparse Core Ops, SparseCore 0:
  194.4 65.5 reduce-scatter.2
  263.0 68.3 reduce-scatter.4
where the time goes:
time: 341 us; the launch traced here: 340 us
  blocking collectives  155 us (45%)
  waiting for transfers between devices  62.3 us (18%)
  other arithmetic  43.7 us (13%)
  matrix products  27.6 us (8%)
  starting transfers between devices  22.8 us (7%)
  between operations  14.3 us (4%)
  local copies, waits for them, and re-layouts  14.1 us (4%)
    psum x1, blocking collectives, per_device(): grad_gates = lax.psum(gate_part, 'expert')  54.8 us
    all_gather x1, blocking collectives, per_device(): lax.all_gather(tokens, 'expert', axis=1, tiled=True)  38.8 us
    all_to_all x1, blocking collectives, per_device(): lax.all_to_all(part_grad.reshape(dp_count, capacity, features), 'dp', spl...  32.7 us
    all_gather x1, blocking collectives, per_device(): lax.all_gather(cotangent, 'expert', axis=1, tiled=True)  28.7 us
    all_to_all x1, waiting for transfers between devices, per_device(): lax.all_to_all(expert_out.reshape(dp_count, capacity, features), 'dp', sp...  22.3 us
    reduce_scatter x1, waiting for transfers between devices, per_device(): lax.psum_scatter(grad_part, 'expert', scatter_dimension=1, tiled=True)  20.1 us
    all_to_all x1, waiting for transfers between devices, per_device(): lax.all_to_all(send_do, 'dp', split_axis=0, concat_axis=0, tiled=True)  19.7 us
    scatter-add x1, other arithmetic, per_device(): out_part = jnp.zeros((tok_count, width_now), jnp.float32).at[slot_token]....  9.44 us
  transfers between devices with their start and end apart: 5, of which 3 were waited for; matrix products, arithmetic and copies ran while one was open for 14% of the time, Pallas kernels for 0%

commit v1 on v0

--- a/solution.py
+++ b/solution.py
@@ -25,19 +25,12 @@
     )
 
 
-def forward_rows(rows_x, gate_w, up_w, down_w):
+def expert_rows(rows_x, rows_do, gate_w, up_w, down_w):
     pre_gate = contract_last(rows_x, gate_w)
     pre_up = contract_last(rows_x, up_w)
     activated, derivative = silu_parts(pre_gate)
     hidden = (activated * pre_up).astype(jnp.bfloat16)
-    return jnp.dot(hidden, down_w, preferred_element_type=jnp.float32).astype(jnp.bfloat16)
-
-
-def backward_rows(rows_x, rows_do, gate_w, up_w, down_w):
-    pre_gate = contract_last(rows_x, gate_w)
-    pre_up = contract_last(rows_x, up_w)
-    activated, derivative = silu_parts(pre_gate)
-    hidden = (activated * pre_up).astype(jnp.bfloat16)
+    part_out = jnp.dot(hidden, down_w, preferred_element_type=jnp.float32).astype(jnp.bfloat16)
     d_hidden = contract_last(rows_do, down_w)
     d_pre_gate = (d_hidden * pre_up * derivative).astype(jnp.bfloat16)
     d_pre_up = (d_hidden * activated).astype(jnp.bfloat16)
@@ -50,14 +43,12 @@
         contract_first(d_pre_up, rows_x),
         contract_first(hidden, rows_do),
     )
-    return (part_grad, gradients)
+    return (part_out, part_grad, gradients)
 
 
 def per_device(tokens, cotangent, expert_ids, gate_weights, w_gate, w_up, w_down):
-    full_x, full_dy = (
-        lax.all_gather(tokens, "expert", axis=1, tiled=True),
-        lax.all_gather(cotangent, "expert", axis=1, tiled=True),
-    )
+    both = lax.all_gather(jnp.stack([tokens, cotangent]), "expert", axis=2, tiled=True)
+    full_x, full_dy = both[0], both[1]
     dp_count = lax.axis_size("dp")
     column_count = lax.axis_size("expert")
     column = lax.axis_index("expert")
@@ -94,35 +85,33 @@
         (slot_gate[:, None] * slot_dy).astype(jnp.bfloat16).reshape(dp_count, capacity, features)
     )
     weights = (w_gate[0], w_up[0], w_down[0])
-    recv_x = lax.all_to_all(send_x, "dp", split_axis=0, concat_axis=0, tiled=True)
-    rows_x = recv_x.reshape(dp_count * capacity, features)
-    expert_out = forward_rows(rows_x, *weights)
-    back_out = lax.all_to_all(
-        expert_out.reshape(dp_count, capacity, features),
+    recv = lax.all_to_all(
+        jnp.concatenate([send_x, send_do], axis=1), "dp", split_axis=0, concat_axis=0, tiled=True
+    )
+    rows_x = recv[:, :capacity].reshape(dp_count * capacity, features)
+    rows_do = recv[:, capacity:].reshape(dp_count * capacity, features)
+    part_out, part_grad, gradients = expert_rows(rows_x, rows_do, *weights)
+    back = lax.all_to_all(
+        jnp.concatenate(
+            [
+                part_out.reshape(dp_count, capacity, features),
+                part_grad.reshape(dp_count, capacity, features),
+            ],
+            axis=1,
+        ),
         "dp",
         split_axis=0,
         concat_axis=0,
         tiled=True,
     )
-    recv_do = lax.all_to_all(send_do, "dp", split_axis=0, concat_axis=0, tiled=True)
-    rows_do = recv_do.reshape(dp_count * capacity, features)
-    part_grad, gradients = backward_rows(rows_x, rows_do, *weights)
-    back_grad = lax.all_to_all(
-        part_grad.reshape(dp_count, capacity, features),
-        "dp",
-        split_axis=0,
-        concat_axis=0,
-        tiled=True,
-    )
-    width_now = back_out.shape[2]
-    out_float = back_out.reshape(dp_count * capacity, width_now).astype(jnp.float32)
-    grad_float = back_grad.reshape(dp_count * capacity, width_now).astype(jnp.float32)
+    out_float = back[:, :capacity].reshape(dp_count * capacity, features).astype(jnp.float32)
+    grad_float = back[:, capacity:].reshape(dp_count * capacity, features).astype(jnp.float32)
     out_part = (
-        jnp.zeros((tok_count, width_now), jnp.float32)
+        jnp.zeros((tok_count, features), jnp.float32)
         .at[slot_token]
         .add(slot_gate[:, None] * out_float)
     )
-    grad_part = jnp.zeros((tok_count, width_now), jnp.float32).at[slot_token].add(grad_float)
+    grad_part = jnp.zeros((tok_count, features), jnp.float32).at[slot_token].add(grad_float)
     gate_terms = jnp.sum(slot_dy * out_float, axis=1)
     gate_part = (
         jnp.zeros((assigned,), jnp.float32)
@@ -130,14 +119,13 @@
         .add(gate_terms, mode="drop")
         .reshape(tok_count, chosen)
     )
-    out_slice, grad_slice = (
-        lax.psum_scatter(out_part, "expert", scatter_dimension=1, tiled=True),
-        lax.psum_scatter(grad_part, "expert", scatter_dimension=1, tiled=True),
+    summed = lax.psum_scatter(
+        jnp.stack([out_part, grad_part]), "expert", scatter_dimension=2, tiled=True
     )
     grad_gates = lax.psum(gate_part, "expert")
     return (
-        out_slice.astype(jnp.bfloat16),
-        grad_slice.astype(jnp.bfloat16),
+        summed[0].astype(jnp.bfloat16),
+        summed[1].astype(jnp.bfloat16),
         grad_gates,
         gradients[0].astype(jnp.bfloat16)[None],
         gradients[1].astype(jnp.bfloat16)[None],

time: 341 us -> 320 us (0.938)
  starting transfers between devices: 22.8 us -> 0.08 us
  matrix products: 27.6 us -> 11.1 us
  blocking collectives: 155 us -> 165 us
  local copies, waits for them, and re-layouts: 14.1 us -> 20.7 us
    all_to_all x1 -> x2, blocking collectives: 32.7 us -> 111 us  [the longest x1 56.2 us: per_device(): lax.all_to_all(jnp.concatenate([send_x, send_do], axis=1), 'dp', split_ax...]
    all_gather x2 -> x0, blocking collectives: 67.5 us -> none  [the longest x1 38.8 us: per_device(): lax.all_gather(tokens, 'expert', axis=1, tiled=True)]
    all_gather x0 -> x1, waiting for transfers between devices: none -> 60 us  [per_device(): lax.all_gather(jnp.stack([tokens, cotangent]), 'expert', axis=2, tiled=True)]
    all_to_all x3 -> x0, waiting for transfers between devices: 42.1 us -> none  [the longest x1 22.3 us: per_device(): lax.all_to_all(expert_out.reshape(dp_count, capacity, features), 'dp', sp...]
    all_to_all x3 -> x0, starting transfers between devices: 22.5 us -> none  [the longest x1 7.79 us: per_device(): lax.all_to_all(send_x, 'dp', split_axis=0, concat_axis=0, tiled=True)]
    reduce_scatter x2 -> x1, waiting for transfers between devices: 20.1 us -> 1.92 us  [per_device(): lax.psum_scatter(jnp.stack([out_part, grad_part]), 'expert', scatter_dime...]
    dot_general x3, matrix products: 9.06 us -> 2.26 us  [the longest x1 0.77 us: expert_rows(): jnp.dot(d_pre_up, up_w, preferred_element_type=jnp.float32)]
    dot_general x3, matrix products: 9.3 us -> 2.72 us  [contract_last(): lax.dot_general(first_op, second_op, (((1,), (1,)), ((), ())), preferred_...]
  transfers between devices with their start and end apart: 5 -> 2, of which waited for: 3 -> 2; matrix products, arithmetic and copies ran while one was open for 14% -> 9% of each run, Pallas kernels for 0% -> 0%
where the time goes in v1:
time: 320 us; the launch traced here: 319 us
  blocking collectives  165 us (52%)
  waiting for transfers between devices  62 us (19%)
  other arithmetic  45.8 us (14%)
  local copies, waits for them, and re-layouts  20.7 us (6%)
  between operations  14.4 us (4%)
  matrix products  11.1 us (3%)
    all_gather x1, waiting for transfers between devices, per_device(): lax.all_gather(jnp.stack([tokens, cotangent]), 'expert', axis=2, tiled=True)  60 us
    all_to_all x1, blocking collectives, per_device(): lax.all_to_all(jnp.concatenate([send_x, send_do], axis=1), 'dp', split_ax...  56.2 us
    psum x1, blocking collectives, per_device(): grad_gates = lax.psum(gate_part, 'expert')  54.6 us
    all_to_all x1, blocking collectives, per_device(): lax.all_to_all(jnp.concatenate([part_out.reshape(dp_count, capacity, feat...  54.4 us
    another operation x3, other arithmetic  9.96 us
    scatter-add x1, other arithmetic, per_device(): out_part = jnp.zeros((tok_count, features), jnp.float32).at[slot_token].a...  9.44 us
    scatter-add x1, other arithmetic, per_device(): jnp.zeros((tok_count, features), jnp.float32).at[slot_token].add(grad_float)  9.14 us
  transfers between devices with their start and end apart: 2, of which 2 were waited for; matrix products, arithmetic and copies ran while one was open for 9% of the time, Pallas kernels for 0%

profile of v1, /device:TPU:6, one launch (start us, length us, event | category | flops | bytes accessed | tf_op | source)
XLA Modules:
  0.0 319.3 jit_solution(1115190527233137053)
XLA Ops:
  7.2 0.0 copy-start
  7.2 0.0 all-gather.2.cloned.1.call-start
  7.2 1.5 pad_maximum_fusion.3
  8.7 0.0 all-gather.2.cloned.1.call-update
  8.7 0.0 reduce-scatter.2.cloned.1.call-start
  8.8 0.8 copy.13
  9.6 0.1 reshape.232
  9.7 0.1 reshape.231
  9.8 0.1 reshape.230
  9.9 0.8 copy.18
  10.7 0.1 reshape.234
  10.8 9.0 %reduce-window.6 = s32[32,8,128]{2,1,0:T(8,128)S(1)} reduce-window(s32[32,8,128]{2,1,0:T(8,128)S(1)} %fusion.25, s32[]{:T(128)} %constant.66.clone.1), window={size=1x1x128 pad=0_0x0_0x127_0}, to_apply=%region_0.1 | reduce-window | flops 4161536 | bytes 262148 | tf_op jit(solution)/shard_map/reduce-window
  19.8 0.1 slice.48
  19.9 0.1 copy.16
  20.1 0.1 copy.17
  20.2 0.1 add_add_fusion
  20.4 4.3 %scatter_custom_fusion = s32[512]{0:T(512)S(1)} fusion(s32[1024]{0:T(1024)S(1)} %bitcast.94, s32[1024]{0:T(1024)S(1)} %iota.11, s32[]{:T(128)} %constant.65.clone.1), kind=kCustom, calls=%fused_computation.100 | custom fusion | bytes 2052 | tf_op jit(solution)/shard_map/scatter | solution.py:74
  24.7 0.1 broadcast_in_dim.62
  24.8 2.3 gather_fusion
  27.2 0.1 mul.64
  27.3 60.0 %all-gather.2.cloned.1.call-done = bf16[2,128,2048]{2,1,0:T(8,128)(2,1)} async-done(((bf16[2,128,128]{2,1,0:T(8,128)(2,1)}), bf16[2,128,2048]{2,1,0:T(8,128)(2,1)}) %all-gather.2.cloned.1.call-update) | async-done | bytes 1048592 | tf_op jit(solution)/shard_map/all_gather | solution.py:50
  87.3 1.3 slice_bitcast_fusion.1
  88.6 3.3 %gather_fusion.2 = bf16[512,2048]{1,0:T(8,128)(2,1)} fusion(bf16[128,2048]{1,0:T(8,128)(2,1)S(1)} %get-tuple-element.19, s32[1024]{0:T(1024)S(1)} %pad_clamp_fusion), kind=kCustom, calls=%fused_computation.2 | custom fusion | bytes 4196352 | tf_op jit(solution)/shard_map/gather | solution.py:80
  91.9 3.3 %gather_fusion.1 = bf16[512,2048]{1,0:T(8,128)(2,1)} fusion(bf16[128,2048]{1,0:T(8,128)(2,1)S(1)} %get-tuple-element.18, s32[1024]{0:T(1024)S(1)} %pad_clamp_fusion), kind=kCustom, calls=%fused_computation.1 | custom fusion | bytes 4196352 | tf_op jit(solution)/shard_map/gather | solution.py:81
  95.2 1.9 broadcast_select_fusion
  97.2 0.3 copy-done.3
  97.4 0.4 fusion
  97.8 0.6 pad_maximum_fusion
  98.4 56.2 %all_to_all.10 = bf16[32,32,2048]{2,1,0:T(8,128)(2,1)S(1)} all-to-all(bf16[32,32,2048]{2,1,0:T(8,128)(2,1)S(1)} %pad_maximum_fusion), channel_id=1, replica_groups=mesh['dp'=32,'expert'=16] {'dp'}, dimensions={0} | all-to-all | bytes 8388608 | tf_op jit(solution)/shard_map/all_to_all | solution.py:88
  154.7 0.6 fusion.38
  155.2 0.0 copy-start.6
  155.3 0.0 copy-start.4
  155.3 0.5 copy-done.8
  155.8 0.9 fusion.7
  156.7 0.8 copy-done.7
  157.5 0.8 fusion.15
  158.4 0.0 copy-done.4
  158.4 0.0 copy-done
  158.4 1.0 multiply_convert_fusion.2
  159.4 0.7 convolution_convert_fusion
  160.1 0.8 fusion.13
  160.9 0.8 add_convert_fusion
  161.7 0.6 pad_maximum_fusion.1
  162.2 54.4 %all_to_all.11 = bf16[32,32,2048]{2,1,0:T(8,128)(2,1)S(1)} all-to-all(bf16[32,32,2048]{2,1,0:T(8,128)(2,1)S(1)} %pad_maximum_fusion.1), channel_id=1, replica_groups=mesh['dp'=32,'expert'=16] {'dp'}, dimensions={0} | all-to-all | bytes 8388608 | tf_op jit(solution)/shard_map/all_to_all | solution.py:94
  216.6 2.5 slice_convert_fusion
  219.1 0.1 copy-done.1
  219.2 2.3 bitcast_multiply_fusion
  221.5 9.4 %scatter_custom_fusion.1 = f32[128,2048]{1,0:T(8,128)} fusion(s32[512]{0:T(512)S(1)} %get-tuple-element.26, f32[512,2048]{1,0:T(8,128)} %bitcast_multiply_fusion, f32[]{:T(128)} %constant.64.clone.1), kind=kCustom, calls=%fused_computation.40 | custom fusion | flops 1048576 | bytes 1049088 | tf_op jit(solution)/shard_map/scatter-add | solution.py:112
  231.0 9.1 %scatter_custom_fusion.2 = f32[128,2048]{1,0:T(8,128)} fusion(s32[512]{0:T(512)S(1)} %get-tuple-element.26, bf16[512,2048]{1,0:T(8,128)(2,1)} %bitcast.82, f32[]{:T(128)} %constant.64.clone.1), kind=kCustom, calls=%fused_computation.13 | custom fusion | flops 2097152 | bytes 3145732 | tf_op jit(solution)/shard_map/scatter-add | solution.py:114
  240.1 3.1 pad_maximum_fusion.2
  243.2 0.0 reduce-scatter.2.cloned.1.call-update
  243.2 0.0 copy-start.5
  243.2 3.2 %fusion.6 = bf16[1,192,2048]{2,1,0:T(8,128)(2,1)} fusion(bf16[512,192]{0,1:T(8,128)(2,1)S(1)} %get-tuple-element.20, bf16[512,2048]{1,0:T(8,128)(2,1)} %bitcast.85), kind=kOutput, calls=%fused_computation.23 | convolution fusion | flops 403046400 | bytes 3080192 | tf_op jit(solution)/shard_map/dot_general | solution.py:23
  246.5 1.5 fusion.4
  247.9 1.5 fusion.5
  249.4 0.6 fusion.1
  250.0 0.1 reshape.295
  250.1 3.5 %scatter_custom_fusion.3 = f32[1024]{0:T(1024)S(1)} fusion(s32[512]{0:T(512)S(1)} %get-tuple-element.25, f32[512]{0:T(512)S(1)} %reshape.295, f32[]{:T(128)} %constant.64.clone.1), kind=kCustom, calls=%fused_computation.94 | custom fusion | flops 512 | bytes 4100 | tf_op jit(solution)/shard_map/scatter-add | solution.py:119
  253.6 0.1 reshape.239
  253.7 54.6 %psum.7 = f32[128,8]{1,0:T(8,128)S(1)} all-reduce(f32[128,8]{1,0:T(8,128)S(1)} %reshape.239), channel_id=1, replica_groups=mesh['dp'=32,'expert'=16] {'expert'}, use_global_device_ids=true, to_apply=%region_9.10 | all-reduce | flops 1024 | bytes 8192 | tf_op jit(solution)/shard_map/psum | solution.py:125
  308.3 0.7 copy.19
  309.0 1.9 reduce-scatter.2.cloned.1.call-done
  310.9 0.9 convert.7
  311.8 0.6 slice_bitcast_fusion.2
  (23 shorter events, 0.2 us)
Async XLA Ops:
  7.2 151.2 %copy-start = (bf16[1,192,2048]{2,1,0:T(8,128)(2,1)S(1)}, bf16[1,192,2048]{2,1,0:T(8,128)(2,1)}, u32[]{:S(2)}) copy-start(bf16[1,192,2048]{2,1,0:T(8,128)(2,1)} %param.12) | copy-start | bytes 2359300
  7.2 80.1 %all-gather.2.cloned.1.call-start = ((), (), s32[]{:S(2)}) async-start(), calls=%async_computation.3 | async-start | bytes 1114112 | tf_op jit(solution)/shard_map/all_gather | solution.py:50
  8.7 302.2 %reduce-scatter.2.cloned.1.call-start = ((), (), s32[]{:S(2)}) async-start(), calls=%async_computation.4 | async-start | bytes 2228224 | tf_op jit(solution)/shard_map/reduce_scatter | solution.py:122
  95.2 2.2 copy-start.3
  154.7 1.1 copy-start.8
  155.2 1.4 copy-start.6
  155.3 3.1 copy-start.4
  155.8 1.7 copy-start.7
  216.6 2.6 copy-start.1
  243.2 3.2 %copy-start.5 = (bf16[32,16,2048]{2,1,0:T(8,128)(2,1)S(1)}, bf16[32,16,2048]{2,1,0:T(8,128)(2,1)}, u32[]{:S(2)}) copy-start(bf16[32,16,2048]{2,1,0:T(8,128)(2,1)} %copy-done.4) | copy-start | bytes 6291460
  246.5 2.9 copy-start.2
Sparse Core Ops, SparseCore 0:
  10.6 76.6 all-gather.1
  243.4 67.4 reduce-scatter.1

commit v2 on v1

--- a/solution.py
+++ b/solution.py
@@ -60,27 +60,26 @@
     assigned = tok_count * chosen
     flat_ids = expert_ids.reshape(-1)
     flat_gates = gate_weights.reshape(-1)
+    slot_total = dp_count * capacity
     owned_here = flat_ids % per_row == column // SHARDS
     target_row = flat_ids // per_row
     onehot = (
         (target_row[:, None] == jnp.arange(dp_count, dtype=jnp.int32)[None, :])
         & owned_here[:, None]
-    ).astype(jnp.int32)
-    rank_of = jnp.sum((jnp.cumsum(onehot, axis=0) - 1) * onehot, axis=1)
-    target = jnp.where(owned_here, target_row * capacity + rank_of, dp_count * capacity)
-    slot_src = (
-        jnp.full((dp_count * capacity,), assigned, jnp.int32)
-        .at[target]
-        .set(jnp.arange(assigned, dtype=jnp.int32), mode="drop")
-    )
-    filled = slot_src < assigned
-    safe_index = jnp.where(filled, slot_src, 0)
-    slot_token = safe_index // chosen
-    slot_gate = jnp.where(filled, flat_gates[safe_index], 0.0)
-    slot_dy = full_dy[slot_token].astype(jnp.float32)
-    send_x = jnp.where(filled[:, None], full_x[slot_token], jnp.zeros((), full_x.dtype)).reshape(
+    ).astype(jnp.bfloat16)
+    order = jnp.arange(assigned, dtype=jnp.int32)
+    earlier = (order[:, None] > order[None, :]).astype(jnp.bfloat16)
+    counts = jnp.dot(earlier, onehot, preferred_element_type=jnp.float32)
+    rank_of = jnp.sum(counts * onehot.astype(jnp.float32), axis=1).astype(jnp.int32)
+    target = jnp.where(owned_here, target_row * capacity + rank_of, slot_total)
+    picks = target[None, :] == jnp.arange(slot_total, dtype=jnp.int32)[:, None]
+    slot_gate = jnp.sum(jnp.where(picks, flat_gates[None, :], 0.0), axis=1)
+    token_of = jnp.any(picks.reshape(slot_total, tok_count, chosen), axis=2)
+    token_pick = token_of.astype(jnp.bfloat16)
+    send_x = jnp.dot(token_pick, full_x, preferred_element_type=jnp.bfloat16).reshape(
         dp_count, capacity, features
     )
+    slot_dy = jnp.dot(token_pick, full_dy, preferred_element_type=jnp.float32)
     send_do = (
         (slot_gate[:, None] * slot_dy).astype(jnp.bfloat16).reshape(dp_count, capacity, features)
     )
@@ -104,20 +103,20 @@
         concat_axis=0,
         tiled=True,
     )
-    out_float = back[:, :capacity].reshape(dp_count * capacity, features).astype(jnp.float32)
-    grad_float = back[:, capacity:].reshape(dp_count * capacity, features).astype(jnp.float32)
-    out_part = (
-        jnp.zeros((tok_count, features), jnp.float32)
-        .at[slot_token]
-        .add(slot_gate[:, None] * out_float)
+    back_out = back[:, :capacity].reshape(slot_total, features)
+    back_grad = back[:, capacity:].reshape(slot_total, features)
+    gated_pick = token_pick.astype(jnp.float32) * slot_gate[:, None]
+    out_part = lax.dot_general(
+        gated_pick,
+        back_out.astype(jnp.float32),
+        (((0,), (0,)), ((), ())),
+        precision=lax.Precision.HIGHEST,
+        preferred_element_type=jnp.float32,
     )
-    grad_part = jnp.zeros((tok_count, features), jnp.float32).at[slot_token].add(grad_float)
-    gate_terms = jnp.sum(slot_dy * out_float, axis=1)
-    gate_part = (
-        jnp.zeros((assigned,), jnp.float32)
-        .at[slot_src]
-        .add(gate_terms, mode="drop")
-        .reshape(tok_count, chosen)
+    grad_part = contract_first(token_pick, back_grad)
+    gate_terms = jnp.sum(slot_dy * back_out.astype(jnp.float32), axis=1)
+    gate_part = jnp.sum(jnp.where(picks, gate_terms[:, None], 0.0), axis=0).reshape(
+        tok_count, chosen
     )
     summed = lax.psum_scatter(
         jnp.stack([out_part, grad_part]), "expert", scatter_dimension=2, tiled=True

time: 320 us -> 290 us (0.906)
  other arithmetic: 45.8 us -> 7.12 us
  waiting for transfers between devices: 62 us -> 80.5 us
  local copies, waits for them, and re-layouts: 20.7 us -> 4.79 us
  matrix products: 11.1 us -> 17.6 us
    scatter-add x3 -> x0, other arithmetic: 22 us -> none  [the longest x1 9.44 us: per_device(): out_part = jnp.zeros((tok_count, features), jnp.float32).at[slot_token].a...]
    all_gather x1, waiting for transfers between devices: 60 us -> 75.4 us  [per_device(): lax.all_gather(jnp.stack([tokens, cotangent]), 'expert', axis=2, tiled=True)]
    another operation x3 -> x1, other arithmetic: 9.96 us -> 0.91 us
    gather x3 -> x0, local copies, waits for them, and re-layouts: 8.92 us -> none  [the longest x1 3.35 us: per_device(): slot_dy = full_dy[slot_token].astype(jnp.float32)]
    dot_general x0 -> x4, matrix products: none -> 6.12 us  [the longest x1 2.62 us: per_device(): slot_dy = jnp.dot(token_pick, full_dy, preferred_element_type=jnp.float32)]
    scatter x1 -> x0, local copies, waits for them, and re-layouts: 4.3 us -> none  [per_device(): slot_src = jnp.full((dp_count * capacity,), assigned, jnp.int32).at[targe...]
    dot_general x3 -> x4, matrix products: 6.13 us -> 6.62 us  [contract_first(): lax.dot_general(first_op, second_op, (((0,), (0,)), ((), ())), preferred_...]
  transfers between devices with their start and end apart: 2 -> 2, of which waited for: 2 -> 2; matrix products, arithmetic and copies ran while one was open for 9% -> 4% of each run, Pallas kernels for 0% -> 0%
where the time goes in v2:
time: 290 us
  blocking collectives  165 us (57%)
  waiting for transfers between devices  80.5 us (28%)
  matrix products  17.6 us (6%)
  between operations  14.3 us (5%)
  other arithmetic  7.12 us (2%)
  local copies, waits for them, and re-layouts  4.79 us (2%)
    all_gather x1, waiting for transfers between devices, per_device(): lax.all_gather(jnp.stack([tokens, cotangent]), 'expert', axis=2, tiled=True)  75.4 us
    all_to_all x1, blocking collectives, per_device(): lax.all_to_all(jnp.concatenate([send_x, send_do], axis=1), 'dp', split_ax...  56.2 us
    psum x1, blocking collectives, per_device(): grad_gates = lax.psum(gate_part, 'expert')  54.6 us
    all_to_all x1, blocking collectives, per_device(): lax.all_to_all(jnp.concatenate([part_out.reshape(dp_count, capacity, feat...  54.4 us
    dot_general x4, matrix products, contract_first(): lax.dot_general(first_op, second_op, (((0,), (0,)), ((), ())), preferred_...  6.62 us
  transfers between devices with their start and end apart: 2, of which 2 were waited for; matrix products, arithmetic and copies ran while one was open for 4% of the time, Pallas kernels for 0%

profile of v2, /device:TPU:6, one launch (start us, length us, event | category | flops | bytes accessed | tf_op | source)
XLA Modules:
  0.0 289.7 jit_solution(13221240471590815233)
XLA Ops:
  7.2 0.0 copy-start
  7.2 0.0 copy-start.8
  7.2 0.0 all-gather.2.cloned.1.call-start
  7.2 1.5 pad_maximum_fusion.3
  8.7 0.0 all-gather.2.cloned.1.call-update
  8.7 0.0 reduce-scatter.2.cloned.1.call-start
  8.8 0.8 copy.21
  9.6 0.1 reshape.162
  9.7 0.5 fusion.6
  10.3 0.1 convert_element_type.66
  10.4 0.1 fusion.30
  10.5 0.0 copy-done.8
  10.5 0.1 copy.27
  10.6 0.1 broadcast_in_dim.51
  10.7 0.9 fusion.4
  11.6 0.3 select_reduce_fusion.1
  11.9 75.4 %all-gather.2.cloned.1.call-done = bf16[2,128,2048]{2,1,0:T(8,128)(2,1)} async-done(((bf16[2,128,128]{2,1,0:T(8,128)(2,1)}), bf16[2,128,2048]{2,1,0:T(8,128)(2,1)}) %all-gather.2.cloned.1.call-update) | async-done | bytes 1048592 | tf_op jit(solution)/shard_map/all_gather | solution.py:50
  87.3 0.0 copy-start.5
  87.3 1.8 fusion.18
  89.1 0.0 copy-done.5
  89.2 2.6 multiply_convert_fusion
  91.8 0.6 pad_maximum_fusion
  92.4 56.2 %all_to_all.10 = bf16[32,32,2048]{2,1,0:T(8,128)(2,1)S(1)} all-to-all(bf16[32,32,2048]{2,1,0:T(8,128)(2,1)S(1)} %pad_maximum_fusion), channel_id=1, replica_groups=mesh['dp'=32,'expert'=16] {'dp'}, dimensions={0} | all-to-all | bytes 8388608 | tf_op jit(solution)/shard_map/all_to_all | solution.py:87
  148.6 0.0 copy-start.7
  148.6 0.4 fusion.39
  149.0 0.0 copy-start.4
  149.0 0.7 copy-done.7
  149.7 0.0 copy-start.6
  149.7 0.8 fusion.7
  150.6 0.0 copy-done.4
  150.6 0.3 copy-done.6
  150.9 0.8 fusion.15
  151.7 0.0 copy-done
  151.7 0.9 multiply_convert_fusion.3
  152.7 0.7 convolution_convert_fusion
  153.5 0.8 fusion.13
  154.2 0.8 add_convert_fusion
  155.0 0.6 pad_maximum_fusion.1
  155.6 54.4 %all_to_all.11 = bf16[32,32,2048]{2,1,0:T(8,128)(2,1)S(1)} all-to-all(bf16[32,32,2048]{2,1,0:T(8,128)(2,1)S(1)} %pad_maximum_fusion.1), channel_id=1, replica_groups=mesh['dp'=32,'expert'=16] {'dp'}, dimensions={0} | all-to-all | bytes 8388608 | tf_op jit(solution)/shard_map/all_to_all | solution.py:93
  209.9 0.6 fusion.38
  210.5 0.0 copy-start.1
  210.5 0.5 convolution_bitcast_fusion.1
  211.0 1.1 convolution_bitcast_fusion
  212.2 0.0 copy-done.1
  212.2 1.5 pad_maximum_fusion.2
  213.7 0.0 reduce-scatter.2.cloned.1.call-update
  213.7 0.0 copy-start.3
  213.7 3.2 %fusion.3 = bf16[1,192,2048]{2,1,0:T(8,128)(2,1)} fusion(bf16[512,192]{0,1:T(8,128)(2,1)S(1)} %get-tuple-element.22, bf16[512,2048]{1,0:T(8,128)(2,1)} %bitcast.75), kind=kOutput, calls=%fused_computation.15 | convolution fusion | flops 403046400 | bytes 3080192 | tf_op jit(solution)/shard_map/dot_general | solution.py:23
  216.9 1.5 fusion.1
  218.4 0.0 copy-start.2
  218.4 1.5 fusion.2
  219.8 0.0 copy-done.3
  219.8 0.2 copy-done.2
  220.0 0.5 multiply_reduce_fusion
  220.5 0.3 select_reduce_fusion
  220.9 0.1 reshape.170
  221.0 54.6 %psum.7 = f32[128,8]{1,0:T(8,128)S(1)} all-reduce(f32[128,8]{1,0:T(8,128)S(1)} %reshape.170), channel_id=1, replica_groups=mesh['dp'=32,'expert'=16] {'expert'}, use_global_device_ids=true, to_apply=%region_6.7 | all-reduce | flops 1024 | bytes 8192 | tf_op jit(solution)/shard_map/psum | solution.py:124
  275.5 0.7 copy.28
  276.2 5.1 %reduce-scatter.2.cloned.1.call-done = f32[2,128,128]{2,1,0:T(8,128)} async-done(((f32[2,128,2048]{2,1,0:T(8,128)}), f32[2,128,128]{2,1,0:T(8,128)}) %reduce-scatter.2.cloned.1.call-update) | async-done | bytes 131088 | tf_op jit(solution)/shard_map/reduce_scatter | solution.py:121
  281.3 0.9 convert.4
  282.2 0.6 slice_bitcast_fusion.4
  (5 shorter events, 0.1 us)
Async XLA Ops:
  7.2 144.6 %copy-start = (bf16[1,192,2048]{2,1,0:T(8,128)(2,1)S(1)}, bf16[1,192,2048]{2,1,0:T(8,128)(2,1)}, u32[]{:S(2)}) copy-start(bf16[1,192,2048]{2,1,0:T(8,128)(2,1)} %param.12) | copy-start | bytes 2359300
  7.2 3.3 %copy-start.8 = (f32[128,8]{0,1:T(8,128)S(1)}, f32[128,8]{0,1:T(8,128)}, u32[]{:S(2)}) copy-start(f32[128,8]{0,1:T(8,128)} %param.10) | copy-start | bytes 12292
  7.2 80.1 %all-gather.2.cloned.1.call-start = ((), (), s32[]{:S(2)}) async-start(), calls=%async_computation.3 | async-start | bytes 1114112 | tf_op jit(solution)/shard_map/all_gather | solution.py:50
  8.7 272.6 %reduce-scatter.2.cloned.1.call-start = ((), (), s32[]{:S(2)}) async-start(), calls=%async_computation.4 | async-start | bytes 2228224 | tf_op jit(solution)/shard_map/reduce_scatter | solution.py:121
  87.3 1.8 copy-start.5
  148.6 1.1 copy-start.7
  149.0 1.5 copy-start.4
  149.7 1.2 copy-start.6
  210.5 1.7 copy-start.1
  213.7 6.1 %copy-start.3 = (f32[512,2048]{1,0:T(8,128)S(1)}, f32[512,2048]{1,0:T(8,128)}, u32[]{:S(2)}) copy-start(f32[512,2048]{1,0:T(8,128)} %get-tuple-element.28) | copy-start | bytes 12582916
  218.4 1.7 copy-start.2
Sparse Core Ops, SparseCore 0:
  10.6 76.6 all-gather.1
  213.8 67.4 reduce-scatter.1

commit v3 on v2

--- a/solution.py
+++ b/solution.py
@@ -47,8 +47,8 @@
 
 
 def per_device(tokens, cotangent, expert_ids, gate_weights, w_gate, w_up, w_down):
-    both = lax.all_gather(jnp.stack([tokens, cotangent]), "expert", axis=2, tiled=True)
-    full_x, full_dy = both[0], both[1]
+    full_x = lax.all_gather(tokens, "expert", axis=1, tiled=True)
+    full_dy = lax.all_gather(cotangent, "expert", axis=1, tiled=True)
     dp_count = lax.axis_size("dp")
     column_count = lax.axis_size("expert")
     column = lax.axis_index("expert")

time: 290 us -> 282 us (0.972)
  waiting for transfers between devices: 80.5 us -> 5.61 us
  blocking collectives: 165 us -> 233 us
    all_gather x1 -> x0, waiting for transfers between devices: 75.4 us -> none  [per_device(): lax.all_gather(jnp.stack([tokens, cotangent]), 'expert', axis=2, tiled=True)]
    all_gather x0 -> x2, blocking collectives: none -> 67.7 us  [the longest x1 38.6 us: per_device(): full_x = lax.all_gather(tokens, 'expert', axis=1, tiled=True)]
  transfers between devices with their start and end apart: 2 -> 1, of which waited for: 2 -> 1; matrix products, arithmetic and copies ran while one was open for 4% -> 3% of each run, Pallas kernels for 0% -> 0%
where the time goes in v3:
time: 282 us; the launch traced here: 281 us
  blocking collectives  233 us (83%)
  matrix products  16.5 us (6%)
  between operations  14.3 us (5%)
  other arithmetic  5.67 us (2%)
  waiting for transfers between devices  5.61 us (2%)
  local copies, waits for them, and re-layouts  5.53 us (2%)
    all_to_all x1, blocking collectives, per_device(): lax.all_to_all(jnp.concatenate([send_x, send_do], axis=1), 'dp', split_ax...  56.4 us
    psum x1, blocking collectives, per_device(): grad_gates = lax.psum(gate_part, 'expert')  54.7 us
    all_to_all x1, blocking collectives, per_device(): lax.all_to_all(jnp.concatenate([part_out.reshape(dp_count, capacity, feat...  54.4 us
    all_gather x1, blocking collectives, per_device(): full_x = lax.all_gather(tokens, 'expert', axis=1, tiled=True)  38.6 us
    all_gather x1, blocking collectives, per_device(): full_dy = lax.all_gather(cotangent, 'expert', axis=1, tiled=True)  29.2 us
    dot_general x4, matrix products, contract_first(): lax.dot_general(first_op, second_op, (((0,), (0,)), ((), ())), preferred_...  6.62 us
  transfers between devices with their start and end apart: 1, of which 1 were waited for; matrix products, arithmetic and copies ran while one was open for 3% of the time, Pallas kernels for 0%

profile of v3, /device:TPU:6, one launch (start us, length us, event | category | flops | bytes accessed | tf_op | source)
XLA Modules:
  0.0 280.9 jit_solution(4906496111635461927)
XLA Ops:
  7.2 0.0 copy-start
  7.2 0.0 copy-start.7
  7.2 0.0 copy-start.8
  7.2 0.0 reduce-scatter.2.cloned.1.call-start
  7.3 0.8 copy.21
  8.1 0.1 reshape.162
  8.2 0.5 fusion.6
  8.8 0.1 convert_element_type.66
  8.9 0.1 fusion.30
  9.0 0.9 fusion.4
  9.9 0.8 copy.27
  10.7 0.1 broadcast_in_dim.51
  10.8 0.0 copy-done.7
  10.8 38.6 %all_gather.6 = bf16[128,2048]{1,0:T(8,128)(2,1)S(1)} all-gather(bf16[128,128]{1,0:T(8,128)(2,1)S(1)} %copy-done.7), channel_id=1, replica_groups=mesh['dp'=32,'expert'=16] {'expert'}, dimensions={1}, use_global_device_ids=true | all-gather | bytes 557056 | tf_op jit(solution)/shard_map/all_gather | solution.py:50
  49.4 0.0 copy-done.8
  49.4 29.2 %all_gather.7 = bf16[128,2048]{1,0:T(8,128)(2,1)S(1)} all-gather(bf16[128,128]{1,0:T(8,128)(2,1)S(1)} %copy-done.8), channel_id=1, replica_groups=mesh['dp'=32,'expert'=16] {'expert'}, dimensions={1}, use_global_device_ids=true | all-gather | bytes 557056 | tf_op jit(solution)/shard_map/all_gather | solution.py:51
  78.6 0.3 select_reduce_fusion.1
  78.8 0.7 fusion.17
  79.6 2.6 multiply_convert_fusion
  82.2 0.6 pad_maximum_fusion
  82.8 56.4 %all_to_all.10 = bf16[32,32,2048]{2,1,0:T(8,128)(2,1)S(1)} all-to-all(bf16[32,32,2048]{2,1,0:T(8,128)(2,1)S(1)} %pad_maximum_fusion), channel_id=1, replica_groups=mesh['dp'=32,'expert'=16] {'dp'}, dimensions={0} | all-to-all | bytes 8388608 | tf_op jit(solution)/shard_map/all_to_all | solution.py:87
  139.1 0.0 copy-start.6
  139.1 0.4 fusion.39
  139.6 0.0 copy-start.4
  139.6 0.7 copy-done.6
  140.3 0.0 copy-start.5
  140.3 0.8 fusion.7
  141.1 0.0 copy-done.4
  141.1 0.3 copy-done.5
  141.4 0.8 fusion.15
  142.3 0.0 copy-done
  142.3 0.9 multiply_convert_fusion.3
  143.2 0.7 convolution_convert_fusion
  144.0 0.8 fusion.13
  144.8 0.8 add_convert_fusion
  145.5 0.6 pad_maximum_fusion.1
  146.1 54.4 %all_to_all.11 = bf16[32,32,2048]{2,1,0:T(8,128)(2,1)S(1)} all-to-all(bf16[32,32,2048]{2,1,0:T(8,128)(2,1)S(1)} %pad_maximum_fusion.1), channel_id=1, replica_groups=mesh['dp'=32,'expert'=16] {'dp'}, dimensions={0} | all-to-all | bytes 8388608 | tf_op jit(solution)/shard_map/all_to_all | solution.py:93
  200.5 0.6 fusion.38
  201.1 0.0 copy-start.1
  201.1 0.5 convolution_bitcast_fusion.1
  201.6 1.1 convolution_bitcast_fusion
  202.7 0.0 copy-done.1
  202.7 1.5 pad_maximum_fusion.2
  204.2 0.0 reduce-scatter.2.cloned.1.call-update
  204.2 0.0 copy-start.3
  204.3 3.2 %fusion.3 = bf16[1,192,2048]{2,1,0:T(8,128)(2,1)} fusion(bf16[512,192]{0,1:T(8,128)(2,1)S(1)} %get-tuple-element.22, bf16[512,2048]{1,0:T(8,128)(2,1)} %bitcast.68), kind=kOutput, calls=%fused_computation.15 | convolution fusion | flops 403046400 | bytes 3080192 | tf_op jit(solution)/shard_map/dot_general | solution.py:23
  207.5 1.5 fusion.1
  208.9 0.0 copy-start.2
  208.9 1.5 fusion.2
  210.4 0.0 copy-done.3
  210.4 0.2 copy-done.2
  210.6 0.5 multiply_reduce_fusion
  211.1 0.3 select_reduce_fusion
  211.4 0.1 reshape.170
  211.5 54.7 %psum.7 = f32[128,8]{1,0:T(8,128)S(1)} all-reduce(f32[128,8]{1,0:T(8,128)S(1)} %reshape.170), channel_id=1, replica_groups=mesh['dp'=32,'expert'=16] {'expert'}, use_global_device_ids=true, to_apply=%region_6.7 | all-reduce | flops 1024 | bytes 8192 | tf_op jit(solution)/shard_map/psum | solution.py:124
  266.2 0.7 copy.28
  266.9 5.6 %reduce-scatter.2.cloned.1.call-done = f32[2,128,128]{2,1,0:T(8,128)} async-done(((f32[2,128,2048]{2,1,0:T(8,128)}), f32[2,128,128]{2,1,0:T(8,128)}) %reduce-scatter.2.cloned.1.call-update) | async-done | bytes 131088 | tf_op jit(solution)/shard_map/reduce_scatter | solution.py:121
  272.5 0.9 convert.4
  273.4 0.6 slice_bitcast_fusion
  (5 shorter events, 0.1 us)
Async XLA Ops:
  7.2 135.1 %copy-start = (bf16[1,192,2048]{2,1,0:T(8,128)(2,1)S(1)}, bf16[1,192,2048]{2,1,0:T(8,128)(2,1)}, u32[]{:S(2)}) copy-start(bf16[1,192,2048]{2,1,0:T(8,128)(2,1)} %param.12) | copy-start | bytes 2359300
  7.2 3.6 %copy-start.7 = (bf16[128,128]{1,0:T(8,128)(2,1)S(1)}, bf16[128,128]{1,0:T(8,128)(2,1)}, u32[]{:S(2)}) copy-start(bf16[128,128]{1,0:T(8,128)(2,1)} %param.7) | copy-start | bytes 98308
  7.2 42.2 %copy-start.8 = (bf16[128,128]{1,0:T(8,128)(2,1)S(1)}, bf16[128,128]{1,0:T(8,128)(2,1)}, u32[]{:S(2)}) copy-start(bf16[128,128]{1,0:T(8,128)(2,1)} %param.8) | copy-start | bytes 98308
  7.2 265.3 %reduce-scatter.2.cloned.1.call-start = ((), (), s32[]{:S(2)}) async-start(), calls=%async_computation.3 | async-start | bytes 2228224 | tf_op jit(solution)/shard_map/reduce_scatter | solution.py:121
  139.1 1.1 copy-start.6
  139.6 1.5 copy-start.4
  140.3 1.2 copy-start.5
  201.1 1.7 copy-start.1
  204.2 6.1 %copy-start.3 = (f32[512,2048]{1,0:T(8,128)S(1)}, f32[512,2048]{1,0:T(8,128)}, u32[]{:S(2)}) copy-start(f32[512,2048]{1,0:T(8,128)} %get-tuple-element.28) | copy-start | bytes 12582916
  208.9 1.7 copy-start.2
Sparse Core Ops, SparseCore 0:
  204.4 68.0 reduce-scatter.1

commit v4 on v3

--- a/solution.py
+++ b/solution.py
@@ -1,6 +1,8 @@
 import jax
 import jax.numpy as jnp
 from jax import lax
+from jax.experimental import pallas as pl
+from jax.experimental.pallas import tpu as pltpu
 from jax.sharding import PartitionSpec as P
 
 SHARDS = 4
@@ -44,6 +46,69 @@
         contract_first(hidden, rows_do),
     )
     return (part_out, part_grad, gradients)
+
+
+def expert_kernel(recv_ref, gate_ref, up_ref, down_ref, back_ref, gw_ref, uw_ref, dw_ref,
+                  acc_g, acc_u, acc_d):
+    step = pl.program_id(0)
+    sources, both, features = recv_ref.shape
+    capacity = both // 2
+    rows = sources * capacity
+    x = recv_ref[:, :capacity, :].reshape(rows, features)
+    do = recv_ref[:, capacity:, :].reshape(rows, features)
+    gate_w = gate_ref[...]
+    up_w = up_ref[...]
+    down_w = down_ref[...]
+    pre_gate = contract_last(x, gate_w)
+    pre_up = contract_last(x, up_w)
+    sigmoid_of = 1.0 / (1.0 + jnp.exp(-pre_gate))
+    activated = pre_gate * sigmoid_of
+    derivative = sigmoid_of * (1.0 + pre_gate * (1.0 - sigmoid_of))
+    hidden = (activated * pre_up).astype(jnp.bfloat16)
+    part_out = jnp.dot(hidden, down_w, preferred_element_type=jnp.float32)
+    d_hidden = contract_last(do, down_w)
+    d_pre_gate = (d_hidden * pre_up * derivative).astype(jnp.bfloat16)
+    d_pre_up = (d_hidden * activated).astype(jnp.bfloat16)
+    part_grad = jnp.dot(d_pre_gate, gate_w, preferred_element_type=jnp.float32) + jnp.dot(
+        d_pre_up, up_w, preferred_element_type=jnp.float32
+    )
+    back_ref[:, :capacity, :] = part_out.astype(jnp.bfloat16).reshape(sources, capacity, features)
+    back_ref[:, capacity:, :] = part_grad.astype(jnp.bfloat16).reshape(sources, capacity, features)
+
+    @pl.when(step == 0)
+    def _():
+        acc_g[...] = jnp.zeros_like(acc_g)
+        acc_u[...] = jnp.zeros_like(acc_u)
+        acc_d[...] = jnp.zeros_like(acc_d)
+
+    acc_g[...] += contract_first(d_pre_gate, x)
+    acc_u[...] += contract_first(d_pre_up, x)
+    acc_d[...] += contract_first(hidden, do)
+
+    @pl.when(step == pl.num_programs(0) - 1)
+    def _():
+        gw_ref[...] = acc_g[...].astype(jnp.bfloat16)
+        uw_ref[...] = acc_u[...].astype(jnp.bfloat16)
+        dw_ref[...] = acc_d[...].astype(jnp.bfloat16)
+
+
+def expert_call(recv, gate_w, up_w, down_w):
+    dp_count, both, features = recv.shape
+    hidden_units = gate_w.shape[0]
+    per_step = 8
+    weight_spec = pl.BlockSpec((hidden_units, features), lambda i: (0, 0))
+    rows_spec = pl.BlockSpec((per_step, both, features), lambda i: (i, 0, 0))
+    grad_shape = jax.ShapeDtypeStruct((hidden_units, features), jnp.bfloat16)
+    return pl.pallas_call(
+        expert_kernel,
+        grid=(dp_count // per_step,),
+        in_specs=[rows_spec, weight_spec, weight_spec, weight_spec],
+        out_specs=[rows_spec, weight_spec, weight_spec, weight_spec],
+        out_shape=[jax.ShapeDtypeStruct(recv.shape, jnp.bfloat16), grad_shape, grad_shape, grad_shape],
+        scratch_shapes=[pltpu.VMEM((hidden_units, features), jnp.float32)] * 3,
+        compiler_params=pltpu.CompilerParams(dimension_semantics=("arbitrary",)),
+        name="expert_mlp",
+    )(recv, gate_w, up_w, down_w)
 
 
 def per_device(tokens, cotangent, expert_ids, gate_weights, w_gate, w_up, w_down):
@@ -87,22 +152,8 @@
     recv = lax.all_to_all(
         jnp.concatenate([send_x, send_do], axis=1), "dp", split_axis=0, concat_axis=0, tiled=True
     )
-    rows_x = recv[:, :capacity].reshape(dp_count * capacity, features)
-    rows_do = recv[:, capacity:].reshape(dp_count * capacity, features)
-    part_out, part_grad, gradients = expert_rows(rows_x, rows_do, *weights)
-    back = lax.all_to_all(
-        jnp.concatenate(
-            [
-                part_out.reshape(dp_count, capacity, features),
-                part_grad.reshape(dp_count, capacity, features),
-            ],
-            axis=1,
-        ),
-        "dp",
-        split_axis=0,
-        concat_axis=0,
-        tiled=True,
-    )
+    back, grad_gate_w, grad_up_w, grad_down_w = expert_call(recv, *weights)
+    back = lax.all_to_all(back, "dp", split_axis=0, concat_axis=0, tiled=True)
     back_out = back[:, :capacity].reshape(slot_total, features)
     back_grad = back[:, capacity:].reshape(slot_total, features)
     gated_pick = token_pick.astype(jnp.float32) * slot_gate[:, None]
@@ -126,9 +177,9 @@
         summed[0].astype(jnp.bfloat16),
         summed[1].astype(jnp.bfloat16),
         grad_gates,
-        gradients[0].astype(jnp.bfloat16)[None],
-        gradients[1].astype(jnp.bfloat16)[None],
-        gradients[2].astype(jnp.bfloat16)[None],
+        grad_gate_w[None],
+        grad_up_w[None],
+        grad_down_w[None],
     )
 
 

time: 282 us -> 290 us (1.028)
  Pallas kernels: 0 us -> 15.8 us
  matrix products: 16.5 us -> 5.46 us
  waiting for transfers between devices: 5.61 us -> 9.68 us
    pallas_call x0 -> x1, Pallas kernels: none -> 15.8 us  [expert_call(): pl.pallas_call(expert_kernel, grid=(dp_count // per_step,), in_specs=[row...]
    dot_general x4 -> x1, matrix products: 6.62 us -> 0.49 us  [contract_first(): lax.dot_general(first_op, second_op, (((0,), (0,)), ((), ())), preferred_...]
    dot_general x6 -> x0, matrix products: 4.9 us -> none  [the longest x3 2.63 us: contract_last(): lax.dot_general(first_op, second_op, (((1,), (1,)), ((), ())), preferred_...]
    reduce_scatter x1, waiting for transfers between devices: 5.59 us -> 9.66 us  [per_device(): lax.psum_scatter(jnp.stack([out_part, grad_part]), 'expert', scatter_dime...]
  transfers between devices with their start and end apart: 1 -> 1, of which waited for: 1 -> 1; matrix products, arithmetic and copies ran while one was open for 3% -> 1% of each run, Pallas kernels for 0% -> 0%
where the time goes in v4:
time: 290 us; the launch traced here: 289 us
  blocking collectives  233 us (80%)
  Pallas kernels  15.8 us (5%)
  between operations  14.2 us (5%)
  waiting for transfers between devices  9.68 us (3%)
  other arithmetic  7.26 us (3%)
  matrix products  5.46 us (2%)
  local copies, waits for them, and re-layouts  3.7 us (1%)
    all_to_all x1, blocking collectives, per_device(): lax.all_to_all(jnp.concatenate([send_x, send_do], axis=1), 'dp', split_ax...  56.5 us
    psum x1, blocking collectives, per_device(): grad_gates = lax.psum(gate_part, 'expert')  54.6 us
    all_to_all x1, blocking collectives, per_device(): back = lax.all_to_all(back, 'dp', split_axis=0, concat_axis=0, tiled=True)  54.6 us
    all_gather x1, blocking collectives, per_device(): full_x = lax.all_gather(tokens, 'expert', axis=1, tiled=True)  38.6 us
    all_gather x1, blocking collectives, per_device(): full_dy = lax.all_gather(cotangent, 'expert', axis=1, tiled=True)  29.2 us
    pallas_call x1, Pallas kernels, expert_call(): pl.pallas_call(expert_kernel, grid=(dp_count // per_step,), in_specs=[row...  15.8 us
    reduce_scatter x1, waiting for transfers between devices, per_device(): lax.psum_scatter(jnp.stack([out_part, grad_part]), 'expert', scatter_dime...  9.66 us
  transfers between devices with their start and end apart: 1, of which 1 were waited for; matrix products, arithmetic and copies ran while one was open for 1% of the time, Pallas kernels for 0%

profile of v4, /device:TPU:6, one launch (start us, length us, event | category | flops | bytes accessed | tf_op | source)
XLA Modules:
  0.0 289.5 jit_solution(16982594839831191628)
XLA Ops:
  7.2 0.0 copy-start
  7.2 0.0 copy-start.1
  7.2 0.0 reduce-scatter.2.cloned.1.call-start
  7.2 0.8 copy.21
  8.0 0.1 reshape.150
  8.2 0.5 fusion.3
  8.7 0.1 convert_element_type.42
  8.8 0.1 fusion.16
  9.0 0.9 fusion.1
  9.9 0.8 copy.27
  10.7 0.1 broadcast_in_dim.51
  10.7 0.0 copy-done
  10.8 38.6 %all_gather.6 = bf16[128,2048]{1,0:T(8,128)(2,1)S(1)} all-gather(bf16[128,128]{1,0:T(8,128)(2,1)S(1)} %copy-done), channel_id=1, replica_groups=mesh['dp'=32,'expert'=16] {'expert'}, dimensions={1}, use_global_device_ids=true | all-gather | bytes 557056 | tf_op jit(solution)/shard_map/all_gather | solution.py:115
  49.3 0.0 copy-done.1
  49.3 29.2 %all_gather.7 = bf16[128,2048]{1,0:T(8,128)(2,1)S(1)} all-gather(bf16[128,128]{1,0:T(8,128)(2,1)S(1)} %copy-done.1), channel_id=1, replica_groups=mesh['dp'=32,'expert'=16] {'expert'}, dimensions={1}, use_global_device_ids=true | all-gather | bytes 557056 | tf_op jit(solution)/shard_map/all_gather | solution.py:116
  78.5 0.3 select_reduce_fusion.1
  78.8 0.7 fusion.4
  79.5 2.6 multiply_convert_fusion
  82.1 0.6 pad_maximum_fusion
  82.7 56.5 %all_to_all.10.recv_ref = bf16[32,32,2048]{2,1,0:T(8,128)(2,1)} all-to-all(bf16[32,32,2048]{2,1,0:T(8,128)(2,1)S(1)} %pad_maximum_fusion), channel_id=1, replica_groups=mesh['dp'=32,'expert'=16] {'dp'}, dimensions={0} | all-to-all | bytes 8388608 | tf_op jit(solution)/shard_map/all_to_all | solution.py:152
  139.2 15.8 %expert_mlp.1 = (bf16[32,32,2048]{2,1,0:T(8,128)(2,1)}, bf16[192,2048]{1,0:T(8,128)(2,1)}, bf16[192,2048]{1,0:T(8,128)(2,1)}, bf16[192,2048]{1,0:T(8,128)(2,1)}) custom-call(bf16[32,32,2048]{2,1,0:T(8,128)(2,1)} %all_to_all.10.recv_ref, bf16[192,2048]{1,0:T(8,128)(2,1)} %bitcast.32, bf16[192,2048]{1,0:T(8,128)(2,1)} %bitcast.33, bf16[192,2048]{1,0:T(8,128)(2,1)} %bitcast.34), custom_call_target="tpu_custom_call" | custom-call | tf_op jit(solution)/shard_map/expert_mlp/pallas_call | solution.py:102
  154.9 54.6 %all_to_all.11 = bf16[32,32,2048]{2,1,0:T(8,128)(2,1)S(1)} all-to-all(bf16[32,32,2048]{2,1,0:T(8,128)(2,1)} %get-tuple-element.10), channel_id=1, replica_groups=mesh['dp'=32,'expert'=16] {'dp'}, dimensions={0} | all-to-all | bytes 8388608 | tf_op jit(solution)/shard_map/all_to_all | solution.py:156
  209.5 0.4 fusion.24
  209.9 0.5 convolution_bitcast_fusion.1
  210.4 1.1 convolution_bitcast_fusion
  211.6 1.5 pad_maximum_fusion.1
  213.1 0.0 reduce-scatter.2.cloned.1.call-update
  213.1 2.7 multiply_reduce_fusion
  215.8 0.3 select_reduce_fusion
  216.1 0.1 reshape.154
  216.2 54.6 %psum.7 = f32[128,8]{1,0:T(8,128)S(1)} all-reduce(f32[128,8]{1,0:T(8,128)S(1)} %reshape.154), channel_id=1, replica_groups=mesh['dp'=32,'expert'=16] {'expert'}, use_global_device_ids=true, to_apply=%region_6.7 | all-reduce | flops 1024 | bytes 8192 | tf_op jit(solution)/shard_map/psum | solution.py:175
  270.8 0.7 copy.28
  271.4 9.7 %reduce-scatter.2.cloned.1.call-done = f32[2,128,128]{2,1,0:T(8,128)} async-done(((f32[2,128,2048]{2,1,0:T(8,128)}), f32[2,128,128]{2,1,0:T(8,128)}) %reduce-scatter.2.cloned.1.call-update) | async-done | bytes 131088 | tf_op jit(solution)/shard_map/reduce_scatter | solution.py:172
  281.1 0.9 convert.4
  282.0 0.6 slice_bitcast_fusion
  (5 shorter events, 0.1 us)
Async XLA Ops:
  7.2 3.6 %copy-start = (bf16[128,128]{1,0:T(8,128)(2,1)S(1)}, bf16[128,128]{1,0:T(8,128)(2,1)}, u32[]{:S(2)}) copy-start(bf16[128,128]{1,0:T(8,128)(2,1)} %param.7) | copy-start | bytes 98308
  7.2 42.1 %copy-start.1 = (bf16[128,128]{1,0:T(8,128)(2,1)S(1)}, bf16[128,128]{1,0:T(8,128)(2,1)}, u32[]{:S(2)}) copy-start(bf16[128,128]{1,0:T(8,128)(2,1)} %param.8) | copy-start | bytes 98308
  7.2 273.9 %reduce-scatter.2.cloned.1.call-start = ((), (), s32[]{:S(2)}) async-start(), calls=%async_computation.3 | async-start | bytes 2228224 | tf_op jit(solution)/shard_map/reduce_scatter | solution.py:172
Sparse Core Ops, SparseCore 0:
  213.2 67.8 reduce-scatter.1

commit v5 on v3

--- a/solution.py
+++ b/solution.py
@@ -84,11 +84,10 @@
         (slot_gate[:, None] * slot_dy).astype(jnp.bfloat16).reshape(dp_count, capacity, features)
     )
     weights = (w_gate[0], w_up[0], w_down[0])
-    recv = lax.all_to_all(
-        jnp.concatenate([send_x, send_do], axis=1), "dp", split_axis=0, concat_axis=0, tiled=True
-    )
-    rows_x = recv[:, :capacity].reshape(dp_count * capacity, features)
-    rows_do = recv[:, capacity:].reshape(dp_count * capacity, features)
+    recv_x = lax.all_to_all(send_x, "dp", split_axis=0, concat_axis=0, tiled=True)
+    recv_do = lax.all_to_all(send_do, "dp", split_axis=0, concat_axis=0, tiled=True)
+    rows_x = recv_x.reshape(slot_total, features)
+    rows_do = recv_do.reshape(slot_total, features)
     part_out, part_grad, gradients = expert_rows(rows_x, rows_do, *weights)
     back = lax.all_to_all(
         jnp.concatenate(

time: 282 us -> 268 us (0.950)
  blocking collectives: 233 us -> 177 us
  waiting for transfers between devices: 5.61 us -> 29.3 us
  starting transfers between devices: 0.04 us -> 15.2 us
  matrix products: 16.5 us -> 22.2 us
    all_to_all x1 -> x0, blocking collectives: 56.4 us -> none  [per_device(): lax.all_to_all(jnp.concatenate([send_x, send_do], axis=1), 'dp', split_ax...]
    all_to_all x0 -> x2, waiting for transfers between devices: none -> 23.6 us  [the longest x1 23.6 us: per_device(): lax.all_to_all(send_do, 'dp', split_axis=0, concat_axis=0, tiled=True)]
    all_to_all x0 -> x2, starting transfers between devices: none -> 15.2 us  [the longest x1 7.75 us: per_device(): lax.all_to_all(send_x, 'dp', split_axis=0, concat_axis=0, tiled=True)]
    dot_general x3, matrix products: 2.63 us -> 6.32 us  [contract_last(): lax.dot_general(first_op, second_op, (((1,), (1,)), ((), ())), preferred_...]
  transfers between devices with their start and end apart: 1 -> 3, of which waited for: 1 -> 2; matrix products, arithmetic and copies ran while one was open for 3% -> 5% of each run, Pallas kernels for 0% -> 0%
where the time goes in v5:
time: 268 us; the launch traced here: 267 us
  blocking collectives  177 us (66%)
  waiting for transfers between devices  29.3 us (11%)
  matrix products  22.2 us (8%)
  starting transfers between devices  15.2 us (6%)
  between operations  14.3 us (5%)
  other arithmetic  5.11 us (2%)
  local copies, waits for them, and re-layouts  3.87 us (1%)
    psum x1, blocking collectives, per_device(): grad_gates = lax.psum(gate_part, 'expert')  54.8 us
    all_to_all x1, blocking collectives, per_device(): lax.all_to_all(jnp.concatenate([part_out.reshape(dp_count, capacity, feat...  54.6 us
    all_gather x1, blocking collectives, per_device(): full_x = lax.all_gather(tokens, 'expert', axis=1, tiled=True)  38.8 us
    all_gather x1, blocking collectives, per_device(): full_dy = lax.all_gather(cotangent, 'expert', axis=1, tiled=True)  28.7 us
    all_to_all x1, waiting for transfers between devices, per_device(): lax.all_to_all(send_do, 'dp', split_axis=0, concat_axis=0, tiled=True)  23.6 us
    all_to_all x1, starting transfers between devices, per_device(): lax.all_to_all(send_x, 'dp', split_axis=0, concat_axis=0, tiled=True)  7.75 us
    all_to_all x1, starting transfers between devices, per_device(): lax.all_to_all(send_do, 'dp', split_axis=0, concat_axis=0, tiled=True)  7.44 us
    dot_general x4, matrix products, contract_first(): lax.dot_general(first_op, second_op, (((0,), (0,)), ((), ())), preferred_...  6.62 us
  transfers between devices with their start and end apart: 3, of which 2 were waited for; matrix products, arithmetic and copies ran while one was open for 5% of the time, Pallas kernels for 0%

profile of v5, /device:TPU:6, one launch (start us, length us, event | category | flops | bytes accessed | tf_op | source)
XLA Modules:
  0.0 266.9 jit_solution(1651257012682768110)
XLA Ops:
  7.2 0.0 copy-start
  7.2 0.9 copy.21
  8.0 0.1 reshape.162
  8.2 0.5 fusion.6
  8.7 0.1 convert_element_type.66
  8.8 0.1 fusion.30
  9.0 0.9 fusion.4
  9.9 38.8 %all_gather.6 = bf16[128,2048]{1,0:T(8,128)(2,1)S(1)} all-gather(bf16[128,128]{1,0:T(8,128)(2,1)} %param.7), channel_id=1, replica_groups=mesh['dp'=32,'expert'=16] {'expert'}, dimensions={1}, use_global_device_ids=true | all-gather | bytes 557056 | tf_op jit(solution)/shard_map/all_gather | solution.py:50
  48.7 2.0 fusion.17
  50.7 0.0 copy-start.7
  50.7 0.0 copy-start.6
  50.7 7.7 %all-to-all-start = ((bf16[32,16,2048]{2,1,0:T(8,128)(2,1)}), bf16[32,16,2048]{2,1,0:T(8,128)(2,1)S(1)}, u32[]{:S(2)}, u32[]{:S(2)}) async-start(bf16[32,16,2048]{2,1,0:T(8,128)(2,1)} %fusion.17), calls=%async_computation | async-start | bytes 4194304 | tf_op jit(solution)/shard_map/all_to_all | solution.py:87
  58.5 0.0 copy-done.7
  58.5 0.1 copy.27
  58.6 0.1 broadcast_in_dim.51
  58.7 0.3 select_reduce_fusion.1
  59.0 0.0 copy-done.6
  59.0 28.7 %all_gather.7 = bf16[128,2048]{1,0:T(8,128)(2,1)S(1)} all-gather(bf16[128,128]{1,0:T(8,128)(2,1)S(1)} %copy-done.6), channel_id=1, replica_groups=mesh['dp'=32,'expert'=16] {'expert'}, dimensions={1}, use_global_device_ids=true | all-gather | bytes 557056 | tf_op jit(solution)/shard_map/all_gather | solution.py:51
  87.7 3.3 %multiply_convert_fusion = (bf16[512,2048]{1,0:T(8,128)(2,1)}, f32[512,2048]{1,0:T(8,128)}) fusion(f32[512]{0:T(512)S(1)} %select_reduce_fusion.1, pred[512,128]{1,0:T(8,128)(4,1)S(1)} %fusion.4, bf16[128,2048]{1,0:T(8,128)(2,1)S(1)} %all_gather.7), kind=kOutput, calls=%fused_computation.3 | convolution fusion | flops 270532608 | bytes 6883328 | tf_op jit(solution)/shard_map/dot_general | solution.py:82
  91.0 0.0 all-to-all-done
  91.0 7.4 %all-to-all-start.1 = ((bf16[32,16,2048]{2,1,0:T(8,128)(2,1)}), bf16[32,16,2048]{2,1,0:T(8,128)(2,1)}, u32[]{:S(2)}, u32[]{:S(2)}) async-start(bf16[32,16,2048]{2,1,0:T(8,128)(2,1)} %bitcast.66), calls=%async_computation.1 | async-start | bytes 4194304 | tf_op jit(solution)/shard_map/all_to_all | solution.py:88
  98.4 0.0 reduce-scatter.2.cloned.1.call-start
  98.5 2.7 %fusion.15 = f32[512,192]{0,1:T(8,128)} fusion(bf16[512,2048]{1,0:T(8,128)(2,1)S(1)} %bitcast.61, bf16[1,192,2048]{2,1,0:T(8,128)(2,1)} %param.11), kind=kOutput, calls=%fused_computation.31 | convolution fusion | flops 402653184 | bytes 3276800 | tf_op jit(solution)/shard_map/dot_general | solution.py:17
  101.2 23.6 %all-to-all-done.1 = bf16[32,16,2048]{2,1,0:T(8,128)(2,1)} async-done(((bf16[32,16,2048]{2,1,0:T(8,128)(2,1)}), bf16[32,16,2048]{2,1,0:T(8,128)(2,1)}, u32[]{:S(2)}, u32[]{:S(2)}) %all-to-all-start.1) | async-done | bytes 2097184 | tf_op jit(solution)/shard_map/all_to_all | solution.py:88
  124.8 0.0 copy-start.8
  124.8 2.7 fusion.7
  127.5 0.0 copy-done
  127.5 0.0 copy-done.8
  127.5 0.0 copy-start.5
  127.5 0.9 multiply_convert_fusion.3
  128.5 0.0 copy-start.4
  128.5 0.2 copy-done.5
  128.6 0.7 convolution_convert_fusion
  129.4 0.3 copy-done.4
  129.6 0.7 fusion.13
  130.4 0.8 add_convert_fusion
  131.2 0.6 pad_maximum_fusion
  131.7 54.6 %all_to_all.15 = bf16[32,32,2048]{2,1,0:T(8,128)(2,1)S(1)} all-to-all(bf16[32,32,2048]{2,1,0:T(8,128)(2,1)S(1)} %pad_maximum_fusion), channel_id=1, replica_groups=mesh['dp'=32,'expert'=16] {'dp'}, dimensions={0} | all-to-all | bytes 8388608 | tf_op jit(solution)/shard_map/all_to_all | solution.py:92
  186.3 0.6 fusion.38
  186.9 0.0 copy-start.1
  186.9 0.5 convolution_bitcast_fusion.1
  187.4 1.1 convolution_bitcast_fusion
  188.6 0.0 copy-done.1
  188.6 1.5 pad_maximum_fusion.1
  190.1 0.0 reduce-scatter.2.cloned.1.call-update
  190.1 0.0 copy-start.3
  190.1 3.2 %fusion.3 = bf16[1,192,2048]{2,1,0:T(8,128)(2,1)} fusion(bf16[512,192]{0,1:T(8,128)(2,1)S(1)} %get-tuple-element.20, bf16[512,2048]{1,0:T(8,128)(2,1)} %bitcast.8), kind=kOutput, calls=%fused_computation.14 | convolution fusion | flops 403046400 | bytes 3080192 | tf_op jit(solution)/shard_map/dot_general | solution.py:23
  193.3 1.5 fusion.1
  194.8 0.0 copy-start.2
  194.8 1.5 fusion.2
  196.2 0.0 copy-done.3
  196.2 0.2 copy-done.2
  196.4 0.5 multiply_reduce_fusion
  196.9 0.3 select_reduce_fusion
  197.3 0.1 reshape.170
  197.4 54.8 %psum.7 = f32[128,8]{1,0:T(8,128)S(1)} all-reduce(f32[128,8]{1,0:T(8,128)S(1)} %reshape.170), channel_id=1, replica_groups=mesh['dp'=32,'expert'=16] {'expert'}, use_global_device_ids=true, to_apply=%region_6.7 | all-reduce | flops 1024 | bytes 8192 | tf_op jit(solution)/shard_map/psum | solution.py:123
  252.2 0.7 copy.28
  252.8 5.7 %reduce-scatter.2.cloned.1.call-done = f32[2,128,128]{2,1,0:T(8,128)} async-done(((f32[2,128,2048]{2,1,0:T(8,128)}), f32[2,128,128]{2,1,0:T(8,128)}) %reduce-scatter.2.cloned.1.call-update) | async-done | bytes 131088 | tf_op jit(solution)/shard_map/reduce_scatter | solution.py:120
  258.5 0.9 convert.4
  259.4 0.6 slice_bitcast_fusion
  (5 shorter events, 0.1 us)
Async XLA Ops:
  7.2 120.3 %copy-start = (bf16[1,192,2048]{2,1,0:T(8,128)(2,1)S(1)}, bf16[1,192,2048]{2,1,0:T(8,128)(2,1)}, u32[]{:S(2)}) copy-start(bf16[1,192,2048]{2,1,0:T(8,128)(2,1)} %param.12) | copy-start | bytes 2359300
  50.7 7.8 %copy-start.7 = (f32[128,8]{0,1:T(8,128)S(1)}, f32[128,8]{0,1:T(8,128)}, u32[]{:S(2)}) copy-start(f32[128,8]{0,1:T(8,128)} %param.10) | copy-start | bytes 12292
  50.7 8.3 %copy-start.6 = (bf16[128,128]{1,0:T(8,128)(2,1)S(1)}, bf16[128,128]{1,0:T(8,128)(2,1)}, u32[]{:S(2)}) copy-start(bf16[128,128]{1,0:T(8,128)(2,1)} %param.8) | copy-start | bytes 98308
  50.7 40.3 %all-to-all-start = ((bf16[32,16,2048]{2,1,0:T(8,128)(2,1)}), bf16[32,16,2048]{2,1,0:T(8,128)(2,1)S(1)}, u32[]{:S(2)}, u32[]{:S(2)}) async-start(bf16[32,16,2048]{2,1,0:T(8,128)(2,1)} %fusion.17), calls=%async_computation | async-start | bytes 4194304 | tf_op jit(solution)/shard_map/all_to_all | solution.py:87
  91.0 33.8 %all-to-all-start.1 = ((bf16[32,16,2048]{2,1,0:T(8,128)(2,1)}), bf16[32,16,2048]{2,1,0:T(8,128)(2,1)}, u32[]{:S(2)}, u32[]{:S(2)}) async-start(bf16[32,16,2048]{2,1,0:T(8,128)(2,1)} %bitcast.66), calls=%async_computation.1 | async-start | bytes 4194304 | tf_op jit(solution)/shard_map/all_to_all | solution.py:88
  98.4 160.1 %reduce-scatter.2.cloned.1.call-start = ((), (), s32[]{:S(2)}) async-start(), calls=%async_computation.4 | async-start | bytes 2228224 | tf_op jit(solution)/shard_map/reduce_scatter | solution.py:120
  124.8 2.7 %copy-start.8 = (f32[512,192]{0,1:T(8,128)S(1)}, f32[512,192]{0,1:T(8,128)}, u32[]{:S(2)}) copy-start(f32[512,192]{0,1:T(8,128)} %fusion.15) | copy-start | bytes 1179652
  127.5 1.1 copy-start.5
  128.5 1.2 copy-start.4
  186.9 1.7 copy-start.1
  190.1 6.2 %copy-start.3 = (f32[512,2048]{1,0:T(8,128)S(1)}, f32[512,2048]{1,0:T(8,128)}, u32[]{:S(2)}) copy-start(f32[512,2048]{1,0:T(8,128)} %get-tuple-element.26) | copy-start | bytes 12582916
  194.8 1.7 copy-start.2
Sparse Core Ops, SparseCore 0:
  190.2 68.2 reduce-scatter.1

commit v6 on v5

--- a/solution.py
+++ b/solution.py
@@ -117,10 +117,28 @@
     gate_part = jnp.sum(jnp.where(picks, gate_terms[:, None], 0.0), axis=0).reshape(
         tok_count, chosen
     )
-    summed = lax.psum_scatter(
-        jnp.stack([out_part, grad_part]), "expert", scatter_dimension=2, tiled=True
+    rounded = []
+    rest = gate_part
+    for _ in range(3):
+        piece = lax.reduce_precision(rest, exponent_bits=8, mantissa_bits=7)
+        rounded.append(piece)
+        rest = rest - piece
+    width = features // column_count
+    parts = jnp.stack([out_part, grad_part]).astype(jnp.bfloat16)
+    parts = parts.reshape(2, tok_count, column_count, width).transpose(2, 0, 1, 3)
+    parts = parts.reshape(column_count, 2 * tok_count * width)
+    gate_flat = jnp.stack(rounded).astype(jnp.bfloat16).reshape(1, 3 * tok_count * chosen)
+    payload = jnp.concatenate(
+        [parts, jnp.broadcast_to(gate_flat, (column_count, 3 * tok_count * chosen))], axis=1
     )
-    grad_gates = lax.psum(gate_part, "expert")
+    arrived = lax.all_to_all(payload, "expert", split_axis=0, concat_axis=0, tiled=True)
+    arrived = arrived.astype(jnp.float32)
+    total = arrived[0]
+    for source in range(1, column_count):
+        total = total + arrived[source]
+    summed = total[: 2 * tok_count * width].reshape(2, tok_count, width)
+    gate_sums = total[2 * tok_count * width :].reshape(3, tok_count, chosen)
+    grad_gates = (gate_sums[0] + gate_sums[1]) + gate_sums[2]
     return (
         summed[0].astype(jnp.bfloat16),
         summed[1].astype(jnp.bfloat16),

time: 268 us -> 283 us (1.056)
  blocking collectives: 177 us -> 122 us
  waiting for transfers between devices: 29.3 us -> 71.5 us
  local copies, waits for them, and re-layouts: 3.87 us -> 24.3 us
  between operations: 14.3 us -> 1.05 us
  starting transfers between devices: 15.2 us -> 23 us
  other arithmetic: 5.11 us -> 12.2 us
  matrix products: 22.2 us -> 26.8 us
    psum x1 -> x0, blocking collectives: 54.8 us -> none  [per_device(): grad_gates = lax.psum(gate_part, 'expert')]
    all_to_all x0 -> x1, waiting for transfers between devices: none -> 47.9 us  [per_device(): lax.all_to_all(payload, 'expert', split_axis=0, concat_axis=0, tiled=True)]
    unnamed x21 -> x34, local copies, waits for them, and re-layouts: 2.28 us -> 12.2 us
    all_to_all x0 -> x1, starting transfers between devices: none -> 7.81 us  [per_device(): lax.all_to_all(payload, 'expert', split_axis=0, concat_axis=0, tiled=True)]
    all_to_all x0 -> x2, other arithmetic: none -> 5.9 us  [per_device(): lax.all_to_all(payload, 'expert', split_axis=0, concat_axis=0, tiled=True)]
    reduce_scatter x1 -> x0, waiting for transfers between devices: 5.71 us -> none  [per_device(): lax.psum_scatter(jnp.stack([out_part, grad_part]), 'expert', scatter_dime...]
    dot_general x0 -> x1, local copies, waits for them, and re-layouts: none -> 3.94 us  [per_device(): lax.dot_general(gated_pick, back_out.astype(jnp.float32), (((0,), (0,)),...]
    reshape x0 -> x1, local copies, waits for them, and re-layouts: none -> 3.94 us  [per_device(): back_grad = back[:, capacity:].reshape(slot_total, features)]
  transfers between devices with their start and end apart: 3 -> 3, of which waited for: 2 -> 2; matrix products, arithmetic and copies ran while one was open for 5% -> 4% of each run, Pallas kernels for 0% -> 0%
where the time goes in v6:
time: 283 us; the launch traced here: 281 us
  blocking collectives  122 us (43%)
  waiting for transfers between devices  71.5 us (25%)
  matrix products  26.8 us (9%)
  local copies, waits for them, and re-layouts  24.3 us (9%)
  starting transfers between devices  23 us (8%)
  other arithmetic  12.2 us (4%)
    all_to_all x1, blocking collectives, per_device(): lax.all_to_all(jnp.concatenate([part_out.reshape(dp_count, capacity, feat...  54.6 us
    all_to_all x1, waiting for transfers between devices, per_device(): lax.all_to_all(payload, 'expert', split_axis=0, concat_axis=0, tiled=True)  47.9 us
    all_gather x1, blocking collectives, per_device(): full_x = lax.all_gather(tokens, 'expert', axis=1, tiled=True)  38.8 us
    all_gather x1, blocking collectives, per_device(): full_dy = lax.all_gather(cotangent, 'expert', axis=1, tiled=True)  28.7 us
    all_to_all x1, waiting for transfers between devices, per_device(): lax.all_to_all(send_do, 'dp', split_axis=0, concat_axis=0, tiled=True)  23.6 us
    unnamed x34, local copies, waits for them, and re-layouts  12.2 us
    dot_general x4, matrix products, contract_first(): lax.dot_general(first_op, second_op, (((0,), (0,)), ((), ())), preferred_...  8.48 us
    all_to_all x1, starting transfers between devices, per_device(): lax.all_to_all(payload, 'expert', split_axis=0, concat_axis=0, tiled=True)  7.81 us
  transfers between devices with their start and end apart: 3, of which 2 were waited for; matrix products, arithmetic and copies ran while one was open for 4% of the time, Pallas kernels for 0%

profile of v6, /device:TPU:6, one launch (start us, length us, event | category | flops | bytes accessed | tf_op | source)
XLA Modules:
  0.0 281.0 jit_solution(6107861342509546391)
XLA Ops:
  0.6 0.0 copy-start
  0.7 0.9 copy.60
  1.5 0.1 reshape.400
  1.7 0.5 fusion.8
  2.2 0.1 convert_element_type.74
  2.3 0.1 fusion.33
  2.4 0.9 fusion.4
  3.3 38.8 %all_gather.6 = bf16[128,2048]{1,0:T(8,128)(2,1)S(1)} all-gather(bf16[128,128]{1,0:T(8,128)(2,1)} %param.7), channel_id=1, replica_groups=mesh['dp'=32,'expert'=16] {'expert'}, dimensions={1}, use_global_device_ids=true | all-gather | bytes 557056 | tf_op jit(solution)/shard_map/all_gather | solution.py:50
  42.1 2.0 fusion.19
  44.2 7.7 %all-to-all-start = ((bf16[32,16,2048]{2,1,0:T(8,128)(2,1)}), bf16[32,16,2048]{2,1,0:T(8,128)(2,1)S(1)}, u32[]{:S(2)}, u32[]{:S(2)}) async-start(bf16[32,16,2048]{2,1,0:T(8,128)(2,1)} %fusion.19), calls=%async_computation | async-start | bytes 4194304 | tf_op jit(solution)/shard_map/all_to_all | solution.py:87
  51.9 0.1 copy.66
  52.0 0.1 broadcast_in_dim.56
  52.1 0.3 select_reduce_fusion.1
  52.4 28.7 %all_gather.7 = bf16[128,2048]{1,0:T(8,128)(2,1)S(1)} all-gather(bf16[128,128]{1,0:T(8,128)(2,1)S(1)} %copy-done.11), channel_id=1, replica_groups=mesh['dp'=32,'expert'=16] {'expert'}, dimensions={1}, use_global_device_ids=true | all-gather | bytes 557056 | tf_op jit(solution)/shard_map/all_gather | solution.py:51
  81.2 3.3 %multiply_convert_fusion = (bf16[512,2048]{1,0:T(8,128)(2,1)}, f32[512,2048]{1,0:T(8,128)}) fusion(f32[512]{0:T(512)S(1)} %select_reduce_fusion.1, pred[512,128]{1,0:T(8,128)(4,1)S(1)} %fusion.4, bf16[128,2048]{1,0:T(8,128)(2,1)S(1)} %all_gather.7), kind=kOutput, calls=%fused_computation.3 | convolution fusion | flops 270532608 | bytes 6883328 | tf_op jit(solution)/shard_map/dot_general | solution.py:82
  84.5 0.0 all-to-all-done
  84.5 7.4 %all-to-all-start.1 = ((bf16[32,16,2048]{2,1,0:T(8,128)(2,1)}), bf16[32,16,2048]{2,1,0:T(8,128)(2,1)}, u32[]{:S(2)}, u32[]{:S(2)}) async-start(bf16[32,16,2048]{2,1,0:T(8,128)(2,1)} %bitcast.86), calls=%async_computation.1 | async-start | bytes 4194304 | tf_op jit(solution)/shard_map/all_to_all | solution.py:88
  91.9 2.7 fusion.17
  94.6 23.6 %all-to-all-done.1 = bf16[32,16,2048]{2,1,0:T(8,128)(2,1)} async-done(((bf16[32,16,2048]{2,1,0:T(8,128)(2,1)}), bf16[32,16,2048]{2,1,0:T(8,128)(2,1)}, u32[]{:S(2)}, u32[]{:S(2)}) %all-to-all-start.1) | async-done | bytes 2097184 | tf_op jit(solution)/shard_map/all_to_all | solution.py:88
  118.3 2.7 fusion.9
  121.0 0.0 copy-start.8
  121.0 0.9 multiply_convert_fusion.3
  121.9 0.0 copy-start.3
  121.9 0.0 copy-start.6
  122.0 0.0 copy-start.5
  122.0 0.1 copy-done.8
  122.1 0.7 convolution_convert_fusion
  122.9 0.5 copy-done.5
  123.3 0.7 fusion.15
  124.1 0.8 add_convert_fusion
  124.9 0.8 pad_maximum_fusion
  125.7 54.6 %all_to_all.24 = bf16[32,32,2048]{2,1,0:T(8,128)(2,1)S(1)} all-to-all(bf16[32,32,2048]{2,1,0:T(8,128)(2,1)S(1)} %pad_maximum_fusion), channel_id=1, replica_groups=mesh['dp'=32,'expert'=16] {'dp'}, dimensions={0} | all-to-all | bytes 8388608 | tf_op jit(solution)/shard_map/all_to_all | solution.py:92
  180.2 1.9 fusion.44
  182.2 1.1 copy-done.2
  183.3 0.6 multiply_reduce_fusion
  183.9 0.3 select_reduce_fusion
  184.3 3.9 %copy.69 = bf16[512,2048]{0,1:T(8,128)(2,1)} copy(bf16[512,2048]{1,0:T(8,128)(2,1)} %bitcast.90) | data formatting | bytes 4194304 | tf_op jit(solution)/shard_map/reshape | solution.py:106
  188.2 2.5 fusion.5
  190.7 3.9 %copy.80 = bf16[2048,512]{1,0:T(8,128)(2,1)} copy(bf16[2048,512]{0,1:T(8,128)(2,1)} %bitcast.85) | data formatting | bytes 4194304 | tf_op jit(solution)/shard_map/dot_general | solution.py:108
  194.6 3.9 %fusion.6 = bf16[1,128,16,128]{3,1,2,0:T(8,128)(2,1)S(1)} fusion(bf16[16,128,512]{2,1,0:T(8,128)(2,1)} %bitcast.87, f32[512]{0:T(512)S(1)} %select_reduce_fusion.1, pred[512,128]{1,0:T(8,128)(4,1)S(1)} %fusion.4), kind=kOutput, calls=%fused_computation.21 | convolution fusion | flops 1611071488 | bytes 2689024 | tf_op jit(solution)/shard_map/dot_general | solution.py:108
  198.5 0.1 maximum_bitcast_fusion.1
  198.6 0.1 copy.71
  198.8 1.7 copy.84
  200.5 0.1 reshape.409
  200.6 0.2 copy.74
  200.8 0.1 reshape.456
  201.0 2.4 maximum_bitcast_fusion
  203.4 0.5 broadcast.171
  203.9 3.5 %reduce.12 = bf16[16,35840]{1,0:T(8,128)(2,1)} reduce(bf16[16,1,35840]{2,0,1:T(8,128)(2,1)} %maximum_bitcast_fusion, bf16[]{:T(256)} %broadcast.171), dimensions={1}, to_apply=%copy.75.reduce_sub_computation | reduce | bytes 2293762 | tf_op jit(solution)/shard_map/all_to_all | solution.py:134
  207.4 2.8 reshape.458
  210.2 7.8 %all-to-all-start.3 = ((bf16[16,2,17920]{2,1,0:T(2,128)(2,1)}), bf16[16,2,17920]{2,1,0:T(2,128)(2,1)}, u32[]{:S(2)}, u32[]{:S(2)}) async-start(bf16[16,2,17920]{2,1,0:T(2,128)(2,1)} %reshape.458), calls=%async_computation.3 | async-start | bytes 2293760 | tf_op jit(solution)/shard_map/all_to_all | solution.py:134
  218.0 0.0 copy-start.4
  218.0 3.1 %fusion.3 = bf16[1,192,2048]{2,1,0:T(8,128)(2,1)} fusion(bf16[512,192]{0,1:T(8,128)(2,1)S(1)} %copy-done.7, bf16[512,2048]{1,0:T(8,128)(2,1)} %bitcast.9), kind=kOutput, calls=%fused_computation.12 | convolution fusion | flops 403046400 | bytes 3080192 | tf_op jit(solution)/shard_map/dot_general | solution.py:23
  221.1 1.5 fusion.1
  222.6 1.5 fusion.2
  224.0 47.9 %all-to-all-done.3 = bf16[16,2,17920]{2,1,0:T(2,128)(2,1)} async-done(((bf16[16,2,17920]{2,1,0:T(2,128)(2,1)}), bf16[16,2,17920]{2,1,0:T(2,128)(2,1)}, u32[]{:S(2)}, u32[]{:S(2)}) %all-to-all-start.3) | async-done | bytes 1146912 | tf_op jit(solution)/shard_map/all_to_all | solution.py:134
  271.9 4.3 %reshape.459 = bf16[16,1,35840]{2,1,0:T(2,128)(2,1)S(1)} reshape(bf16[16,2,17920]{2,1,0:T(2,128)(2,1)} %all-to-all-done.3) | data formatting | bytes 2293760
  276.2 2.4 convert_element_type.85
  278.5 0.8 slice_add_fusion
  279.4 0.1 reshape.435
  279.5 0.1 reshape.434
  279.6 0.1 reshape.436
  279.7 0.7 copy.76
  280.4 0.6 fusion.45
  (31 shorter events, 0.3 us)
Async XLA Ops:
  0.6 120.3 %copy-start = (bf16[1,192,2048]{2,1,0:T(8,128)(2,1)S(1)}, bf16[1,192,2048]{2,1,0:T(8,128)(2,1)}, u32[]{:S(2)}) copy-start(bf16[1,192,2048]{2,1,0:T(8,128)(2,1)} %param.12) | copy-start | bytes 2359300
  44.2 7.8 %copy-start.12 = (f32[128,8]{0,1:T(8,128)S(1)}, f32[128,8]{0,1:T(8,128)}, u32[]{:S(2)}) copy-start(f32[128,8]{0,1:T(8,128)} %param.10) | copy-start | bytes 12292
  44.2 8.3 %copy-start.11 = (bf16[128,128]{1,0:T(8,128)(2,1)S(1)}, bf16[128,128]{1,0:T(8,128)(2,1)}, u32[]{:S(2)}) copy-start(bf16[128,128]{1,0:T(8,128)(2,1)} %param.8) | copy-start | bytes 98308
  44.2 40.3 %all-to-all-start = ((bf16[32,16,2048]{2,1,0:T(8,128)(2,1)}), bf16[32,16,2048]{2,1,0:T(8,128)(2,1)S(1)}, u32[]{:S(2)}, u32[]{:S(2)}) async-start(bf16[32,16,2048]{2,1,0:T(8,128)(2,1)} %fusion.19), calls=%async_computation | async-start | bytes 4194304 | tf_op jit(solution)/shard_map/all_to_all | solution.py:87
  84.5 33.8 %all-to-all-start.1 = ((bf16[32,16,2048]{2,1,0:T(8,128)(2,1)}), bf16[32,16,2048]{2,1,0:T(8,128)(2,1)}, u32[]{:S(2)}, u32[]{:S(2)}) async-start(bf16[32,16,2048]{2,1,0:T(8,128)(2,1)} %bitcast.86), calls=%async_computation.1 | async-start | bytes 4194304 | tf_op jit(solution)/shard_map/all_to_all | solution.py:88
  118.3 2.7 copy-start.13
  121.0 1.1 copy-start.8
  121.9 2.2 copy-start.3
  121.9 2.2 copy-start.6
  122.0 2.2 copy-start.9
  122.0 1.4 copy-start.5
  180.2 3.1 %copy-start.2 = (f32[512,2048]{1,0:T(8,128)S(1)}, f32[512,2048]{1,0:T(8,128)}, u32[]{:S(2)}) copy-start(f32[512,2048]{1,0:T(8,128)} %get-tuple-element.44) | copy-start | bytes 12582916
  182.2 1.7 copy-start.1
  207.4 10.6 %copy-start.7 = (bf16[512,192]{0,1:T(8,128)(2,1)S(1)}, bf16[512,192]{0,1:T(8,128)(2,1)}, u32[]{:S(2)}) copy-start(bf16[512,192]{0,1:T(8,128)(2,1)} %copy-done.6) | copy-start | bytes 589828
  210.2 61.7 %all-to-all-start.3 = ((bf16[16,2,17920]{2,1,0:T(2,128)(2,1)}), bf16[16,2,17920]{2,1,0:T(2,128)(2,1)}, u32[]{:S(2)}, u32[]{:S(2)}) async-start(bf16[16,2,17920]{2,1,0:T(2,128)(2,1)} %reshape.458), calls=%async_computation.3 | async-start | bytes 2293760 | tf_op jit(solution)/shard_map/all_to_all | solution.py:134
  218.0 3.1 %copy-start.4 = (bf16[512,192]{0,1:T(8,128)(2,1)S(1)}, bf16[512,192]{0,1:T(8,128)(2,1)}, u32[]{:S(2)}) copy-start(bf16[512,192]{0,1:T(8,128)(2,1)} %copy-done.3) | copy-start | bytes 589828
  221.1 1.5 copy-start.10

commit v7 on v5

--- a/solution.py
+++ b/solution.py
@@ -1,6 +1,8 @@
 import jax
 import jax.numpy as jnp
 from jax import lax
+from jax.experimental import pallas as pl
+from jax.experimental.pallas import tpu as pltpu
 from jax.sharding import PartitionSpec as P
 
 SHARDS = 4
@@ -46,6 +48,30 @@
     return (part_out, part_grad, gradients)
 
 
+def pick_kernel(pick_ref, scale_ref, rows_ref, out_ref):
+    picked = jnp.dot(pick_ref[...], rows_ref[...], preferred_element_type=jnp.float32)
+    out_ref[...] = (scale_ref[...] * picked).astype(out_ref.dtype)
+
+
+def pick_rows(pick, scale, rows):
+    slots, tokens = pick.shape
+    features = rows.shape[1]
+    block = 128
+    return pl.pallas_call(
+        pick_kernel,
+        grid=(slots // block,),
+        in_specs=[
+            pl.BlockSpec((block, tokens), lambda i: (i, 0)),
+            pl.BlockSpec((block, 1), lambda i: (i, 0)),
+            pl.BlockSpec((tokens, features), lambda i: (0, 0)),
+        ],
+        out_specs=pl.BlockSpec((block, features), lambda i: (i, 0)),
+        out_shape=jax.ShapeDtypeStruct((slots, features), jnp.bfloat16),
+        compiler_params=pltpu.CompilerParams(dimension_semantics=("arbitrary",)),
+        name="pick_rows",
+    )(pick, scale, rows)
+
+
 def per_device(tokens, cotangent, expert_ids, gate_weights, w_gate, w_up, w_down):
     full_x = lax.all_gather(tokens, "expert", axis=1, tiled=True)
     full_dy = lax.all_gather(cotangent, "expert", axis=1, tiled=True)
@@ -76,12 +102,11 @@
     slot_gate = jnp.sum(jnp.where(picks, flat_gates[None, :], 0.0), axis=1)
     token_of = jnp.any(picks.reshape(slot_total, tok_count, chosen), axis=2)
     token_pick = token_of.astype(jnp.bfloat16)
-    send_x = jnp.dot(token_pick, full_x, preferred_element_type=jnp.bfloat16).reshape(
+    send_x = pick_rows(token_pick, jnp.ones((slot_total, 1), jnp.float32), full_x).reshape(
         dp_count, capacity, features
     )
-    slot_dy = jnp.dot(token_pick, full_dy, preferred_element_type=jnp.float32)
-    send_do = (
-        (slot_gate[:, None] * slot_dy).astype(jnp.bfloat16).reshape(dp_count, capacity, features)
+    send_do = pick_rows(token_pick, slot_gate[:, None], full_dy).reshape(
+        dp_count, capacity, features
     )
     weights = (w_gate[0], w_up[0], w_down[0])
     recv_x = lax.all_to_all(send_x, "dp", split_axis=0, concat_axis=0, tiled=True)
@@ -113,7 +138,9 @@
         preferred_element_type=jnp.float32,
     )
     grad_part = contract_first(token_pick, back_grad)
-    gate_terms = jnp.sum(slot_dy * back_out.astype(jnp.float32), axis=1)
+    gate_terms = jnp.sum(
+        token_pick.astype(jnp.float32) * contract_last(back_out, full_dy), axis=1
+    )
     gate_part = jnp.sum(jnp.where(picks, gate_terms[:, None], 0.0), axis=0).reshape(
         tok_count, chosen
     )

time: 268 us -> 277 us (1.034)
  Pallas kernels: 0 us -> 8.31 us
  matrix products: 22.2 us -> 17.5 us
  blocking collectives: 177 us -> 181 us
    pallas_call x0 -> x2, Pallas kernels: none -> 8.31 us  [pick_rows(): pl.pallas_call(pick_kernel, grid=(slots // block,), in_specs=[pl.BlockSpe...]
    dot_general x2 -> x0, matrix products: 5.32 us -> none  [the longest x1 3.3 us: per_device(): slot_dy = jnp.dot(token_pick, full_dy, preferred_element_type=jnp.float32)]
    dot_general x3 -> x4, matrix products: 6.32 us -> 7.11 us  [contract_last(): lax.dot_general(first_op, second_op, (((1,), (1,)), ((), ())), preferred_...]
  transfers between devices with their start and end apart: 3 -> 3, of which waited for: 2 -> 2; matrix products, arithmetic and copies ran while one was open for 5% -> 4% of each run, Pallas kernels for 0% -> 2%
where the time goes in v7:
time: 277 us; the launch traced here: 276 us
  blocking collectives  181 us (65%)
  waiting for transfers between devices  28.9 us (10%)
  matrix products  17.5 us (6%)
  starting transfers between devices  15.3 us (6%)
  between operations  14.3 us (5%)
  Pallas kernels  8.31 us (3%)
  local copies, waits for them, and re-layouts  5.75 us (2%)
  other arithmetic  5.24 us (2%)
    psum x1, blocking collectives, per_device(): grad_gates = lax.psum(gate_part, 'expert')  54.8 us
    all_to_all x1, blocking collectives, per_device(): lax.all_to_all(jnp.concatenate([part_out.reshape(dp_count, capacity, feat...  54.6 us
    all_gather x1, blocking collectives, per_device(): full_x = lax.all_gather(tokens, 'expert', axis=1, tiled=True)  40.5 us
    all_gather x1, blocking collectives, per_device(): full_dy = lax.all_gather(cotangent, 'expert', axis=1, tiled=True)  31 us
    all_to_all x1, waiting for transfers between devices, per_device(): lax.all_to_all(send_do, 'dp', split_axis=0, concat_axis=0, tiled=True)  23.6 us
    pallas_call x2, Pallas kernels, pick_rows(): pl.pallas_call(pick_kernel, grid=(slots // block,), in_specs=[pl.BlockSpe...  8.31 us
    all_to_all x1, starting transfers between devices, per_device(): lax.all_to_all(send_x, 'dp', split_axis=0, concat_axis=0, tiled=True)  7.75 us
    all_to_all x1, starting transfers between devices, per_device(): lax.all_to_all(send_do, 'dp', split_axis=0, concat_axis=0, tiled=True)  7.56 us
  transfers between devices with their start and end apart: 3, of which 2 were waited for; matrix products, arithmetic and copies ran while one was open for 4% of the time, Pallas kernels for 2%

profile of v7, /device:TPU:6, one launch (start us, length us, event | category | flops | bytes accessed | tf_op | source)
XLA Modules:
  0.0 276.3 jit_solution(5908823898385211353)
XLA Ops:
  7.2 0.0 copy-start
  7.2 0.0 copy-start.6
  7.2 0.9 copy.24
  8.1 0.1 reshape.163
  8.2 0.5 fusion.7
  8.8 0.1 convert_element_type.61
  8.8 0.1 fusion.26
  9.0 0.9 fusion.4
  9.9 0.7 convert_element_type.62.pick_ref
  10.6 0.0 copy-done.6
  10.6 40.5 %all_gather.6.rows_ref = bf16[128,2048]{1,0:T(8,128)(2,1)} all-gather(bf16[128,128]{1,0:T(8,128)(2,1)S(1)} %copy-done.6), channel_id=1, replica_groups=mesh['dp'=32,'expert'=16] {'expert'}, dimensions={1}, use_global_device_ids=true | all-gather | bytes 557056 | tf_op jit(solution)/shard_map/all_gather | solution.py:76
  51.1 0.7 broadcast_in_dim.59.scale_ref
  51.8 4.1 %pick_rows.2 = bf16[512,2048]{1,0:T(8,128)(2,1)} custom-call(bf16[512,128]{1,0:T(8,128)(2,1)} %convert_element_type.62.pick_ref, f32[512,1]{1,0:T(8,128)} %broadcast_in_dim.59.scale_ref, bf16[128,2048]{1,0:T(8,128)(2,1)} %all_gather.6.rows_ref), custom_call_target="tpu_custom_call" | custom-call | tf_op jit(solution)/shard_map/pick_rows/pallas_call | solution.py:60
  55.9 0.0 copy-start.8
  55.9 0.0 copy-start.7
  55.9 7.7 %all-to-all-start = ((bf16[32,16,2048]{2,1,0:T(8,128)(2,1)}), bf16[32,16,2048]{2,1,0:T(8,128)(2,1)S(1)}, u32[]{:S(2)}, u32[]{:S(2)}) async-start(bf16[32,16,2048]{2,1,0:T(8,128)(2,1)} %bitcast.61), calls=%async_computation | async-start | bytes 4194304 | tf_op jit(solution)/shard_map/all_to_all | solution.py:112
  63.7 0.0 copy-done.8
  63.7 0.1 copy.30
  63.8 0.1 broadcast_in_dim.56
  63.9 0.3 select_reduce_fusion.1
  64.2 0.9 copy.31.scale_ref
  65.1 0.0 copy-done.7
  65.1 31.0 %all_gather.7.rows_ref = bf16[128,2048]{1,0:T(8,128)(2,1)} all-gather(bf16[128,128]{1,0:T(8,128)(2,1)S(1)} %copy-done.7), channel_id=1, replica_groups=mesh['dp'=32,'expert'=16] {'expert'}, dimensions={1}, use_global_device_ids=true | all-gather | bytes 557056 | tf_op jit(solution)/shard_map/all_gather | solution.py:77
  96.1 4.2 %pick_rows.3 = bf16[512,2048]{1,0:T(8,128)(2,1)} custom-call(bf16[512,128]{1,0:T(8,128)(2,1)} %convert_element_type.62.pick_ref, f32[512,1]{1,0:T(8,128)} %copy.31.scale_ref, bf16[128,2048]{1,0:T(8,128)(2,1)} %all_gather.7.rows_ref), custom_call_target="tpu_custom_call" | custom-call | tf_op jit(solution)/shard_map/pick_rows/pallas_call | solution.py:60
  100.3 0.0 all-to-all-done
  100.3 7.6 %all-to-all-start.1 = ((bf16[32,16,2048]{2,1,0:T(8,128)(2,1)}), bf16[32,16,2048]{2,1,0:T(8,128)(2,1)}, u32[]{:S(2)}, u32[]{:S(2)}) async-start(bf16[32,16,2048]{2,1,0:T(8,128)(2,1)} %bitcast.62), calls=%async_computation.1 | async-start | bytes 4194304 | tf_op jit(solution)/shard_map/all_to_all | solution.py:113
  107.8 0.0 reduce-scatter.2.cloned.1.call-start
  107.9 2.7 fusion.16
  110.6 23.6 %all-to-all-done.1 = bf16[32,16,2048]{2,1,0:T(8,128)(2,1)} async-done(((bf16[32,16,2048]{2,1,0:T(8,128)(2,1)}), bf16[32,16,2048]{2,1,0:T(8,128)(2,1)}, u32[]{:S(2)}, u32[]{:S(2)}) %all-to-all-start.1) | async-done | bytes 2097184 | tf_op jit(solution)/shard_map/all_to_all | solution.py:113
  134.2 0.0 copy-start.9
  134.2 2.7 fusion.8
  136.9 0.0 copy-done
  136.9 0.0 copy-done.9
  136.9 0.0 copy-start.5
  136.9 0.9 multiply_convert_fusion.2
  137.9 0.0 copy-start.4
  137.9 0.2 copy-done.5
  138.0 0.7 convolution_convert_fusion
  138.8 0.3 copy-done.4
  139.0 0.7 fusion.14
  139.8 0.8 add_convert_fusion
  140.6 0.6 pad_maximum_fusion
  141.1 54.6 %all_to_all.15 = bf16[32,32,2048]{2,1,0:T(8,128)(2,1)S(1)} all-to-all(bf16[32,32,2048]{2,1,0:T(8,128)(2,1)S(1)} %pad_maximum_fusion), channel_id=1, replica_groups=mesh['dp'=32,'expert'=16] {'dp'}, dimensions={0} | all-to-all | bytes 8388608 | tf_op jit(solution)/shard_map/all_to_all | solution.py:117
  195.7 0.6 fusion.35
  196.3 0.0 copy-start.1
  196.3 1.1 convolution_bitcast_fusion
  197.5 0.5 convolution_bitcast_fusion.1
  198.0 0.0 copy-done.1
  198.0 1.4 pad_maximum_fusion.1
  199.4 0.0 reduce-scatter.2.cloned.1.call-update
  199.5 3.1 %fusion.3 = bf16[1,192,2048]{2,1,0:T(8,128)(2,1)} fusion(bf16[512,192]{0,1:T(8,128)(2,1)S(1)} %get-tuple-element.20, bf16[512,2048]{1,0:T(8,128)(2,1)} %bitcast.8), kind=kOutput, calls=%fused_computation.12 | convolution fusion | flops 403046400 | bytes 3080192 | tf_op jit(solution)/shard_map/dot_general | solution.py:25
  202.5 1.5 fusion.1
  204.0 0.0 copy-start.2
  204.0 1.5 fusion.2
  205.4 0.2 copy-done.2
  205.6 0.3 copy-done.3
  205.9 0.8 fusion.5
  206.7 0.3 select_reduce_fusion
  207.1 0.1 reshape.172
  207.2 54.8 %psum.7 = f32[128,8]{1,0:T(8,128)S(1)} all-reduce(f32[128,8]{1,0:T(8,128)S(1)} %reshape.172), channel_id=1, replica_groups=mesh['dp'=32,'expert'=16] {'expert'}, use_global_device_ids=true, to_apply=%region_6.7 | all-reduce | flops 1024 | bytes 8192 | tf_op jit(solution)/shard_map/psum | solution.py:150
  261.9 0.7 copy.33
  262.6 5.3 %reduce-scatter.2.cloned.1.call-done = f32[2,128,128]{2,1,0:T(8,128)} async-done(((f32[2,128,2048]{2,1,0:T(8,128)}), f32[2,128,128]{2,1,0:T(8,128)}) %reduce-scatter.2.cloned.1.call-update) | async-done | bytes 131088 | tf_op jit(solution)/shard_map/reduce_scatter | solution.py:147
  267.9 0.9 convert.4
  268.8 0.6 slice_bitcast_fusion
  (6 shorter events, 0.1 us)
Async XLA Ops:
  7.2 129.7 %copy-start = (bf16[1,192,2048]{2,1,0:T(8,128)(2,1)S(1)}, bf16[1,192,2048]{2,1,0:T(8,128)(2,1)}, u32[]{:S(2)}) copy-start(bf16[1,192,2048]{2,1,0:T(8,128)(2,1)} %param.12) | copy-start | bytes 2359300
  7.2 3.4 %copy-start.6 = (bf16[128,128]{1,0:T(8,128)(2,1)S(1)}, bf16[128,128]{1,0:T(8,128)(2,1)}, u32[]{:S(2)}) copy-start(bf16[128,128]{1,0:T(8,128)(2,1)} %param.7) | copy-start | bytes 98308
  55.9 7.8 %copy-start.8 = (f32[128,8]{0,1:T(8,128)S(1)}, f32[128,8]{0,1:T(8,128)}, u32[]{:S(2)}) copy-start(f32[128,8]{0,1:T(8,128)} %param.10) | copy-start | bytes 12292
  55.9 9.1 %copy-start.7 = (bf16[128,128]{1,0:T(8,128)(2,1)S(1)}, bf16[128,128]{1,0:T(8,128)(2,1)}, u32[]{:S(2)}) copy-start(bf16[128,128]{1,0:T(8,128)(2,1)} %param.8) | copy-start | bytes 98308
  55.9 44.3 %all-to-all-start = ((bf16[32,16,2048]{2,1,0:T(8,128)(2,1)}), bf16[32,16,2048]{2,1,0:T(8,128)(2,1)S(1)}, u32[]{:S(2)}, u32[]{:S(2)}) async-start(bf16[32,16,2048]{2,1,0:T(8,128)(2,1)} %bitcast.61), calls=%async_computation | async-start | bytes 4194304 | tf_op jit(solution)/shard_map/all_to_all | solution.py:112
  100.3 33.9 %all-to-all-start.1 = ((bf16[32,16,2048]{2,1,0:T(8,128)(2,1)}), bf16[32,16,2048]{2,1,0:T(8,128)(2,1)}, u32[]{:S(2)}, u32[]{:S(2)}) async-start(bf16[32,16,2048]{2,1,0:T(8,128)(2,1)} %bitcast.62), calls=%async_computation.1 | async-start | bytes 4194304 | tf_op jit(solution)/shard_map/all_to_all | solution.py:113
  107.8 160.0 %reduce-scatter.2.cloned.1.call-start = ((), (), s32[]{:S(2)}) async-start(), calls=%async_computation.4 | async-start | bytes 2228224 | tf_op jit(solution)/shard_map/reduce_scatter | solution.py:147
  134.2 2.7 copy-start.9
  136.9 1.1 copy-start.5
  137.9 1.2 copy-start.4
  196.3 1.7 copy-start.1
  204.0 1.7 copy-start.2
  204.0 2.0 copy-start.3
Sparse Core Ops, SparseCore 0:
  199.6 68.2 reduce-scatter.1

commit v8 on v5

--- a/solution.py
+++ b/solution.py
@@ -113,7 +113,9 @@
         preferred_element_type=jnp.float32,
     )
     grad_part = contract_first(token_pick, back_grad)
-    gate_terms = jnp.sum(slot_dy * back_out.astype(jnp.float32), axis=1)
+    gate_terms = jnp.sum(
+        token_pick.astype(jnp.float32) * contract_last(back_out, full_dy), axis=1
+    )
     gate_part = jnp.sum(jnp.where(picks, gate_terms[:, None], 0.0), axis=0).reshape(
         tok_count, chosen
     )

time: 268 us -> 277 us (1.034)
  blocking collectives: 177 us -> 122 us
  waiting for transfers between devices: 29.3 us -> 82.4 us
  starting transfers between devices: 15.2 us -> 22.8 us
    all_to_all x1 -> x0, blocking collectives: 54.6 us -> none  [per_device(): lax.all_to_all(jnp.concatenate([part_out.reshape(dp_count, capacity, feat...]
    all_to_all x0 -> x1, waiting for transfers between devices: none -> 50.5 us  [per_device(): lax.all_to_all(jnp.concatenate([part_out.reshape(dp_count, capacity, feat...]
    all_to_all x0 -> x1, starting transfers between devices: none -> 7.39 us  [per_device(): lax.all_to_all(jnp.concatenate([part_out.reshape(dp_count, capacity, feat...]
    dot_general x3 -> x4, matrix products: 6.32 us -> 7.18 us  [contract_last(): lax.dot_general(first_op, second_op, (((1,), (1,)), ((), ())), preferred_...]
  transfers between devices with their start and end apart: 3 -> 4, of which waited for: 2 -> 3; matrix products, arithmetic and copies ran while one was open for 5% -> 5% of each run, Pallas kernels for 0% -> 0%
where the time goes in v8:
time: 277 us; the launch traced here: 276 us
  blocking collectives  122 us (44%)
  waiting for transfers between devices  82.4 us (30%)
  starting transfers between devices  22.8 us (8%)
  matrix products  21.7 us (8%)
  between operations  14.4 us (5%)
  other arithmetic  6.57 us (2%)
  local copies, waits for them, and re-layouts  6.38 us (2%)
    psum x1, blocking collectives, per_device(): grad_gates = lax.psum(gate_part, 'expert')  54.8 us
    all_to_all x1, waiting for transfers between devices, per_device(): lax.all_to_all(jnp.concatenate([part_out.reshape(dp_count, capacity, feat...  50.5 us
    all_gather x1, blocking collectives, per_device(): full_x = lax.all_gather(tokens, 'expert', axis=1, tiled=True)  38.8 us
    all_gather x1, blocking collectives, per_device(): full_dy = lax.all_gather(cotangent, 'expert', axis=1, tiled=True)  28.7 us
    all_to_all x1, waiting for transfers between devices, per_device(): lax.all_to_all(send_do, 'dp', split_axis=0, concat_axis=0, tiled=True)  23.7 us
    reduce_scatter x1, waiting for transfers between devices, per_device(): lax.psum_scatter(jnp.stack([out_part, grad_part]), 'expert', scatter_dime...  8.18 us
    all_to_all x1, starting transfers between devices, per_device(): lax.all_to_all(send_x, 'dp', split_axis=0, concat_axis=0, tiled=True)  7.75 us
    all_to_all x1, starting transfers between devices, per_device(): lax.all_to_all(send_do, 'dp', split_axis=0, concat_axis=0, tiled=True)  7.44 us
  transfers between devices with their start and end apart: 4, of which 3 were waited for; matrix products, arithmetic and copies ran while one was open for 5% of the time, Pallas kernels for 0%

profile of v8, /device:TPU:6, one launch (start us, length us, event | category | flops | bytes accessed | tf_op | source)
XLA Modules:
  0.0 276.5 jit_solution(9143943340222234590)
XLA Ops:
  7.2 0.0 copy-start
  7.2 0.9 copy.23
  8.0 0.1 reshape.162
  8.2 0.5 fusion.7
  8.7 0.1 convert_element_type.64
  8.8 0.1 fusion.29
  9.0 0.9 fusion.4
  9.9 38.8 %all_gather.6 = bf16[128,2048]{1,0:T(8,128)(2,1)S(1)} all-gather(bf16[128,128]{1,0:T(8,128)(2,1)} %param.7), channel_id=1, replica_groups=mesh['dp'=32,'expert'=16] {'expert'}, dimensions={1}, use_global_device_ids=true | all-gather | bytes 557056 | tf_op jit(solution)/shard_map/all_gather | solution.py:50
  48.7 2.0 fusion.18
  50.7 7.8 %all-to-all-start = ((bf16[32,16,2048]{2,1,0:T(8,128)(2,1)}), bf16[32,16,2048]{2,1,0:T(8,128)(2,1)S(1)}, u32[]{:S(2)}, u32[]{:S(2)}) async-start(bf16[32,16,2048]{2,1,0:T(8,128)(2,1)} %fusion.18), calls=%async_computation | async-start | bytes 4194304 | tf_op jit(solution)/shard_map/all_to_all | solution.py:87
  58.4 0.0 copy-done.11
  58.4 0.1 copy.30
  58.5 0.1 broadcast_in_dim.51
  58.7 0.3 select_reduce_fusion.1
  58.9 0.0 copy-done.10
  59.0 28.7 %all_gather.7 = bf16[128,2048]{1,0:T(8,128)(2,1)S(1)} all-gather(bf16[128,128]{1,0:T(8,128)(2,1)S(1)} %copy-done.10), channel_id=1, replica_groups=mesh['dp'=32,'expert'=16] {'expert'}, dimensions={1}, use_global_device_ids=true | all-gather | bytes 557056 | tf_op jit(solution)/shard_map/all_gather | solution.py:51
  87.7 2.0 multiply_convert_fusion
  89.7 0.0 all-to-all-done
  89.7 7.4 %all-to-all-start.1 = ((bf16[32,16,2048]{2,1,0:T(8,128)(2,1)}), bf16[32,16,2048]{2,1,0:T(8,128)(2,1)}, u32[]{:S(2)}, u32[]{:S(2)}) async-start(bf16[32,16,2048]{2,1,0:T(8,128)(2,1)} %bitcast.66), calls=%async_computation.1 | async-start | bytes 4194304 | tf_op jit(solution)/shard_map/all_to_all | solution.py:88
  97.2 2.7 fusion.16
  99.9 23.7 %all-to-all-done.1 = bf16[32,16,2048]{2,1,0:T(8,128)(2,1)} async-done(((bf16[32,16,2048]{2,1,0:T(8,128)(2,1)}), bf16[32,16,2048]{2,1,0:T(8,128)(2,1)}, u32[]{:S(2)}, u32[]{:S(2)}) %all-to-all-start.1) | async-done | bytes 2097184 | tf_op jit(solution)/shard_map/all_to_all | solution.py:88
  123.5 2.7 fusion.8
  126.2 0.0 copy-done
  126.2 0.0 copy-done.12
  126.2 0.0 copy-start.7
  126.2 0.9 multiply_convert_fusion.3
  127.2 0.0 copy-start.3
  127.2 0.0 copy-start.6
  127.2 0.0 copy-start.8
  127.2 0.0 copy-start.5
  127.2 0.1 copy-done.7
  127.4 0.7 convolution_convert_fusion
  128.1 0.5 copy-done.5
  128.6 0.7 fusion.14
  129.3 0.0 copy-done.3
  129.3 0.0 copy-done.6
  129.4 0.0 copy-done.8
  129.4 0.8 add_convert_fusion
  130.1 2.6 pad_maximum_fusion
  132.7 7.4 %all-to-all-start.2 = ((bf16[32,32,2048]{2,1,0:T(8,128)(2,1)}), bf16[32,32,2048]{2,1,0:T(8,128)(2,1)}, u32[]{:S(2)}, u32[]{:S(2)}) async-start(bf16[32,32,2048]{2,1,0:T(8,128)(2,1)} %pad_maximum_fusion), calls=%async_computation.2 | async-start | bytes 8388608 | tf_op jit(solution)/shard_map/all_to_all | solution.py:92
  140.1 0.2 reduce-scatter.2.cloned.1.call-start
  140.3 0.1 copy.29
  140.5 50.5 %all-to-all-done.2 = bf16[32,32,2048]{2,1,0:T(8,128)(2,1)} async-done(((bf16[32,32,2048]{2,1,0:T(8,128)(2,1)}), bf16[32,32,2048]{2,1,0:T(8,128)(2,1)}, u32[]{:S(2)}, u32[]{:S(2)}) %all-to-all-start.2) | async-done | bytes 4194336 | tf_op jit(solution)/shard_map/all_to_all | solution.py:92
  191.0 2.7 fusion.37
  193.7 0.0 copy-start.1
  193.8 0.5 convolution_bitcast_fusion.1
  194.3 1.1 convolution_bitcast_fusion
  195.3 1.5 pad_maximum_fusion.1
  196.8 0.0 reduce-scatter.2.cloned.1.call-update
  196.8 0.0 copy-start.4
  196.8 3.2 %fusion.3 = bf16[1,192,2048]{2,1,0:T(8,128)(2,1)} fusion(bf16[512,192]{0,1:T(8,128)(2,1)} %copy-done.6, bf16[512,2048]{1,0:T(8,128)(2,1)} %bitcast.8), kind=kOutput, calls=%fused_computation.13 | convolution fusion | flops 403046400 | bytes 3080192 | tf_op jit(solution)/shard_map/dot_general | solution.py:23
  200.0 0.0 copy-done.4
  200.1 1.5 fusion.1
  201.5 0.0 copy-done.9
  201.5 1.5 fusion.2
  203.0 0.2 copy-done.2
  203.2 0.9 fusion.5
  204.0 0.3 select_reduce_fusion
  204.4 0.1 reshape.170
  204.5 54.8 %psum.7 = f32[128,8]{1,0:T(8,128)S(1)} all-reduce(f32[128,8]{1,0:T(8,128)S(1)} %reshape.170), channel_id=1, replica_groups=mesh['dp'=32,'expert'=16] {'expert'}, use_global_device_ids=true, to_apply=%region_6.7 | all-reduce | flops 1024 | bytes 8192 | tf_op jit(solution)/shard_map/psum | solution.py:125
  259.2 0.7 copy.31
  259.9 8.2 %reduce-scatter.2.cloned.1.call-done = f32[2,128,128]{2,1,0:T(8,128)} async-done(((f32[2,128,2048]{2,1,0:T(8,128)}), f32[2,128,128]{2,1,0:T(8,128)}) %reduce-scatter.2.cloned.1.call-update) | async-done | bytes 131088 | tf_op jit(solution)/shard_map/reduce_scatter | solution.py:122
  268.1 0.9 convert.4
  269.0 0.6 slice_bitcast_fusion
  (11 shorter events, 0.1 us)
Async XLA Ops:
  7.2 119.0 %copy-start = (bf16[1,192,2048]{2,1,0:T(8,128)(2,1)S(1)}, bf16[1,192,2048]{2,1,0:T(8,128)(2,1)}, u32[]{:S(2)}) copy-start(bf16[1,192,2048]{2,1,0:T(8,128)(2,1)} %param.12) | copy-start | bytes 2359300
  50.7 7.8 %copy-start.11 = (f32[128,8]{0,1:T(8,128)S(1)}, f32[128,8]{0,1:T(8,128)}, u32[]{:S(2)}) copy-start(f32[128,8]{0,1:T(8,128)} %param.10) | copy-start | bytes 12292
  50.7 8.3 %copy-start.10 = (bf16[128,128]{1,0:T(8,128)(2,1)S(1)}, bf16[128,128]{1,0:T(8,128)(2,1)}, u32[]{:S(2)}) copy-start(bf16[128,128]{1,0:T(8,128)(2,1)} %param.8) | copy-start | bytes 98308
  50.7 39.0 %all-to-all-start = ((bf16[32,16,2048]{2,1,0:T(8,128)(2,1)}), bf16[32,16,2048]{2,1,0:T(8,128)(2,1)S(1)}, u32[]{:S(2)}, u32[]{:S(2)}) async-start(bf16[32,16,2048]{2,1,0:T(8,128)(2,1)} %fusion.18), calls=%async_computation | async-start | bytes 4194304 | tf_op jit(solution)/shard_map/all_to_all | solution.py:87
  89.7 33.8 %all-to-all-start.1 = ((bf16[32,16,2048]{2,1,0:T(8,128)(2,1)}), bf16[32,16,2048]{2,1,0:T(8,128)(2,1)}, u32[]{:S(2)}, u32[]{:S(2)}) async-start(bf16[32,16,2048]{2,1,0:T(8,128)(2,1)} %bitcast.66), calls=%async_computation.1 | async-start | bytes 4194304 | tf_op jit(solution)/shard_map/all_to_all | solution.py:88
  123.5 2.7 copy-start.12
  126.2 1.1 copy-start.7
  127.2 2.2 copy-start.3
  127.2 2.2 copy-start.6
  127.2 2.2 copy-start.8
  127.2 1.4 copy-start.5
  132.7 58.3 %all-to-all-start.2 = ((bf16[32,32,2048]{2,1,0:T(8,128)(2,1)}), bf16[32,32,2048]{2,1,0:T(8,128)(2,1)}, u32[]{:S(2)}, u32[]{:S(2)}) async-start(bf16[32,32,2048]{2,1,0:T(8,128)(2,1)} %pad_maximum_fusion), calls=%async_computation.2 | async-start | bytes 8388608 | tf_op jit(solution)/shard_map/all_to_all | solution.py:92
  140.1 128.0 %reduce-scatter.2.cloned.1.call-start = ((), (), s32[]{:S(2)}) async-start(), calls=%async_computation.4 | async-start | bytes 2228224 | tf_op jit(solution)/shard_map/reduce_scatter | solution.py:122
  193.7 1.6 copy-start.1
  196.8 3.2 %copy-start.4 = (bf16[512,192]{0,1:T(8,128)(2,1)S(1)}, bf16[512,192]{0,1:T(8,128)(2,1)}, u32[]{:S(2)}) copy-start(bf16[512,192]{0,1:T(8,128)(2,1)} %copy-done.3) | copy-start | bytes 589828
  200.0 1.5 copy-start.9
  201.5 1.7 copy-start.2
Sparse Core Ops, SparseCore 0:
  196.9 71.0 reduce-scatter.1

commit v9 on v5

--- a/solution.py
+++ b/solution.py
@@ -120,7 +120,10 @@
     summed = lax.psum_scatter(
         jnp.stack([out_part, grad_part]), "expert", scatter_dimension=2, tiled=True
     )
-    grad_gates = lax.psum(gate_part, "expert")
+    gate_all = lax.all_gather(gate_part, "expert", axis=0, tiled=False)
+    grad_gates = gate_all[0]
+    for source in range(1, column_count):
+        grad_gates = grad_gates + gate_all[source]
     return (
         summed[0].astype(jnp.bfloat16),
         summed[1].astype(jnp.bfloat16),

time: 268 us -> 268 us (level)
  waiting for transfers between devices: 29.3 us -> 55.8 us
  blocking collectives: 177 us -> 151 us
    psum x1 -> x0, blocking collectives: 54.8 us -> none  [per_device(): grad_gates = lax.psum(gate_part, 'expert')]
    all_gather x0 -> x1, blocking collectives: none -> 28.4 us  [per_device(): gate_all = lax.all_gather(gate_part, 'expert', axis=0, tiled=False)]
    reduce_scatter x1, waiting for transfers between devices: 5.71 us -> 32.2 us  [per_device(): lax.psum_scatter(jnp.stack([out_part, grad_part]), 'expert', scatter_dime...]
where the time goes in v9:
time: 268 us; the launch traced here: 267 us
  blocking collectives  151 us (56%)
  waiting for transfers between devices  55.8 us (21%)
  matrix products  22.2 us (8%)
  starting transfers between devices  15.2 us (6%)
  between operations  14.3 us (5%)
  other arithmetic  5.73 us (2%)
  local copies, waits for them, and re-layouts  3.26 us (1%)
    all_to_all x1, blocking collectives, per_device(): lax.all_to_all(jnp.concatenate([part_out.reshape(dp_count, capacity, feat...  54.6 us
    all_gather x1, blocking collectives, per_device(): full_x = lax.all_gather(tokens, 'expert', axis=1, tiled=True)  38.8 us
    reduce_scatter x1, waiting for transfers between devices, per_device(): lax.psum_scatter(jnp.stack([out_part, grad_part]), 'expert', scatter_dime...  32.2 us
    all_gather x1, blocking collectives, per_device(): full_dy = lax.all_gather(cotangent, 'expert', axis=1, tiled=True)  28.7 us
    all_gather x1, blocking collectives, per_device(): gate_all = lax.all_gather(gate_part, 'expert', axis=0, tiled=False)  28.4 us
    all_to_all x1, waiting for transfers between devices, per_device(): lax.all_to_all(send_do, 'dp', split_axis=0, concat_axis=0, tiled=True)  23.6 us
    all_to_all x1, starting transfers between devices, per_device(): lax.all_to_all(send_x, 'dp', split_axis=0, concat_axis=0, tiled=True)  7.75 us
    all_to_all x1, starting transfers between devices, per_device(): lax.all_to_all(send_do, 'dp', split_axis=0, concat_axis=0, tiled=True)  7.44 us
  transfers between devices with their start and end apart: 3, of which 2 were waited for; matrix products, arithmetic and copies ran while one was open for 5% of the time, Pallas kernels for 0%

profile of v9, /device:TPU:6, one launch (start us, length us, event | category | flops | bytes accessed | tf_op | source)
XLA Modules:
  0.0 267.0 jit_solution(2629839589481128594)
XLA Ops:
  7.2 0.0 copy-start
  7.2 0.9 copy.28
  8.0 0.1 reshape.163
  8.2 0.5 fusion.6
  8.7 0.1 convert_element_type.66
  8.8 0.1 fusion.30
  9.0 0.9 fusion.4
  9.9 38.8 %all_gather.9 = bf16[128,2048]{1,0:T(8,128)(2,1)S(1)} all-gather(bf16[128,128]{1,0:T(8,128)(2,1)} %param.7), channel_id=1, replica_groups=mesh['dp'=32,'expert'=16] {'expert'}, dimensions={1}, use_global_device_ids=true | all-gather | bytes 557056 | tf_op jit(solution)/shard_map/all_gather | solution.py:50
  48.7 2.0 fusion.17
  50.7 0.0 copy-start.7
  50.7 0.0 copy-start.6
  50.7 7.7 %all-to-all-start = ((bf16[32,16,2048]{2,1,0:T(8,128)(2,1)}), bf16[32,16,2048]{2,1,0:T(8,128)(2,1)S(1)}, u32[]{:S(2)}, u32[]{:S(2)}) async-start(bf16[32,16,2048]{2,1,0:T(8,128)(2,1)} %fusion.17), calls=%async_computation | async-start | bytes 4194304 | tf_op jit(solution)/shard_map/all_to_all | solution.py:87
  58.4 0.0 copy-done.7
  58.4 0.1 copy.34
  58.5 0.1 broadcast_in_dim.51
  58.7 0.3 select_reduce_fusion.1
  59.0 0.0 copy-done.6
  59.0 28.7 %all_gather.10 = bf16[128,2048]{1,0:T(8,128)(2,1)S(1)} all-gather(bf16[128,128]{1,0:T(8,128)(2,1)S(1)} %copy-done.6), channel_id=1, replica_groups=mesh['dp'=32,'expert'=16] {'expert'}, dimensions={1}, use_global_device_ids=true | all-gather | bytes 557056 | tf_op jit(solution)/shard_map/all_gather | solution.py:51
  87.7 3.3 %multiply_convert_fusion = (bf16[512,2048]{1,0:T(8,128)(2,1)}, f32[512,2048]{1,0:T(8,128)}) fusion(f32[512]{0:T(512)S(1)} %select_reduce_fusion.1, pred[512,128]{1,0:T(8,128)(4,1)S(1)} %fusion.4, bf16[128,2048]{1,0:T(8,128)(2,1)S(1)} %all_gather.10), kind=kOutput, calls=%fused_computation.3 | convolution fusion | flops 270532608 | bytes 6883328 | tf_op jit(solution)/shard_map/dot_general | solution.py:82
  91.0 0.0 all-to-all-done
  91.0 7.4 %all-to-all-start.1 = ((bf16[32,16,2048]{2,1,0:T(8,128)(2,1)}), bf16[32,16,2048]{2,1,0:T(8,128)(2,1)}, u32[]{:S(2)}, u32[]{:S(2)}) async-start(bf16[32,16,2048]{2,1,0:T(8,128)(2,1)} %bitcast.68), calls=%async_computation.1 | async-start | bytes 4194304 | tf_op jit(solution)/shard_map/all_to_all | solution.py:88
  98.4 0.0 reduce-scatter.2.cloned.1.call-start
  98.5 2.7 %fusion.15 = f32[512,192]{0,1:T(8,128)} fusion(bf16[512,2048]{1,0:T(8,128)(2,1)S(1)} %bitcast.63, bf16[1,192,2048]{2,1,0:T(8,128)(2,1)} %param.11), kind=kOutput, calls=%fused_computation.31 | convolution fusion | flops 402653184 | bytes 3276800 | tf_op jit(solution)/shard_map/dot_general | solution.py:17
  101.2 23.6 %all-to-all-done.1 = bf16[32,16,2048]{2,1,0:T(8,128)(2,1)} async-done(((bf16[32,16,2048]{2,1,0:T(8,128)(2,1)}), bf16[32,16,2048]{2,1,0:T(8,128)(2,1)}, u32[]{:S(2)}, u32[]{:S(2)}) %all-to-all-start.1) | async-done | bytes 2097184 | tf_op jit(solution)/shard_map/all_to_all | solution.py:88
  124.8 0.0 copy-start.8
  124.8 2.7 fusion.7
  127.5 0.0 copy-done
  127.5 0.0 copy-done.8
  127.5 0.0 copy-start.5
  127.5 0.9 multiply_convert_fusion.3
  128.5 0.0 copy-start.4
  128.5 0.2 copy-done.5
  128.6 0.7 convolution_convert_fusion
  129.4 0.3 copy-done.4
  129.6 0.7 fusion.13
  130.4 0.8 add_convert_fusion
  131.2 0.6 pad_maximum_fusion
  131.7 54.6 %all_to_all.15 = bf16[32,32,2048]{2,1,0:T(8,128)(2,1)S(1)} all-to-all(bf16[32,32,2048]{2,1,0:T(8,128)(2,1)S(1)} %pad_maximum_fusion), channel_id=1, replica_groups=mesh['dp'=32,'expert'=16] {'dp'}, dimensions={0} | all-to-all | bytes 8388608 | tf_op jit(solution)/shard_map/all_to_all | solution.py:92
  186.3 0.6 fusion.39
  186.9 0.0 copy-start.1
  186.9 0.5 convolution_bitcast_fusion.1
  187.4 1.1 convolution_bitcast_fusion
  188.6 0.0 copy-done.1
  188.6 1.5 pad_maximum_fusion.1
  190.1 0.0 reduce-scatter.2.cloned.1.call-update
  190.1 0.0 copy-start.3
  190.1 3.2 %fusion.3 = bf16[1,192,2048]{2,1,0:T(8,128)(2,1)} fusion(bf16[512,192]{0,1:T(8,128)(2,1)S(1)} %get-tuple-element.14, bf16[512,2048]{1,0:T(8,128)(2,1)} %bitcast.8), kind=kOutput, calls=%fused_computation.14 | convolution fusion | flops 403046400 | bytes 3080192 | tf_op jit(solution)/shard_map/dot_general | solution.py:23
  193.3 1.5 fusion.1
  194.8 0.0 copy-start.2
  194.8 1.5 fusion.2
  196.2 0.0 copy-done.3
  196.2 0.2 copy-done.2
  196.4 0.5 multiply_reduce_fusion
  196.9 0.3 select_reduce_fusion
  197.3 0.1 all_gather_reshape.3
  197.4 28.4 %all_gather.11 = f32[16,128,8]{1,2,0:T(8,128)S(1)} all-gather(f32[1,128,8]{1,2,0:T(8,128)S(1)} %copy.35), channel_id=1, replica_groups=mesh['dp'=32,'expert'=16] {'expert'}, dimensions={0}, use_global_device_ids=true | all-gather | bytes 69632 | tf_op jit(solution)/shard_map/all_gather | solution.py:123
  225.8 0.6 fusion.36
  226.4 32.2 %reduce-scatter.2.cloned.1.call-done = f32[2,128,128]{2,1,0:T(8,128)} async-done(((f32[2,128,2048]{2,1,0:T(8,128)}), f32[2,128,128]{2,1,0:T(8,128)}) %reduce-scatter.2.cloned.1.call-update) | async-done | bytes 131088 | tf_op jit(solution)/shard_map/reduce_scatter | solution.py:120
  258.6 0.9 convert.4
  259.5 0.6 slice_bitcast_fusion
  (6 shorter events, 0.1 us)
Async XLA Ops:
  7.2 120.3 %copy-start = (bf16[1,192,2048]{2,1,0:T(8,128)(2,1)S(1)}, bf16[1,192,2048]{2,1,0:T(8,128)(2,1)}, u32[]{:S(2)}) copy-start(bf16[1,192,2048]{2,1,0:T(8,128)(2,1)} %param.12) | copy-start | bytes 2359300
  50.7 7.8 %copy-start.7 = (f32[128,8]{0,1:T(8,128)S(1)}, f32[128,8]{0,1:T(8,128)}, u32[]{:S(2)}) copy-start(f32[128,8]{0,1:T(8,128)} %param.10) | copy-start | bytes 12292
  50.7 8.3 %copy-start.6 = (bf16[128,128]{1,0:T(8,128)(2,1)S(1)}, bf16[128,128]{1,0:T(8,128)(2,1)}, u32[]{:S(2)}) copy-start(bf16[128,128]{1,0:T(8,128)(2,1)} %param.8) | copy-start | bytes 98308
  50.7 40.3 %all-to-all-start = ((bf16[32,16,2048]{2,1,0:T(8,128)(2,1)}), bf16[32,16,2048]{2,1,0:T(8,128)(2,1)S(1)}, u32[]{:S(2)}, u32[]{:S(2)}) async-start(bf16[32,16,2048]{2,1,0:T(8,128)(2,1)} %fusion.17), calls=%async_computation | async-start | bytes 4194304 | tf_op jit(solution)/shard_map/all_to_all | solution.py:87
  91.0 33.8 %all-to-all-start.1 = ((bf16[32,16,2048]{2,1,0:T(8,128)(2,1)}), bf16[32,16,2048]{2,1,0:T(8,128)(2,1)}, u32[]{:S(2)}, u32[]{:S(2)}) async-start(bf16[32,16,2048]{2,1,0:T(8,128)(2,1)} %bitcast.68), calls=%async_computation.1 | async-start | bytes 4194304 | tf_op jit(solution)/shard_map/all_to_all | solution.py:88
  98.4 160.2 %reduce-scatter.2.cloned.1.call-start = ((), (), s32[]{:S(2)}) async-start(), calls=%async_computation.4 | async-start | bytes 2228224 | tf_op jit(solution)/shard_map/reduce_scatter | solution.py:120
  124.8 2.7 %copy-start.8 = (f32[512,192]{0,1:T(8,128)S(1)}, f32[512,192]{0,1:T(8,128)}, u32[]{:S(2)}) copy-start(f32[512,192]{0,1:T(8,128)} %fusion.15) | copy-start | bytes 1179652
  127.5 1.1 copy-start.5
  128.5 1.2 copy-start.4
  186.9 1.7 copy-start.1
  190.1 6.1 %copy-start.3 = (f32[512,2048]{1,0:T(8,128)S(1)}, f32[512,2048]{1,0:T(8,128)}, u32[]{:S(2)}) copy-start(f32[512,2048]{1,0:T(8,128)} %get-tuple-element.20) | copy-start | bytes 12582916
  194.8 1.7 copy-start.2
Sparse Core Ops, SparseCore 0:
  190.2 68.3 reduce-scatter.1

commit v10 on v9

--- a/solution.py
+++ b/solution.py
@@ -117,8 +117,18 @@
     gate_part = jnp.sum(jnp.where(picks, gate_terms[:, None], 0.0), axis=0).reshape(
         tok_count, chosen
     )
+    group = SHARDS
+    outer = column_count // group
+    width = features // column_count
+    stacked = jnp.stack([out_part, grad_part]).reshape(2, tok_count, outer, group, width)
+    stacked = stacked.transpose(0, 1, 3, 2, 4).reshape(2, tok_count, features)
+    near = [[g * group + i for i in range(group)] for g in range(outer)]
+    far = [[g * group + i for g in range(outer)] for i in range(group)]
     summed = lax.psum_scatter(
-        jnp.stack([out_part, grad_part]), "expert", scatter_dimension=2, tiled=True
+        stacked, "expert", scatter_dimension=2, axis_index_groups=near, tiled=True
+    )
+    summed = lax.psum_scatter(
+        summed, "expert", scatter_dimension=2, axis_index_groups=far, tiled=True
     )
     gate_all = lax.all_gather(gate_part, "expert", axis=0, tiled=False)
     grad_gates = gate_all[0]

time: 268 us -> 313 us (1.17)
  waiting for transfers between devices: 55.8 us -> 73.4 us
  local copies, waits for them, and re-layouts: 3.26 us -> 15.4 us
  blocking collectives: 151 us -> 160 us
  matrix products: 22.2 us -> 27.4 us
    reduce_scatter x1 -> x2, waiting for transfers between devices: 32.2 us -> 49.8 us  [the longest x1 46.3 us: per_device(): lax.psum_scatter(stacked, 'expert', scatter_dimension=2, axis_index_group...]
    all_gather x1, blocking collectives: 28.4 us -> 37.5 us  [per_device(): gate_all = lax.all_gather(gate_part, 'expert', axis=0, tiled=False)]
    reshape x0 -> x1, local copies, waits for them, and re-layouts: none -> 3.93 us  [per_device(): back_grad = back[:, capacity:].reshape(slot_total, features)]
    dot_general x0 -> x1, local copies, waits for them, and re-layouts: none -> 3.92 us  [per_device(): lax.dot_general(gated_pick, back_out.astype(jnp.float32), (((0,), (0,)),...]
  transfers between devices with their start and end apart: 3 -> 4, of which waited for: 2 -> 3; matrix products, arithmetic and copies ran while one was open for 5% -> 5% of each run, Pallas kernels for 0% -> 0%
where the time goes in v10:
time: 313 us; the launch traced here: 312 us
  blocking collectives  160 us (51%)
  waiting for transfers between devices  73.4 us (23%)
  matrix products  27.4 us (9%)
  local copies, waits for them, and re-layouts  15.4 us (5%)
  starting transfers between devices  15.2 us (5%)
  between operations  14.3 us (5%)
  other arithmetic  6.62 us (2%)
    all_to_all x1, blocking collectives, per_device(): lax.all_to_all(jnp.concatenate([part_out.reshape(dp_count, capacity, feat...  54.6 us
    reduce_scatter x1, waiting for transfers between devices, per_device(): lax.psum_scatter(stacked, 'expert', scatter_dimension=2, axis_index_group...  46.3 us
    all_gather x1, blocking collectives, per_device(): full_x = lax.all_gather(tokens, 'expert', axis=1, tiled=True)  38.8 us
    all_gather x1, blocking collectives, per_device(): gate_all = lax.all_gather(gate_part, 'expert', axis=0, tiled=False)  37.5 us
    all_gather x1, blocking collectives, per_device(): full_dy = lax.all_gather(cotangent, 'expert', axis=1, tiled=True)  28.7 us
    all_to_all x1, waiting for transfers between devices, per_device(): lax.all_to_all(send_do, 'dp', split_axis=0, concat_axis=0, tiled=True)  23.6 us
    dot_general x4, matrix products, contract_first(): lax.dot_general(first_op, second_op, (((0,), (0,)), ((), ())), preferred_...  9.34 us
    all_to_all x1, starting transfers between devices, per_device(): lax.all_to_all(send_x, 'dp', split_axis=0, concat_axis=0, tiled=True)  7.72 us
  transfers between devices with their start and end apart: 4, of which 3 were waited for; matrix products, arithmetic and copies ran while one was open for 5% of the time, Pallas kernels for 0%

profile of v10, /device:TPU:6, one launch (start us, length us, event | category | flops | bytes accessed | tf_op | source)
XLA Modules:
  0.0 311.9 jit_solution(1997480866062890495)
XLA Ops:
  7.2 0.0 copy-start
  7.2 0.9 copy.40
  8.1 0.1 reshape.181
  8.2 0.5 fusion.6
  8.7 0.1 convert_element_type.66
  8.8 0.1 fusion.32
  9.0 0.9 fusion.4
  9.9 38.8 %all_gather.9 = bf16[128,2048]{1,0:T(8,128)(2,1)S(1)} all-gather(bf16[128,128]{1,0:T(8,128)(2,1)} %param.7), channel_id=1, replica_groups=mesh['dp'=32,'expert'=16] {'expert'}, dimensions={1}, use_global_device_ids=true | all-gather | bytes 557056 | tf_op jit(solution)/shard_map/all_gather | solution.py:50
  48.7 2.0 fusion.17
  50.7 0.0 copy-start.6
  50.7 0.0 copy-start.5
  50.7 7.7 %all-to-all-start = ((bf16[32,16,2048]{2,1,0:T(8,128)(2,1)}), bf16[32,16,2048]{2,1,0:T(8,128)(2,1)S(1)}, u32[]{:S(2)}, u32[]{:S(2)}) async-start(bf16[32,16,2048]{2,1,0:T(8,128)(2,1)} %fusion.17), calls=%async_computation | async-start | bytes 4194304 | tf_op jit(solution)/shard_map/all_to_all | solution.py:87
  58.4 0.0 copy-done.6
  58.4 0.1 copy.46
  58.5 0.1 broadcast_in_dim.51
  58.7 0.3 select_reduce_fusion.1
  58.9 0.0 copy-done.5
  59.0 28.7 %all_gather.10 = bf16[128,2048]{1,0:T(8,128)(2,1)S(1)} all-gather(bf16[128,128]{1,0:T(8,128)(2,1)S(1)} %copy-done.5), channel_id=1, replica_groups=mesh['dp'=32,'expert'=16] {'expert'}, dimensions={1}, use_global_device_ids=true | all-gather | bytes 557056 | tf_op jit(solution)/shard_map/all_gather | solution.py:51
  87.7 3.3 %multiply_convert_fusion = (bf16[512,2048]{1,0:T(8,128)(2,1)}, f32[512,2048]{1,0:T(8,128)}) fusion(f32[512]{0:T(512)S(1)} %select_reduce_fusion.1, pred[512,128]{1,0:T(8,128)(4,1)S(1)} %fusion.4, bf16[128,2048]{1,0:T(8,128)(2,1)S(1)} %all_gather.10), kind=kOutput, calls=%fused_computation.3 | convolution fusion | flops 270532608 | bytes 6883328 | tf_op jit(solution)/shard_map/dot_general | solution.py:82
  91.0 0.0 all-to-all-done
  91.0 7.4 %all-to-all-start.1 = ((bf16[32,16,2048]{2,1,0:T(8,128)(2,1)}), bf16[32,16,2048]{2,1,0:T(8,128)(2,1)}, u32[]{:S(2)}, u32[]{:S(2)}) async-start(bf16[32,16,2048]{2,1,0:T(8,128)(2,1)} %bitcast.86), calls=%async_computation.1 | async-start | bytes 4194304 | tf_op jit(solution)/shard_map/all_to_all | solution.py:88
  98.4 0.0 reduce-scatter.3.cloned.1.call-start
  98.5 2.7 fusion.15
  101.2 23.6 %all-to-all-done.1 = bf16[32,16,2048]{2,1,0:T(8,128)(2,1)} async-done(((bf16[32,16,2048]{2,1,0:T(8,128)(2,1)}), bf16[32,16,2048]{2,1,0:T(8,128)(2,1)}, u32[]{:S(2)}, u32[]{:S(2)}) %all-to-all-start.1) | async-done | bytes 2097184 | tf_op jit(solution)/shard_map/all_to_all | solution.py:88
  124.8 0.0 copy-start.7
  124.8 2.7 fusion.7
  127.5 0.0 copy-done
  127.5 0.0 copy-done.7
  127.5 0.0 copy-start.4
  127.5 0.9 multiply_convert_fusion.3
  128.4 0.0 copy-start.3
  128.4 0.2 copy-done.4
  128.6 0.7 convolution_convert_fusion
  129.4 0.3 copy-done.3
  129.6 0.7 fusion.13
  130.4 0.8 add_convert_fusion
  131.1 0.6 pad_maximum_fusion
  131.7 54.6 %all_to_all.15 = bf16[32,32,2048]{2,1,0:T(8,128)(2,1)S(1)} all-to-all(bf16[32,32,2048]{2,1,0:T(8,128)(2,1)S(1)} %pad_maximum_fusion), channel_id=1, replica_groups=mesh['dp'=32,'expert'=16] {'dp'}, dimensions={0} | all-to-all | bytes 8388608 | tf_op jit(solution)/shard_map/all_to_all | solution.py:92
  186.3 2.6 fusion.41
  188.9 3.9 %copy.48 = bf16[512,2048]{0,1:T(8,128)(2,1)} copy(bf16[512,2048]{1,0:T(8,128)(2,1)} %bitcast.92) | data formatting | bytes 4194304 | tf_op jit(solution)/shard_map/reshape | solution.py:106
  192.8 3.4 %convolution_bitcast_fusion.1 = f32[1,128,4,4,128]{1,4,3,2,0:T(8,128)} fusion(bf16[4,4,128,512]{3,2,1,0:T(8,128)(2,1)} %bitcast.90, pred[512,128]{1,0:T(8,128)(4,1)S(1)} %fusion.4), kind=kOutput, calls=%fused_computation.20 | convolution fusion | flops 268435456 | bytes 3211264 | tf_op jit(solution)/shard_map/dot_general | solution.py:23
  196.2 3.9 %copy.55 = bf16[2048,512]{1,0:T(8,128)(2,1)} copy(bf16[2048,512]{0,1:T(8,128)(2,1)} %bitcast.85) | data formatting | bytes 4194304 | tf_op jit(solution)/shard_map/dot_general | solution.py:108
  200.1 0.0 copy-start.2
  200.1 3.6 %convolution_bitcast_fusion = f32[1,128,4,4,128]{1,4,3,2,0:T(8,128)S(1)} fusion(bf16[4,4,128,512]{3,2,1,0:T(8,128)(2,1)} %bitcast.89, f32[512]{0:T(512)S(1)} %select_reduce_fusion.1, pred[512,128]{1,0:T(8,128)(4,1)S(1)} %fusion.4), kind=kOutput, calls=%fused_computation.19 | convolution fusion | flops 1610809344 | bytes 3213312 | tf_op jit(solution)/shard_map/dot_general | solution.py:108
  203.7 0.0 copy-done.2
  203.7 0.2 maximum_bitcast_fusion
  203.9 1.5 copy.49
  205.4 0.0 reduce-scatter.3.cloned.1.call-update
  205.5 0.0 reduce-scatter.5.cloned.1.call-start
  205.5 3.1 fusion.3
  208.6 46.3 %reduce-scatter.3.cloned.1.call-done = f32[2,128,512]{1,2,0:T(8,128)} async-done(((f32[2,128,2048]{1,2,0:T(8,128)}), f32[2,128,512]{1,2,0:T(8,128)}) %reduce-scatter.3.cloned.1.call-update) | async-done | bytes 524304 | tf_op jit(solution)/shard_map/reduce_scatter | solution.py:127
  254.9 0.0 reduce-scatter.5.cloned.1.call-update
  254.9 1.5 fusion.1
  256.4 1.5 fusion.2
  257.8 0.2 copy-done.1
  258.0 2.7 multiply_reduce_fusion
  260.7 0.3 select_reduce_fusion
  261.0 0.1 all_gather_reshape.3
  261.2 37.5 %all_gather.11 = f32[16,128,8]{1,2,0:T(8,128)S(1)} all-gather(f32[1,128,8]{1,2,0:T(8,128)S(1)} %copy.50), channel_id=1, replica_groups=mesh['dp'=32,'expert'=16] {'expert'}, dimensions={0}, use_global_device_ids=true | all-gather | bytes 69632 | tf_op jit(solution)/shard_map/all_gather | solution.py:133
  298.6 0.6 fusion.38
  299.2 3.5 %reduce-scatter.5.cloned.1.call-done = f32[2,128,128]{1,2,0:T(8,128)} async-done(((f32[2,128,512]{1,2,0:T(8,128)}), f32[2,128,128]{1,2,0:T(8,128)}) %reduce-scatter.5.cloned.1.call-update) | async-done | bytes 131088 | tf_op jit(solution)/shard_map/reduce_scatter | solution.py:130
  302.7 0.9 convert.4
  303.6 0.7 copy.52
  304.4 0.7 copy.51
  (8 shorter events, 0.1 us)
Async XLA Ops:
  7.2 120.3 %copy-start = (bf16[1,192,2048]{2,1,0:T(8,128)(2,1)S(1)}, bf16[1,192,2048]{2,1,0:T(8,128)(2,1)}, u32[]{:S(2)}) copy-start(bf16[1,192,2048]{2,1,0:T(8,128)(2,1)} %param.12) | copy-start | bytes 2359300
  50.7 7.7 %copy-start.6 = (f32[128,8]{0,1:T(8,128)S(1)}, f32[128,8]{0,1:T(8,128)}, u32[]{:S(2)}) copy-start(f32[128,8]{0,1:T(8,128)} %param.10) | copy-start | bytes 12292
  50.7 8.2 %copy-start.5 = (bf16[128,128]{1,0:T(8,128)(2,1)S(1)}, bf16[128,128]{1,0:T(8,128)(2,1)}, u32[]{:S(2)}) copy-start(bf16[128,128]{1,0:T(8,128)(2,1)} %param.8) | copy-start | bytes 98308
  50.7 40.3 %all-to-all-start = ((bf16[32,16,2048]{2,1,0:T(8,128)(2,1)}), bf16[32,16,2048]{2,1,0:T(8,128)(2,1)S(1)}, u32[]{:S(2)}, u32[]{:S(2)}) async-start(bf16[32,16,2048]{2,1,0:T(8,128)(2,1)} %fusion.17), calls=%async_computation | async-start | bytes 4194304 | tf_op jit(solution)/shard_map/all_to_all | solution.py:87
  91.0 33.8 %all-to-all-start.1 = ((bf16[32,16,2048]{2,1,0:T(8,128)(2,1)}), bf16[32,16,2048]{2,1,0:T(8,128)(2,1)}, u32[]{:S(2)}, u32[]{:S(2)}) async-start(bf16[32,16,2048]{2,1,0:T(8,128)(2,1)} %bitcast.86), calls=%async_computation.1 | async-start | bytes 4194304 | tf_op jit(solution)/shard_map/all_to_all | solution.py:88
  98.4 156.4 %reduce-scatter.3.cloned.1.call-start = ((), (), s32[]{:S(2)}) async-start(), calls=%async_computation.5 | async-start | bytes 2621440 | tf_op jit(solution)/shard_map/reduce_scatter | solution.py:127
  124.8 2.7 copy-start.7
  127.5 1.1 copy-start.4
  128.4 1.2 copy-start.3
  200.1 3.6 %copy-start.2 = (f32[1,128,4,4,128]{1,4,3,2,0:T(8,128)S(1)}, f32[1,128,4,4,128]{1,4,3,2,0:T(8,128)}, u32[]{:S(2)}) copy-start(f32[1,128,4,4,128]{1,4,3,2,0:T(8,128)} %convolution_bitcast_fusion.1) | copy-start | bytes 3145732
  205.5 97.3 %reduce-scatter.5.cloned.1.call-start = ((), (), s32[]{:S(2)}) async-start(), calls=%async_computation.6 | async-start | bytes 655360 | tf_op jit(solution)/shard_map/reduce_scatter | solution.py:130
  256.4 1.7 copy-start.1
Sparse Core Ops, SparseCore 0:
  205.6 49.2 reduce-scatter.2
  257.9 44.7 reduce-scatter.4

commit v11 on v9

--- a/solution.py
+++ b/solution.py
@@ -113,7 +113,8 @@
         preferred_element_type=jnp.float32,
     )
     grad_part = contract_first(token_pick, back_grad)
-    gate_terms = jnp.sum(slot_dy * back_out.astype(jnp.float32), axis=1)
+    dy_rows = jnp.dot(token_pick, full_dy, preferred_element_type=jnp.bfloat16)
+    gate_terms = jnp.sum(dy_rows.astype(jnp.float32) * back_out.astype(jnp.float32), axis=1)
     gate_part = jnp.sum(jnp.where(picks, gate_terms[:, None], 0.0), axis=0).reshape(
         tok_count, chosen
     )

time: 268 us -> 267 us (level)
  no operation moved by 1% of the time
where the time goes in v11:
time: 267 us; the launch traced here: 266 us
  blocking collectives  151 us (57%)
  waiting for transfers between devices  55.7 us (21%)
  matrix products  21.7 us (8%)
  starting transfers between devices  15.2 us (6%)
  between operations  14.3 us (5%)
  other arithmetic  5.18 us (2%)
  local copies, waits for them, and re-layouts  3.48 us (1%)
    all_to_all x1, blocking collectives, per_device(): lax.all_to_all(jnp.concatenate([part_out.reshape(dp_count, capacity, feat...  54.6 us
    all_gather x1, blocking collectives, per_device(): full_x = lax.all_gather(tokens, 'expert', axis=1, tiled=True)  38.8 us
    reduce_scatter x1, waiting for transfers between devices, per_device(): lax.psum_scatter(jnp.stack([out_part, grad_part]), 'expert', scatter_dime...  32.1 us
    all_gather x1, blocking collectives, per_device(): full_dy = lax.all_gather(cotangent, 'expert', axis=1, tiled=True)  28.7 us
    all_gather x1, blocking collectives, per_device(): gate_all = lax.all_gather(gate_part, 'expert', axis=0, tiled=False)  28.4 us
    all_to_all x1, waiting for transfers between devices, per_device(): lax.all_to_all(send_do, 'dp', split_axis=0, concat_axis=0, tiled=True)  23.6 us
    all_to_all x1, starting transfers between devices, per_device(): lax.all_to_all(send_x, 'dp', split_axis=0, concat_axis=0, tiled=True)  7.75 us
    all_to_all x1, starting transfers between devices, per_device(): lax.all_to_all(send_do, 'dp', split_axis=0, concat_axis=0, tiled=True)  7.44 us
  transfers between devices with their start and end apart: 3, of which 2 were waited for; matrix products, arithmetic and copies ran while one was open for 5% of the time, Pallas kernels for 0%

profile of v11, /device:TPU:6, one launch (start us, length us, event | category | flops | bytes accessed | tf_op | source)
XLA Modules:
  0.0 266.1 jit_solution(12503990114173280256)
XLA Ops:
  7.2 0.0 copy-start
  7.2 0.9 copy.28
  8.0 0.1 reshape.163
  8.2 0.5 fusion.6
  8.7 0.1 convert_element_type.69
  8.8 0.1 fusion.30
  9.0 0.9 fusion.4
  9.9 38.8 %all_gather.9 = bf16[128,2048]{1,0:T(8,128)(2,1)S(1)} all-gather(bf16[128,128]{1,0:T(8,128)(2,1)} %param.7), channel_id=1, replica_groups=mesh['dp'=32,'expert'=16] {'expert'}, dimensions={1}, use_global_device_ids=true | all-gather | bytes 557056 | tf_op jit(solution)/shard_map/all_gather | solution.py:50
  48.7 2.0 fusion.17
  50.7 0.0 copy-start.10
  50.7 7.7 %all-to-all-start = ((bf16[32,16,2048]{2,1,0:T(8,128)(2,1)}), bf16[32,16,2048]{2,1,0:T(8,128)(2,1)S(1)}, u32[]{:S(2)}, u32[]{:S(2)}) async-start(bf16[32,16,2048]{2,1,0:T(8,128)(2,1)} %fusion.17), calls=%async_computation | async-start | bytes 4194304 | tf_op jit(solution)/shard_map/all_to_all | solution.py:87
  58.5 0.0 copy-done.11
  58.5 0.1 copy.34
  58.6 0.1 broadcast_in_dim.51
  58.7 0.3 select_reduce_fusion.1
  59.0 0.0 copy-done.10
  59.0 28.7 %all_gather.10 = bf16[128,2048]{1,0:T(8,128)(2,1)S(1)} all-gather(bf16[128,128]{1,0:T(8,128)(2,1)S(1)} %copy-done.10), channel_id=1, replica_groups=mesh['dp'=32,'expert'=16] {'expert'}, dimensions={1}, use_global_device_ids=true | all-gather | bytes 557056 | tf_op jit(solution)/shard_map/all_gather | solution.py:51
  87.7 2.0 multiply_convert_fusion
  89.7 0.0 all-to-all-done
  89.7 7.4 %all-to-all-start.1 = ((bf16[32,16,2048]{2,1,0:T(8,128)(2,1)}), bf16[32,16,2048]{2,1,0:T(8,128)(2,1)}, u32[]{:S(2)}, u32[]{:S(2)}) async-start(bf16[32,16,2048]{2,1,0:T(8,128)(2,1)} %bitcast.68), calls=%async_computation.1 | async-start | bytes 4194304 | tf_op jit(solution)/shard_map/all_to_all | solution.py:88
  97.2 0.0 reduce-scatter.2.cloned.1.call-start
  97.2 2.7 %fusion.15 = f32[512,192]{0,1:T(8,128)} fusion(bf16[512,2048]{1,0:T(8,128)(2,1)S(1)} %bitcast.64, bf16[1,192,2048]{2,1,0:T(8,128)(2,1)} %param.11), kind=kOutput, calls=%fused_computation.31 | convolution fusion | flops 402653184 | bytes 3276800 | tf_op jit(solution)/shard_map/dot_general | solution.py:17
  99.9 23.6 %all-to-all-done.1 = bf16[32,16,2048]{2,1,0:T(8,128)(2,1)} async-done(((bf16[32,16,2048]{2,1,0:T(8,128)(2,1)}), bf16[32,16,2048]{2,1,0:T(8,128)(2,1)}, u32[]{:S(2)}, u32[]{:S(2)}) %all-to-all-start.1) | async-done | bytes 2097184 | tf_op jit(solution)/shard_map/all_to_all | solution.py:88
  123.5 2.7 fusion.7
  126.2 0.0 copy-done
  126.2 0.0 copy-done.12
  126.2 0.0 copy-start.7
  126.2 0.9 multiply_convert_fusion.3
  127.2 0.0 copy-start.3
  127.2 0.0 copy-start.6
  127.2 0.0 copy-start.8
  127.2 0.0 copy-start.5
  127.2 0.1 copy-done.7
  127.4 0.7 convolution_convert_fusion
  128.1 0.5 copy-done.5
  128.6 0.7 fusion.13
  129.3 0.0 copy-done.3
  129.3 0.0 copy-done.6
  129.3 0.0 copy-done.8
  129.3 0.8 add_convert_fusion
  130.1 0.6 pad_maximum_fusion
  130.7 54.6 %all_to_all.15 = bf16[32,32,2048]{2,1,0:T(8,128)(2,1)S(1)} all-to-all(bf16[32,32,2048]{2,1,0:T(8,128)(2,1)S(1)} %pad_maximum_fusion), channel_id=1, replica_groups=mesh['dp'=32,'expert'=16] {'dp'}, dimensions={0} | all-to-all | bytes 8388608 | tf_op jit(solution)/shard_map/all_to_all | solution.py:92
  185.3 0.6 fusion.39
  185.9 0.0 copy-start.1
  185.9 1.1 convolution_bitcast_fusion
  187.0 0.5 convolution_bitcast_fusion.1
  187.5 0.0 copy-done.1
  187.5 1.4 pad_maximum_fusion.1
  189.0 0.0 reduce-scatter.2.cloned.1.call-update
  189.0 0.0 copy-start.4
  189.0 3.2 %fusion.3 = bf16[1,192,2048]{2,1,0:T(8,128)(2,1)} fusion(bf16[512,192]{0,1:T(8,128)(2,1)} %copy-done.6, bf16[512,2048]{1,0:T(8,128)(2,1)} %bitcast.8), kind=kOutput, calls=%fused_computation.14 | convolution fusion | flops 403046400 | bytes 3080192 | tf_op jit(solution)/shard_map/dot_general | solution.py:23
  192.2 0.0 copy-done.4
  192.2 1.5 fusion.1
  193.7 0.0 copy-done.9
  193.7 1.5 fusion.2
  195.2 0.2 copy-done.2
  195.4 0.8 multiply_reduce_fusion
  196.2 0.3 select_reduce_fusion
  196.5 0.1 all_gather_reshape.3
  196.6 28.4 %all_gather.11 = f32[16,128,8]{1,2,0:T(8,128)S(1)} all-gather(f32[1,128,8]{1,2,0:T(8,128)S(1)} %copy.35), channel_id=1, replica_groups=mesh['dp'=32,'expert'=16] {'expert'}, dimensions={0}, use_global_device_ids=true | all-gather | bytes 69632 | tf_op jit(solution)/shard_map/all_gather | solution.py:124
  225.1 0.6 fusion.36
  225.7 32.1 %reduce-scatter.2.cloned.1.call-done = f32[2,128,128]{2,1,0:T(8,128)} async-done(((f32[2,128,2048]{2,1,0:T(8,128)}), f32[2,128,128]{2,1,0:T(8,128)}) %reduce-scatter.2.cloned.1.call-update) | async-done | bytes 131088 | tf_op jit(solution)/shard_map/reduce_scatter | solution.py:121
  257.7 0.9 convert.4
  258.6 0.6 slice_bitcast_fusion
  (10 shorter events, 0.1 us)
Async XLA Ops:
  7.2 119.0 %copy-start = (bf16[1,192,2048]{2,1,0:T(8,128)(2,1)S(1)}, bf16[1,192,2048]{2,1,0:T(8,128)(2,1)}, u32[]{:S(2)}) copy-start(bf16[1,192,2048]{2,1,0:T(8,128)(2,1)} %param.12) | copy-start | bytes 2359300
  50.7 7.8 %copy-start.11 = (f32[128,8]{0,1:T(8,128)S(1)}, f32[128,8]{0,1:T(8,128)}, u32[]{:S(2)}) copy-start(f32[128,8]{0,1:T(8,128)} %param.10) | copy-start | bytes 12292
  50.7 8.3 %copy-start.10 = (bf16[128,128]{1,0:T(8,128)(2,1)S(1)}, bf16[128,128]{1,0:T(8,128)(2,1)}, u32[]{:S(2)}) copy-start(bf16[128,128]{1,0:T(8,128)(2,1)} %param.8) | copy-start | bytes 98308
  50.7 39.0 %all-to-all-start = ((bf16[32,16,2048]{2,1,0:T(8,128)(2,1)}), bf16[32,16,2048]{2,1,0:T(8,128)(2,1)S(1)}, u32[]{:S(2)}, u32[]{:S(2)}) async-start(bf16[32,16,2048]{2,1,0:T(8,128)(2,1)} %fusion.17), calls=%async_computation | async-start | bytes 4194304 | tf_op jit(solution)/shard_map/all_to_all | solution.py:87
  89.7 33.8 %all-to-all-start.1 = ((bf16[32,16,2048]{2,1,0:T(8,128)(2,1)}), bf16[32,16,2048]{2,1,0:T(8,128)(2,1)}, u32[]{:S(2)}, u32[]{:S(2)}) async-start(bf16[32,16,2048]{2,1,0:T(8,128)(2,1)} %bitcast.68), calls=%async_computation.1 | async-start | bytes 4194304 | tf_op jit(solution)/shard_map/all_to_all | solution.py:88
  97.2 160.6 %reduce-scatter.2.cloned.1.call-start = ((), (), s32[]{:S(2)}) async-start(), calls=%async_computation.4 | async-start | bytes 2228224 | tf_op jit(solution)/shard_map/reduce_scatter | solution.py:121
  123.5 2.7 %copy-start.12 = (f32[512,192]{0,1:T(8,128)S(1)}, f32[512,192]{0,1:T(8,128)}, u32[]{:S(2)}) copy-start(f32[512,192]{0,1:T(8,128)} %fusion.15) | copy-start | bytes 1179652
  126.2 1.1 copy-start.7
  127.2 2.1 copy-start.3
  127.2 2.1 copy-start.6
  127.2 2.1 copy-start.8
  127.2 1.4 copy-start.5
  185.9 1.7 copy-start.1
  189.0 3.2 %copy-start.4 = (bf16[512,192]{0,1:T(8,128)(2,1)S(1)}, bf16[512,192]{0,1:T(8,128)(2,1)}, u32[]{:S(2)}) copy-start(bf16[512,192]{0,1:T(8,128)(2,1)} %copy-done.3) | copy-start | bytes 589828
  192.2 1.5 copy-start.9
  193.7 1.7 copy-start.2
Sparse Core Ops, SparseCore 0:
  189.1 68.5 reduce-scatter.1

commit v12 on v11

--- a/solution.py
+++ b/solution.py
@@ -104,14 +104,19 @@
     )
     back_out = back[:, :capacity].reshape(slot_total, features)
     back_grad = back[:, capacity:].reshape(slot_total, features)
-    gated_pick = token_pick.astype(jnp.float32) * slot_gate[:, None]
-    out_part = lax.dot_general(
-        gated_pick,
-        back_out.astype(jnp.float32),
-        (((0,), (0,)), ((), ())),
-        precision=lax.Precision.HIGHEST,
-        preferred_element_type=jnp.float32,
-    )
+    gate_hi = lax.reduce_precision(slot_gate, exponent_bits=8, mantissa_bits=7)
+    gate_rest = slot_gate - gate_hi
+    gate_mid = lax.reduce_precision(gate_rest, exponent_bits=8, mantissa_bits=7)
+    gate_lo = gate_rest - gate_mid
+    pick_float = token_pick.astype(jnp.float32)
+    gate_cols = jnp.concatenate(
+        [pick_float * gate_hi[:, None], pick_float * gate_mid[:, None], pick_float * gate_lo[:, None]],
+        axis=1,
+    ).astype(jnp.bfloat16)
+    out_pieces = contract_first(gate_cols, back_out)
+    out_part = (out_pieces[:tok_count] + out_pieces[tok_count : 2 * tok_count]) + out_pieces[
+        2 * tok_count :
+    ]
     grad_part = contract_first(token_pick, back_grad)
     dy_rows = jnp.dot(token_pick, full_dy, preferred_element_type=jnp.bfloat16)
     gate_terms = jnp.sum(dy_rows.astype(jnp.float32) * back_out.astype(jnp.float32), axis=1)

time: 267 us -> 278 us (1.041)
  blocking collectives: 151 us -> 96 us
  waiting for transfers between devices: 55.7 us -> 108 us
  starting transfers between devices: 15.2 us -> 22.8 us
  other arithmetic: 5.18 us -> 8.34 us
  local copies, waits for them, and re-layouts: 3.48 us -> 6.59 us
    all_to_all x1 -> x0, blocking collectives: 54.6 us -> none  [per_device(): lax.all_to_all(jnp.concatenate([part_out.reshape(dp_count, capacity, feat...]
    all_to_all x0 -> x1, waiting for transfers between devices: none -> 49.7 us  [per_device(): lax.all_to_all(jnp.concatenate([part_out.reshape(dp_count, capacity, feat...]
    all_to_all x0 -> x1, starting transfers between devices: none -> 7.38 us  [per_device(): lax.all_to_all(jnp.concatenate([part_out.reshape(dp_count, capacity, feat...]
    dot_general x4 -> x5, matrix products: 6.63 us -> 7.63 us  [contract_first(): lax.dot_general(first_op, second_op, (((0,), (0,)), ((), ())), preferred_...]
  transfers between devices with their start and end apart: 3 -> 4, of which waited for: 2 -> 3; matrix products, arithmetic and copies ran while one was open for 5% -> 5% of each run, Pallas kernels for 0% -> 0%
where the time goes in v12:
time: 278 us
  waiting for transfers between devices  108 us (39%)
  blocking collectives  96 us (35%)
  starting transfers between devices  22.8 us (8%)
  matrix products  21.6 us (8%)
  between operations  14.4 us (5%)
  other arithmetic  8.34 us (3%)
  local copies, waits for them, and re-layouts  6.59 us (2%)
    all_to_all x1, waiting for transfers between devices, per_device(): lax.all_to_all(jnp.concatenate([part_out.reshape(dp_count, capacity, feat...  49.7 us
    all_gather x1, blocking collectives, per_device(): full_x = lax.all_gather(tokens, 'expert', axis=1, tiled=True)  38.8 us
    reduce_scatter x1, waiting for transfers between devices, per_device(): lax.psum_scatter(jnp.stack([out_part, grad_part]), 'expert', scatter_dime...  34.6 us
    all_gather x1, blocking collectives, per_device(): full_dy = lax.all_gather(cotangent, 'expert', axis=1, tiled=True)  28.7 us
    all_gather x1, blocking collectives, per_device(): gate_all = lax.all_gather(gate_part, 'expert', axis=0, tiled=False)  28.4 us
    all_to_all x1, waiting for transfers between devices, per_device(): lax.all_to_all(send_do, 'dp', split_axis=0, concat_axis=0, tiled=True)  23.7 us
    all_to_all x1, starting transfers between devices, per_device(): lax.all_to_all(send_x, 'dp', split_axis=0, concat_axis=0, tiled=True)  7.75 us
    dot_general x5, matrix products, contract_first(): lax.dot_general(first_op, second_op, (((0,), (0,)), ((), ())), preferred_...  7.63 us
  transfers between devices with their start and end apart: 4, of which 3 were waited for; matrix products, arithmetic and copies ran while one was open for 5% of the time, Pallas kernels for 0%

profile of v12, /device:TPU:6, one launch (start us, length us, event | category | flops | bytes accessed | tf_op | source)
XLA Modules:
  0.0 277.6 jit_solution(7142397829866909350)
XLA Ops:
  7.2 0.0 copy-start
  7.2 0.9 copy.28
  8.0 0.1 reshape.173
  8.2 0.5 fusion.6
  8.7 0.1 convert_element_type.69
  8.8 0.1 fusion.36
  9.0 0.9 fusion.4
  9.9 38.8 %all_gather.9 = bf16[128,2048]{1,0:T(8,128)(2,1)S(1)} all-gather(bf16[128,128]{1,0:T(8,128)(2,1)} %param.7), channel_id=1, replica_groups=mesh['dp'=32,'expert'=16] {'expert'}, dimensions={1}, use_global_device_ids=true | all-gather | bytes 557056 | tf_op jit(solution)/shard_map/all_gather | solution.py:50
  48.7 2.0 fusion.18
  50.7 7.8 %all-to-all-start = ((bf16[32,16,2048]{2,1,0:T(8,128)(2,1)}), bf16[32,16,2048]{2,1,0:T(8,128)(2,1)S(1)}, u32[]{:S(2)}, u32[]{:S(2)}) async-start(bf16[32,16,2048]{2,1,0:T(8,128)(2,1)} %fusion.18), calls=%async_computation | async-start | bytes 4194304 | tf_op jit(solution)/shard_map/all_to_all | solution.py:87
  58.4 0.0 copy-done.14
  58.4 0.1 copy.34
  58.5 0.1 broadcast_in_dim.53
  58.7 0.3 select_reduce_fusion.1
  59.0 0.0 copy-done.13
  59.0 28.7 %all_gather.10 = bf16[128,2048]{1,0:T(8,128)(2,1)S(1)} all-gather(bf16[128,128]{1,0:T(8,128)(2,1)S(1)} %copy-done.13), channel_id=1, replica_groups=mesh['dp'=32,'expert'=16] {'expert'}, dimensions={1}, use_global_device_ids=true | all-gather | bytes 557056 | tf_op jit(solution)/shard_map/all_gather | solution.py:51
  87.7 2.0 multiply_convert_fusion
  89.7 0.0 all-to-all-done
  89.7 7.4 %all-to-all-start.1 = ((bf16[32,16,2048]{2,1,0:T(8,128)(2,1)}), bf16[32,16,2048]{2,1,0:T(8,128)(2,1)}, u32[]{:S(2)}, u32[]{:S(2)}) async-start(bf16[32,16,2048]{2,1,0:T(8,128)(2,1)} %bitcast.68), calls=%async_computation.1 | async-start | bytes 4194304 | tf_op jit(solution)/shard_map/all_to_all | solution.py:88
  97.2 2.7 fusion.16
  99.9 23.7 %all-to-all-done.1 = bf16[32,16,2048]{2,1,0:T(8,128)(2,1)} async-done(((bf16[32,16,2048]{2,1,0:T(8,128)(2,1)}), bf16[32,16,2048]{2,1,0:T(8,128)(2,1)}, u32[]{:S(2)}, u32[]{:S(2)}) %all-to-all-start.1) | async-done | bytes 2097184 | tf_op jit(solution)/shard_map/all_to_all | solution.py:88
  123.5 2.7 fusion.8
  126.2 0.0 copy-done
  126.2 0.0 copy-done.15
  126.2 0.0 copy-start.7
  126.2 0.9 multiply_convert_fusion.3
  127.2 0.0 copy-start.3
  127.2 0.0 copy-start.6
  127.2 0.0 copy-start.8
  127.2 0.0 copy-start.5
  127.2 0.1 copy-done.7
  127.4 0.7 convolution_convert_fusion
  128.1 0.5 copy-done.5
  128.6 0.7 fusion.14
  129.4 0.8 add_convert_fusion
  130.1 2.5 pad_maximum_fusion
  132.7 7.4 %all-to-all-start.2 = ((bf16[32,32,2048]{2,1,0:T(8,128)(2,1)}), bf16[32,32,2048]{2,1,0:T(8,128)(2,1)}, u32[]{:S(2)}, u32[]{:S(2)}) async-start(bf16[32,32,2048]{2,1,0:T(8,128)(2,1)} %pad_maximum_fusion), calls=%async_computation.2 | async-start | bytes 8388608 | tf_op jit(solution)/shard_map/all_to_all | solution.py:92
  140.1 0.2 reduce-scatter.2.cloned.1.call-start
  140.3 1.0 fusion.27
  141.3 49.7 %all-to-all-done.2 = bf16[32,32,2048]{2,1,0:T(8,128)(2,1)} async-done(((bf16[32,32,2048]{2,1,0:T(8,128)(2,1)}), bf16[32,32,2048]{2,1,0:T(8,128)(2,1)}, u32[]{:S(2)}, u32[]{:S(2)}) %all-to-all-start.2) | async-done | bytes 4194336 | tf_op jit(solution)/shard_map/all_to_all | solution.py:92
  191.0 2.7 fusion.46
  193.8 0.0 copy-start.10
  193.8 0.5 convolution_bitcast_fusion
  194.3 0.5 copy-done.10
  194.8 0.2 copy-done.11
  195.0 0.2 copy-done.12
  195.2 1.0 fusion.20
  196.2 0.2 fusion.7
  196.4 1.5 pad_maximum_fusion.1
  197.9 0.0 reduce-scatter.2.cloned.1.call-update
  197.9 0.0 copy-start.4
  197.9 3.2 %fusion.3 = bf16[1,192,2048]{2,1,0:T(8,128)(2,1)} fusion(bf16[512,192]{0,1:T(8,128)(2,1)} %copy-done.6, bf16[512,2048]{1,0:T(8,128)(2,1)} %bitcast.8), kind=kOutput, calls=%fused_computation.13 | convolution fusion | flops 403046400 | bytes 3080192 | tf_op jit(solution)/shard_map/dot_general | solution.py:23
  201.2 1.5 fusion.1
  202.6 0.0 copy-done.9
  202.6 1.5 fusion.2
  204.1 0.2 copy-done.2
  204.3 0.8 multiply_reduce_fusion
  205.1 0.3 select_reduce_fusion
  205.4 0.1 all_gather_reshape.3
  205.6 28.4 %all_gather.11 = f32[16,128,8]{1,2,0:T(8,128)S(1)} all-gather(f32[1,128,8]{1,2,0:T(8,128)S(1)} %copy.35), channel_id=1, replica_groups=mesh['dp'=32,'expert'=16] {'expert'}, dimensions={0}, use_global_device_ids=true | all-gather | bytes 69632 | tf_op jit(solution)/shard_map/all_gather | solution.py:129
  234.0 0.6 fusion.42
  234.6 34.6 %reduce-scatter.2.cloned.1.call-done = f32[2,128,128]{2,1,0:T(8,128)} async-done(((f32[2,128,2048]{2,1,0:T(8,128)}), f32[2,128,128]{2,1,0:T(8,128)}) %reduce-scatter.2.cloned.1.call-update) | async-done | bytes 131088 | tf_op jit(solution)/shard_map/reduce_scatter | solution.py:126
  269.2 0.9 convert.16
  270.1 0.6 slice_bitcast_fusion
  (20 shorter events, 0.2 us)
Async XLA Ops:
  7.2 119.0 %copy-start = (bf16[1,192,2048]{2,1,0:T(8,128)(2,1)S(1)}, bf16[1,192,2048]{2,1,0:T(8,128)(2,1)}, u32[]{:S(2)}) copy-start(bf16[1,192,2048]{2,1,0:T(8,128)(2,1)} %param.12) | copy-start | bytes 2359300
  50.7 7.8 %copy-start.14 = (f32[128,8]{0,1:T(8,128)S(1)}, f32[128,8]{0,1:T(8,128)}, u32[]{:S(2)}) copy-start(f32[128,8]{0,1:T(8,128)} %param.10) | copy-start | bytes 12292
  50.7 8.3 %copy-start.13 = (bf16[128,128]{1,0:T(8,128)(2,1)S(1)}, bf16[128,128]{1,0:T(8,128)(2,1)}, u32[]{:S(2)}) copy-start(bf16[128,128]{1,0:T(8,128)(2,1)} %param.8) | copy-start | bytes 98308
  50.7 39.0 %all-to-all-start = ((bf16[32,16,2048]{2,1,0:T(8,128)(2,1)}), bf16[32,16,2048]{2,1,0:T(8,128)(2,1)S(1)}, u32[]{:S(2)}, u32[]{:S(2)}) async-start(bf16[32,16,2048]{2,1,0:T(8,128)(2,1)} %fusion.18), calls=%async_computation | async-start | bytes 4194304 | tf_op jit(solution)/shard_map/all_to_all | solution.py:87
  89.7 33.8 %all-to-all-start.1 = ((bf16[32,16,2048]{2,1,0:T(8,128)(2,1)}), bf16[32,16,2048]{2,1,0:T(8,128)(2,1)}, u32[]{:S(2)}, u32[]{:S(2)}) async-start(bf16[32,16,2048]{2,1,0:T(8,128)(2,1)} %bitcast.68), calls=%async_computation.1 | async-start | bytes 4194304 | tf_op jit(solution)/shard_map/all_to_all | solution.py:88
  123.5 2.7 copy-start.15
  126.2 1.1 copy-start.7
  127.2 2.2 copy-start.3
  127.2 2.2 copy-start.6
  127.2 2.2 copy-start.8
  127.2 1.4 copy-start.5
  132.7 58.3 %all-to-all-start.2 = ((bf16[32,32,2048]{2,1,0:T(8,128)(2,1)}), bf16[32,32,2048]{2,1,0:T(8,128)(2,1)}, u32[]{:S(2)}, u32[]{:S(2)}) async-start(bf16[32,32,2048]{2,1,0:T(8,128)(2,1)} %pad_maximum_fusion), calls=%async_computation.2 | async-start | bytes 8388608 | tf_op jit(solution)/shard_map/all_to_all | solution.py:92
  140.1 129.1 %reduce-scatter.2.cloned.1.call-start = ((), (), s32[]{:S(2)}) async-start(), calls=%async_computation.4 | async-start | bytes 2228224 | tf_op jit(solution)/shard_map/reduce_scatter | solution.py:126
  193.7 2.5 copy-start.1
  193.8 1.0 copy-start.10
  193.8 1.3 copy-start.11
  193.8 1.5 copy-start.12
  197.9 3.2 %copy-start.4 = (bf16[512,192]{0,1:T(8,128)(2,1)S(1)}, bf16[512,192]{0,1:T(8,128)(2,1)}, u32[]{:S(2)}) copy-start(bf16[512,192]{0,1:T(8,128)(2,1)} %copy-done.3) | copy-start | bytes 589828
  201.1 1.5 copy-start.9
  202.6 1.7 copy-start.2
Sparse Core Ops, SparseCore 0:
  198.0 71.1 reduce-scatter.1

commit v13 on v11

--- a/solution.py
+++ b/solution.py
@@ -46,6 +46,31 @@
     return (part_out, part_grad, gradients)
 
 
+def forward_part(rows_x, gate_w, up_w, down_w):
+    pre_gate = contract_last(rows_x, gate_w)
+    pre_up = contract_last(rows_x, up_w)
+    activated, derivative = silu_parts(pre_gate)
+    hidden = (activated * pre_up).astype(jnp.bfloat16)
+    part_out = jnp.dot(hidden, down_w, preferred_element_type=jnp.float32).astype(jnp.bfloat16)
+    return (pre_up, activated, derivative, hidden, part_out)
+
+
+def backward_part(rows_x, rows_do, gate_w, up_w, down_w, pre_up, activated, derivative, hidden):
+    d_hidden = contract_last(rows_do, down_w)
+    d_pre_gate = (d_hidden * pre_up * derivative).astype(jnp.bfloat16)
+    d_pre_up = (d_hidden * activated).astype(jnp.bfloat16)
+    part_grad = (
+        jnp.dot(d_pre_gate, gate_w, preferred_element_type=jnp.float32)
+        + jnp.dot(d_pre_up, up_w, preferred_element_type=jnp.float32)
+    ).astype(jnp.bfloat16)
+    gradients = (
+        contract_first(d_pre_gate, rows_x),
+        contract_first(d_pre_up, rows_x),
+        contract_first(hidden, rows_do),
+    )
+    return (part_grad, gradients)
+
+
 def per_device(tokens, cotangent, expert_ids, gate_weights, w_gate, w_up, w_down):
     full_x = lax.all_gather(tokens, "expert", axis=1, tiled=True)
     full_dy = lax.all_gather(cotangent, "expert", axis=1, tiled=True)
@@ -88,7 +113,11 @@
     recv_do = lax.all_to_all(send_do, "dp", split_axis=0, concat_axis=0, tiled=True)
     rows_x = recv_x.reshape(slot_total, features)
     rows_do = recv_do.reshape(slot_total, features)
-    part_out, part_grad, gradients = expert_rows(rows_x, rows_do, *weights)
+    pre_up, activated, derivative, hidden, part_out = forward_part(rows_x, *weights)
+    part_out, hidden, rows_do = lax.optimization_barrier((part_out, hidden, rows_do))
+    part_grad, gradients = backward_part(
+        rows_x, rows_do, *weights, pre_up, activated, derivative, hidden
+    )
     back = lax.all_to_all(
         jnp.concatenate(
             [

time: 267 us -> 266 us (level)
  waiting for transfers between devices: 55.7 us -> 51.1 us
    all_to_all x1, waiting for transfers between devices: 23.6 us -> 19.9 us  [per_device(): lax.all_to_all(send_do, 'dp', split_axis=0, concat_axis=0, tiled=True)]
  transfers between devices with their start and end apart: 3 -> 3, of which waited for: 2 -> 2; matrix products, arithmetic and copies ran while one was open for 5% -> 6% of each run, Pallas kernels for 0% -> 0%
where the time goes in v13:
time: 266 us; the launch traced here: 265 us
  blocking collectives  150 us (56%)
  waiting for transfers between devices  51.1 us (19%)
  matrix products  24 us (9%)
  starting transfers between devices  15.2 us (6%)
  between operations  14.3 us (5%)
  other arithmetic  5.18 us (2%)
  local copies, waits for them, and re-layouts  4.67 us (2%)
    all_to_all x1, blocking collectives, per_device(): lax.all_to_all(jnp.concatenate([part_out.reshape(dp_count, capacity, feat...  54.6 us
    all_gather x1, blocking collectives, per_device(): full_x = lax.all_gather(tokens, 'expert', axis=1, tiled=True)  38.8 us
    reduce_scatter x1, waiting for transfers between devices, per_device(): lax.psum_scatter(jnp.stack([out_part, grad_part]), 'expert', scatter_dime...  31.2 us
    all_gather x1, blocking collectives, per_device(): full_dy = lax.all_gather(cotangent, 'expert', axis=1, tiled=True)  28.7 us
    all_gather x1, blocking collectives, per_device(): gate_all = lax.all_gather(gate_part, 'expert', axis=0, tiled=False)  28.4 us
    all_to_all x1, waiting for transfers between devices, per_device(): lax.all_to_all(send_do, 'dp', split_axis=0, concat_axis=0, tiled=True)  19.9 us
    all_to_all x1, starting transfers between devices, per_device(): lax.all_to_all(send_x, 'dp', split_axis=0, concat_axis=0, tiled=True)  7.75 us
    dot_general x4, matrix products, contract_first(): lax.dot_general(first_op, second_op, (((0,), (0,)), ((), ())), preferred_...  7.59 us
  transfers between devices with their start and end apart: 3, of which 2 were waited for; matrix products, arithmetic and copies ran while one was open for 6% of the time, Pallas kernels for 0%

profile of v13, /device:TPU:6, one launch (start us, length us, event | category | flops | bytes accessed | tf_op | source)
XLA Modules:
  0.0 265.0 jit_solution(6410177237351230202)
XLA Ops:
  7.2 0.0 copy-start
  7.2 0.9 copy.28
  8.0 0.1 reshape.163
  8.2 0.5 fusion.6
  8.7 0.1 convert_element_type.69
  8.8 0.1 fusion.30
  9.0 0.9 fusion.4
  9.9 38.8 %all_gather.9 = bf16[128,2048]{1,0:T(8,128)(2,1)S(1)} all-gather(bf16[128,128]{1,0:T(8,128)(2,1)} %param.7), channel_id=1, replica_groups=mesh['dp'=32,'expert'=16] {'expert'}, dimensions={1}, use_global_device_ids=true | all-gather | bytes 557056 | tf_op jit(solution)/shard_map/all_gather | solution.py:75
  48.7 2.0 fusion.17
  50.7 7.7 %all-to-all-start = ((bf16[32,16,2048]{2,1,0:T(8,128)(2,1)}), bf16[32,16,2048]{2,1,0:T(8,128)(2,1)S(1)}, u32[]{:S(2)}, u32[]{:S(2)}) async-start(bf16[32,16,2048]{2,1,0:T(8,128)(2,1)} %fusion.17), calls=%async_computation | async-start | bytes 4194304 | tf_op jit(solution)/shard_map/all_to_all | solution.py:112
  58.5 0.0 copy-done.13
  58.5 0.1 copy.34
  58.6 0.1 broadcast_in_dim.51
  58.7 0.3 select_reduce_fusion.1
  59.0 0.0 copy-done.12
  59.0 28.7 %all_gather.10 = bf16[128,2048]{1,0:T(8,128)(2,1)S(1)} all-gather(bf16[128,128]{1,0:T(8,128)(2,1)S(1)} %copy-done.12), channel_id=1, replica_groups=mesh['dp'=32,'expert'=16] {'expert'}, dimensions={1}, use_global_device_ids=true | all-gather | bytes 557056 | tf_op jit(solution)/shard_map/all_gather | solution.py:76
  87.7 2.0 multiply_convert_fusion
  89.7 0.0 all-to-all-done
  89.7 7.4 %all-to-all-start.1 = ((bf16[32,16,2048]{2,1,0:T(8,128)(2,1)}), bf16[32,16,2048]{2,1,0:T(8,128)(2,1)}, u32[]{:S(2)}, u32[]{:S(2)}) async-start(bf16[32,16,2048]{2,1,0:T(8,128)(2,1)} %bitcast.70), calls=%async_computation.1 | async-start | bytes 4194304 | tf_op jit(solution)/shard_map/all_to_all | solution.py:113
  97.2 0.0 reduce-scatter.2.cloned.1.call-start
  97.2 0.0 copy-start.7
  97.2 2.1 fusion.15
  99.3 0.0 copy-done.7
  99.3 0.0 copy-start.14
  99.3 1.6 multiply_convert_fusion.3
  100.9 0.0 copy-done.14
  100.9 0.7 copy-done.9
  101.6 0.0 copy-done
  101.6 2.1 convolution_convert_fusion
  103.7 19.9 %all-to-all-done.1 = bf16[32,16,2048]{2,1,0:T(8,128)(2,1)} async-done(((bf16[32,16,2048]{2,1,0:T(8,128)(2,1)}), bf16[32,16,2048]{2,1,0:T(8,128)(2,1)}, u32[]{:S(2)}, u32[]{:S(2)}) %all-to-all-start.1) | async-done | bytes 2097184 | tf_op jit(solution)/shard_map/all_to_all | solution.py:113
  123.5 2.7 %multiply_convert_fusion.1 = (bf16[512,192]{0,1:T(8,128)(2,1)S(1)}, bf16[512,192]{0,1:T(8,128)(2,1)S(1)}) fusion(f32[512,192]{0,1:T(8,128)} %copy-done.14, f32[512,192]{0,1:T(8,128)} %get-tuple-element.25, bf16[512,2048]{1,0:T(8,128)(2,1)} %bitcast.7, bf16[1,192,2048]{2,1,0:T(8,128)(2,1)S(1)} %copy-done), kind=kOutput, calls=%fused_computation.35 | convolution fusion | flops 403931136 | bytes 4063232 | tf_op jit(solution)/shard_map/dot_general | solution.py:17
  126.3 0.0 copy-start.4
  126.3 0.0 copy-start.11
  126.3 0.0 copy-done.6
  126.3 0.0 copy-start.8
  126.3 0.7 fusion.13
  127.1 0.0 copy-done.4
  127.1 0.0 copy-done.11
  127.1 0.5 copy-done.8
  127.6 0.7 add_convert_fusion
  128.3 0.8 copy-done.3
  129.2 0.6 pad_maximum_fusion
  129.8 54.6 %all_to_all.15 = bf16[32,32,2048]{2,1,0:T(8,128)(2,1)S(1)} all-to-all(bf16[32,32,2048]{2,1,0:T(8,128)(2,1)S(1)} %pad_maximum_fusion), channel_id=1, replica_groups=mesh['dp'=32,'expert'=16] {'dp'}, dimensions={0} | all-to-all | bytes 8388608 | tf_op jit(solution)/shard_map/all_to_all | solution.py:121
  184.3 0.6 fusion.39
  184.9 0.0 copy-start.1
  184.9 1.1 convolution_bitcast_fusion
  186.1 0.5 convolution_bitcast_fusion.1
  186.6 0.0 copy-done.1
  186.6 1.4 pad_maximum_fusion.1
  188.0 0.0 reduce-scatter.2.cloned.1.call-update
  188.1 0.0 copy-start.5
  188.1 2.4 fusion.2
  190.5 0.0 copy-done.5
  190.5 1.5 fusion.1
  192.0 0.0 copy-done.10
  192.0 3.2 %fusion.3 = bf16[1,192,2048]{2,1,0:T(8,128)(2,1)} fusion(bf16[512,192]{0,1:T(8,128)(2,1)S(1)} %copy-done.10, bf16[512,2048]{1,0:T(8,128)(2,1)} %bitcast.7), kind=kOutput, calls=%fused_computation.14 | convolution fusion | flops 403046400 | bytes 3080192 | tf_op jit(solution)/shard_map/dot_general | solution.py:23
  195.2 0.8 multiply_reduce_fusion
  196.0 0.3 select_reduce_fusion
  196.3 0.1 all_gather_reshape.3
  196.4 28.4 %all_gather.11 = f32[16,128,8]{1,2,0:T(8,128)S(1)} all-gather(f32[1,128,8]{1,2,0:T(8,128)S(1)} %copy.35), channel_id=1, replica_groups=mesh['dp'=32,'expert'=16] {'expert'}, dimensions={0}, use_global_device_ids=true | all-gather | bytes 69632 | tf_op jit(solution)/shard_map/all_gather | solution.py:153
  224.8 0.6 fusion.36
  225.4 31.2 %reduce-scatter.2.cloned.1.call-done = f32[2,128,128]{2,1,0:T(8,128)} async-done(((f32[2,128,2048]{2,1,0:T(8,128)}), f32[2,128,128]{2,1,0:T(8,128)}) %reduce-scatter.2.cloned.1.call-update) | async-done | bytes 131088 | tf_op jit(solution)/shard_map/reduce_scatter | solution.py:150
  256.6 0.9 convert.4
  257.5 0.6 slice_bitcast_fusion
  (14 shorter events, 0.2 us)
Async XLA Ops:
  7.2 94.4 %copy-start = (bf16[1,192,2048]{2,1,0:T(8,128)(2,1)S(1)}, bf16[1,192,2048]{2,1,0:T(8,128)(2,1)}, u32[]{:S(2)}) copy-start(bf16[1,192,2048]{2,1,0:T(8,128)(2,1)} %param.13) | copy-start | bytes 2359300
  50.7 7.8 %copy-start.13 = (f32[128,8]{0,1:T(8,128)S(1)}, f32[128,8]{0,1:T(8,128)}, u32[]{:S(2)}) copy-start(f32[128,8]{0,1:T(8,128)} %param.10) | copy-start | bytes 12292
  50.7 8.3 %copy-start.12 = (bf16[128,128]{1,0:T(8,128)(2,1)S(1)}, bf16[128,128]{1,0:T(8,128)(2,1)}, u32[]{:S(2)}) copy-start(bf16[128,128]{1,0:T(8,128)(2,1)} %param.8) | copy-start | bytes 98308
  50.7 39.0 %all-to-all-start = ((bf16[32,16,2048]{2,1,0:T(8,128)(2,1)}), bf16[32,16,2048]{2,1,0:T(8,128)(2,1)S(1)}, u32[]{:S(2)}, u32[]{:S(2)}) async-start(bf16[32,16,2048]{2,1,0:T(8,128)(2,1)} %fusion.17), calls=%async_computation | async-start | bytes 4194304 | tf_op jit(solution)/shard_map/all_to_all | solution.py:112
  89.7 33.8 %all-to-all-start.1 = ((bf16[32,16,2048]{2,1,0:T(8,128)(2,1)}), bf16[32,16,2048]{2,1,0:T(8,128)(2,1)}, u32[]{:S(2)}, u32[]{:S(2)}) async-start(bf16[32,16,2048]{2,1,0:T(8,128)(2,1)} %bitcast.70), calls=%async_computation.1 | async-start | bytes 4194304 | tf_op jit(solution)/shard_map/all_to_all | solution.py:113
  97.2 159.4 %reduce-scatter.2.cloned.1.call-start = ((), (), s32[]{:S(2)}) async-start(), calls=%async_computation.4 | async-start | bytes 2228224 | tf_op jit(solution)/shard_map/reduce_scatter | solution.py:150
  97.2 2.1 copy-start.7
  99.3 1.6 copy-start.14
  100.9 0.7 copy-start.9
  123.5 2.8 %copy-start.6 = (bf16[1,192,2048]{2,1,0:T(8,128)(2,1)S(1)}, bf16[1,192,2048]{2,1,0:T(8,128)(2,1)}, u32[]{:S(2)}) copy-start(bf16[1,192,2048]{2,1,0:T(8,128)(2,1)} %param.11) | copy-start | bytes 2359300
  126.3 0.8 copy-start.4
  126.3 0.8 copy-start.11
  126.3 1.3 copy-start.8
  127.6 1.6 copy-start.3
  184.9 1.7 copy-start.1
  188.1 2.4 copy-start.5
  190.5 1.5 copy-start.10
  192.0 3.2 %copy-start.2 = (bf16[32,16,2048]{2,1,0:T(8,128)(2,1)S(1)}, bf16[32,16,2048]{2,1,0:T(8,128)(2,1)}, u32[]{:S(2)}) copy-start(bf16[32,16,2048]{2,1,0:T(8,128)(2,1)} %copy-done.1) | copy-start | bytes 6291460
Sparse Core Ops, SparseCore 0:
  188.2 68.3 reduce-scatter.1
